TPU v7x, 32 devices: a whole 2x2x4 slice. The times are simulated.
32 devices in a mesh: grp: 2 (over y), cin: 4 (over z), cout: 4 (over x, core).
Axes of the slice: x: 2, y: 2, z: 4, core: 2. Of those that a mesh axis runs over, the one named last changes fastest.
Arguments:
- volume: bfloat16 [128, 8, 16, 256], P(None, ('grp', 'cin'), 'cout'), parts along dimension 1, may hold values from -6 to 6
- first_filter: bfloat16 [128, 27, 128], replicated, may hold values from -0.109375 to 0.109375
- second_filter: bfloat16 [128, 27, 128], replicated, may hold values from -0.109375 to 0.109375
- cotangent: bfloat16 [128, 8, 16, 256], P(None, ('grp', 'cin'), 'cout'), parts along dimension 1, may hold values from -6 to 6
Outputs:
- second_out: bfloat16 [128, 8, 16, 256], P(None, ('grp', 'cin'), 'cout'), parts along dimension 1
- first_filter_grad: float32 [128, 54, 128], P('cout', 'grp', 'cin'), parts along dimension 1
- second_filter_grad: float32 [128, 54, 128], P('cout', 'grp', 'cin'), parts along dimension 1
There are 2 independent parts, one for each index of `grp`. A program takes and returns all parts, laid end to end along the dimension named above; an argument that names none is the same for every part. Nothing has to cross between parts.
All inputs are finite; a program needn't handle non-finite values.
Results may differ from a plain program's by a relative error of at most 0.005.
Values may be sent and summed in bfloat16 or wider, within the bound.
No kernel may reach another device: no remote copies, remote signals or barrier semaphores. Data moves between devices by JAX's collectives and lax.ppermute only.
A program may use at most 64 MiB of HBM per device.

v0:
```python
import math

import jax
import jax.numpy as jnp
from jax import lax
from jax.sharding import PartitionSpec as P


def extended(cells, sides, width):
    for axis, dim in sides:
        count = lax.axis_size(axis)
        ends = count - 1
        head = lax.slice_in_dim(cells, 0, width, axis=dim)
        tail = lax.slice_in_dim(cells, cells.shape[dim] - width, cells.shape[dim], axis=dim)
        cells = jnp.concatenate(
            [
                lax.ppermute(tail, axis, [(i, (i + 1) % count) for i in range(ends)]),
                cells,
                lax.ppermute(head, axis, [((i + 1) % count, i) for i in range(ends)]),
            ],
            axis=dim,
        )
    return cells


def widen_cells(values):
    return jnp.pad(values, ((0, 0), (0, 0), (0, 0), (1, 1)))


def kernel_of(weight):
    outs = weight.shape[0]
    ins = weight.shape[2]
    return weight.reshape(outs, 3, 3, 3, ins).transpose(0, 4, 1, 2, 3)


def run_conv(padded, kernel):
    result = lax.conv_general_dilated(
        padded[None],
        kernel,
        (1, 1, 1),
        "VALID",
        dimension_numbers=("NCDHW", "OIDHW", "NCDHW"),
        preferred_element_type=jnp.float32,
    )
    return result[0]


def tap_products(padded, gradient):
    planes = gradient.shape[1]
    rows = gradient.shape[2]
    width = gradient.shape[3]
    flat_grad = gradient.reshape(gradient.shape[0], -1)
    pieces = []
    for first in range(3):
        for second in range(3):
            for third in range(3):
                window = padded[
                    :, first : first + planes, second : second + rows, third : third + width
                ].reshape(padded.shape[0], -1)
                pieces.append(
                    jnp.einsum("oc,ic->oi", flat_grad, window, preferred_element_type=jnp.float32)
                )
    return jnp.stack(pieces, axis=1)


def body(volume, first_filter, second_filter, cotangent):
    planes = volume.shape[1]
    rows = volume.shape[2]
    width = volume.shape[3]
    cells_total = lax.axis_size("cin") * planes * lax.axis_size("cout") * rows * width
    factor = 1.0 / math.sqrt(cells_total)
    volume_field = widen_cells(extended(volume, (("cin", 1), ("cout", 2)), 1))
    first_out = run_conv(volume_field, kernel_of(first_filter))
    hidden = jax.nn.silu(first_out).astype(jnp.bfloat16)
    hidden_field = widen_cells(extended(hidden, (("cin", 1), ("cout", 2)), 1))
    second_out = run_conv(hidden_field, kernel_of(second_filter)).astype(jnp.bfloat16)
    cotangent_field = widen_cells(extended(cotangent, (("cin", 1), ("cout", 2)), 1))
    outs = second_filter.shape[0]
    ins = second_filter.shape[2]
    back_kernel = jnp.flip(
        second_filter.reshape(outs, 3, 3, 3, ins).transpose(4, 0, 1, 2, 3), axis=(2, 3, 4)
    )
    hidden_grad = run_conv(cotangent_field, back_kernel)
    second_grads = tap_products(hidden_field, cotangent)
    logistic = jax.nn.sigmoid(first_out)
    first_grad = (hidden_grad * logistic * (1.0 + first_out * (1.0 - logistic))).astype(
        jnp.bfloat16
    )
    first_grads = tap_products(volume_field, first_grad)
    first_part, second_part = (
        lax.psum_scatter(first_grads, "cin", scatter_dimension=2, tiled=True),
        lax.psum_scatter(second_grads, "cin", scatter_dimension=2, tiled=True),
    )
    first_sum, second_sum = (
        lax.psum_scatter(first_part, "cout", scatter_dimension=0, tiled=True),
        lax.psum_scatter(second_part, "cout", scatter_dimension=0, tiled=True),
    )
    return (second_out, first_sum * factor, second_sum * factor)


def solution(mesh):
    return jax.shard_map(
        body,
        mesh=mesh,
        in_specs=(
            P(None, ("grp", "cin"), "cout", None),
            P(),
            P(),
            P(None, ("grp", "cin"), "cout", None),
        ),
        out_specs=(
            P(None, ("grp", "cin"), "cout", None),
            P("cout", "grp", "cin"),
            P("cout", "grp", "cin"),
        ),
        check_vma=False,
    )
```

profile of v0, /device:TPU:0, one launch (start us, length us, event | category | flops | bytes accessed | tf_op | source)
XLA Modules:
  0.0 254.7 jit_solution(6101132300400608593)
XLA Ops:
  8.3 5.1 %collective-permute-start = (bf16[128,1,4,256]{3,0,2,1:T(8,128)(2,1)S(1)}, bf16[128,1,4,256]{3,0,2,1:T(8,128)(2,1)S(1)}, u32[]{:S(2)}, u32[]{:S(2)}) collective-permute-start(bf16[128,1,4,256]{3,0,2,1:T(8,128)(2,1)S(1)} %copy.195), channel_id=1, source_target_pairs={{0,4},{4,8},{8,12},{1,5},{5,9},{9,13},{2,6},{6,10},{10,14},{3,7},{... | collective-permute-start | bytes 786440 | tf_op jit(solution)/shard_map/ppermute | solution.py:17
  15.7 4.6 %collective-permute-start.8 = (bf16[128,1,4,256]{3,0,2,1:T(8,128)(2,1)S(1)}, bf16[128,1,4,256]{3,0,2,1:T(8,128)(2,1)S(1)}, u32[]{:S(2)}, u32[]{:S(2)}) collective-permute-start(bf16[128,1,4,256]{3,0,2,1:T(8,128)(2,1)S(1)} %copy.207), channel_id=1, source_target_pairs={{0,4},{4,8},{8,12},{1,5},{5,9},{9,13},{2,6},{6,10},{10,14},{3,7},{... | collective-permute-start | bytes 786440 | tf_op jit(solution)/shard_map/ppermute | solution.py:17
  24.4 3.0 %collective-permute-start.2 = (bf16[128,3,1,256]{3,0,2,1:T(8,128)(2,1)S(1)}, bf16[128,3,1,256]{3,0,2,1:T(8,128)(2,1)S(1)}, u32[]{:S(2)}, u32[]{:S(2)}) collective-permute-start(bf16[128,3,1,256]{3,0,2,1:T(8,128)(2,1)S(1)} %get-tuple-element.16), channel_id=1, source_target_pairs={{0,1},{1,2},{2,3},{4,5},{5,6},{6,7},{8,9},{9,10},{10,11},{12,13},{... | collective-permute-start | bytes 589832 | tf_op jit(solution)/shard_map/ppermute | solution.py:17
  31.5 3.7 %collective-permute-start.10 = (bf16[128,3,1,256]{3,0,2,1:T(8,128)(2,1)}, bf16[128,3,1,256]{3,0,2,1:T(8,128)(2,1)}, u32[]{:S(2)}, u32[]{:S(2)}) collective-permute-start(bf16[128,3,1,256]{3,0,2,1:T(8,128)(2,1)} %get-tuple-element.12), channel_id=1, source_target_pairs={{0,1},{1,2},{2,3},{4,5},{5,6},{6,7},{8,9},{9,10},{10,11},{12,13},{... | collective-permute-start | bytes 589832 | tf_op jit(solution)/shard_map/ppermute | solution.py:17
  37.5 2.6 %copy.257 = bf16[128,3,6,1,258]{0,4,2,1,3:T(8,128)(2,1)} copy(bf16[128,3,6,1,258]{4,0,2,1,3:T(8,128)(2,1)} %fusion.239) | data formatting | bytes 2377728
  40.1 2.4 pad.13.clone
  42.5 3.0 %reshape.451 = bf16[128,3,6,1,8,33]{0,5,4,2,1,3:T(8,128)(2,1)} reshape(bf16[128,3,6,1,264]{0,4,2,1,3:T(8,128)(2,1)} %pad.13.clone) | data formatting | bytes 2433024 | tf_op jit(solution)/shard_map/conv_general_dilated | solution.py:37
  47.2 2.8 %multiply_convert_fusion = (bf16[1,4,8,33,128]{4,2,3,1,0:T(8,128)(2,1)}, f32[1,4,8,33,128]{4,2,3,1,0:T(8,128)S(1)}) fusion(bf16[128,3,3,3,128]{4,0,3,2,1:T(8,128)(2,1)S(1)} %bitcast.648, bf16[128,3,6,1,7,2]{0,4,5,2,1,3:T(8,128)(2,1)S(1)} %slice.267, bf16[128,3,6,1,8,33]{0,4,5,2,1,3:T(8,128)(2,1)S(1)} %copy.200, pred[8,33]{0,1:T(8,128)(4,1)S(1)} %copy-done.13), kind=kOutput, calls=%fused_computation.152 | convolution fusion | flops 938962944 | bytes 2977032 | tf_op jit(solution)/shard_map/conv_general_dilated | solution.py:37
  54.3 4.7 %collective-permute-start.4 = (bf16[128,1,4,256]{3,0,2,1:T(8,128)(2,1)S(1)}, bf16[128,1,4,256]{3,0,2,1:T(8,128)(2,1)S(1)}, u32[]{:S(2)}, u32[]{:S(2)}) collective-permute-start(bf16[128,1,4,256]{3,0,2,1:T(8,128)(2,1)S(1)} %fusion.107), channel_id=1, source_target_pairs={{0,4},{4,8},{8,12},{1,5},{5,9},{9,13},{2,6},{6,10},{10,14},{3,7},{... | collective-permute-start | bytes 786440 | tf_op jit(solution)/shard_map/ppermute | solution.py:17
  59.0 3.4 %fusion.4 = bf16[128,3,6,1,258]{4,0,2,1,3:T(8,128)(2,1)} fusion(bf16[128,3,1,256]{3,0,2,1:T(8,128)(2,1)S(1)} %collective-permute-done.11, bf16[128,3,4,256]{3,0,2,1:T(8,128)(2,1)} %copy-done.2, bf16[128,3,1,256]{3,0,2,1:T(8,128)(2,1)} %collective-permute-done.10), kind=kLoop, calls=%fused_computation.8 | loop fusion | flops 7133184 | bytes 2368512 | tf_op jit(solution)/shard_map/broadcast_in_dim | solution.py:38
  62.5 2.6 %copy.258 = bf16[128,3,6,1,258]{0,4,2,1,3:T(8,128)(2,1)} copy(bf16[128,3,6,1,258]{4,0,2,1,3:T(8,128)(2,1)} %fusion.4) | data formatting | bytes 2377728
  65.1 2.4 pad.17.clone
  67.5 3.0 %reshape.467 = bf16[128,3,6,1,8,33]{0,5,4,2,1,3:T(8,128)(2,1)} reshape(bf16[128,3,6,1,264]{0,4,2,1,3:T(8,128)(2,1)} %pad.17.clone) | data formatting | bytes 2433024 | tf_op jit(solution)/shard_map/conv_general_dilated | solution.py:37
  101.9 3.0 %collective-permute-start.6 = (bf16[128,3,1,256]{3,0,2,1:T(8,128)(2,1)S(1)}, bf16[128,3,1,256]{3,0,2,1:T(8,128)(2,1)S(1)}, u32[]{:S(2)}, u32[]{:S(2)}) collective-permute-start(bf16[128,3,1,256]{3,0,2,1:T(8,128)(2,1)S(1)} %get-tuple-element.14), channel_id=1, source_target_pairs={{0,1},{1,2},{2,3},{4,5},{5,6},{6,7},{8,9},{9,10},{10,11},{12,13},{... | collective-permute-start | bytes 589832 | tf_op jit(solution)/shard_map/ppermute | solution.py:17
  105.9 3.1 %copy.216 = f32[128,27,128]{0,1,2:T(8,128)} copy(f32[128,27,128]{2,0,1:T(8,128)} %fusion.74) | data formatting | bytes 3538944 | tf_op jit(solution)/shard_map/stack | solution.py:63
  121.2 32.1 %reduce-scatter.9.cloned.1.call-done = f32[128,27,32]{0,1,2:T(8,128)} async-done(((f32[128,27,128]{0,1,2:T(8,128)}), f32[128,27,32]{0,1,2:T(8,128)}) %reduce-scatter.9.cloned.1.call-update) | async-done | bytes 442384 | tf_op jit(solution)/shard_map/reduce_scatter | solution.py:91
  153.3 3.9 %copy.250 = f32[128,27,32]{1,2,0:T(8,128)} copy(f32[128,27,32]{0,1,2:T(8,128)} %reduce-scatter.9.cloned.1.call-done) | data formatting | bytes 884736
  157.2 3.6 %reshape.542 = f32[128,864]{1,0:T(8,128)} reshape(f32[128,32,27]{2,1,0:T(8,128)} %bitcast.676) | data formatting | bytes 884736
  161.2 37.4 %reduce-scatter.11.cloned.1.call-done = f32[128,27,32]{0,1,2:T(8,128)} async-done(((f32[128,27,128]{0,1,2:T(8,128)}), f32[128,27,32]{0,1,2:T(8,128)}) %reduce-scatter.11.cloned.1.call-update) | async-done | bytes 442384 | tf_op jit(solution)/shard_map/reduce_scatter | solution.py:92
  198.6 3.9 %copy.252 = f32[128,27,32]{1,2,0:T(8,128)} copy(f32[128,27,32]{0,1,2:T(8,128)} %reduce-scatter.11.cloned.1.call-done) | data formatting | bytes 884736
  202.4 3.6 %reshape.544 = f32[128,864]{1,0:T(8,128)} reshape(f32[128,32,27]{2,1,0:T(8,128)} %bitcast.677) | data formatting | bytes 884736
  206.1 2.6 %fusion.238 = bf16[128,3,6,1,258]{4,0,2,1,3:T(8,128)(2,1)} fusion(bf16[128,3,1,256]{3,0,2,1:T(8,128)(2,1)S(1)} %collective-permute-done.7, bf16[128,1,4,256]{3,0,2,1:T(8,128)(2,1)S(1)} %collective-permute-done.5, bf16[128,1,4,256]{3,0,2,1:T(8,128)(2,1)S(1)} %fusion.107, bf16[128,1,4,256]{3,0,2,1:T(8,128)(2,1)S(1)} %collective-permute-done.4, ...), kind=kLoop, calls=%fused_computation.347 | loop fusion | flops 10699776 | bytes 2368512 | tf_op jit(solution)/shard_map/broadcast_in_dim | solution.py:38
  218.5 3.2 %reduce-scatter.13.cloned.1.call-done = f32[32,864]{1,0:T(8,128)} async-done(((f32[128,864]{1,0:T(8,128)}), f32[32,864]{1,0:T(8,128)}) %reduce-scatter.13.cloned.1.call-update) | async-done | bytes 110608
  224.6 20.6 %reduce-scatter.15.cloned.1.call-done = f32[32,864]{1,0:T(8,128)} async-done(((f32[128,864]{1,0:T(8,128)}), f32[32,864]{1,0:T(8,128)}) %reduce-scatter.15.cloned.1.call-update) | async-done | bytes 110608
  (155 shorter events, 79.8 us)
Async XLA Ops:
  7.2 40.0 %copy-start = (bf16[128,27,128]{2,0,1:T(8,128)(2,1)S(1)}, bf16[128,27,128]{2,0,1:T(8,128)(2,1)}, u32[]{:S(2)}) copy-start(bf16[128,27,128]{2,0,1:T(8,128)(2,1)} %param.5) | copy-start | bytes 2654212
  7.2 146.1 %reduce-scatter.9.cloned.1.call-start = ((), (), s32[]{:S(2)}) async-start(), calls=%async_computation.4 | async-start | bytes 2621440 | tf_op jit(solution)/shard_map/reduce_scatter | solution.py:91
  8.3 19.2 %copy-start.1 = (bf16[128,1,4,256]{3,2,1,0:T(4,128)(2,1)S(1)}, bf16[128,1,4,256]{3,2,1,0:T(4,128)(2,1)}, u32[]{:S(2)}) copy-start(bf16[128,1,4,256]{3,2,1,0:T(4,128)(2,1)} %param.7) | copy-start | bytes 786436
  8.3 13.2 %collective-permute-start = (bf16[128,1,4,256]{3,0,2,1:T(8,128)(2,1)S(1)}, bf16[128,1,4,256]{3,0,2,1:T(8,128)(2,1)S(1)}, u32[]{:S(2)}, u32[]{:S(2)}) collective-permute-start(bf16[128,1,4,256]{3,0,2,1:T(8,128)(2,1)S(1)} %copy.195), channel_id=1, source_target_pairs={{0,4},{4,8},{8,12},{1,5},{5,9},{9,13},{2,6},{6,10},{10,14},{3,7},{... | collective-permute-start | bytes 786440 | tf_op jit(solution)/shard_map/ppermute | solution.py:17
  13.4 9.7 %collective-permute-start.1 = (bf16[128,1,4,256]{3,0,2,1:T(8,128)(2,1)S(1)}, bf16[128,1,4,256]{3,0,2,1:T(8,128)(2,1)S(1)}, u32[]{:S(2)}, u32[]{:S(2)}) collective-permute-start(bf16[128,1,4,256]{3,0,2,1:T(8,128)(2,1)S(1)} %copy.195), channel_id=1, source_target_pairs={{4,0},{8,4},{12,8},{5,1},{9,5},{13,9},{6,2},{10,6},{14,10},{7,3},{... | collective-permute-start | bytes 786440 | tf_op jit(solution)/shard_map/ppermute | solution.py:19
  15.7 11.8 %collective-permute-start.8 = (bf16[128,1,4,256]{3,0,2,1:T(8,128)(2,1)S(1)}, bf16[128,1,4,256]{3,0,2,1:T(8,128)(2,1)S(1)}, u32[]{:S(2)}, u32[]{:S(2)}) collective-permute-start(bf16[128,1,4,256]{3,0,2,1:T(8,128)(2,1)S(1)} %copy.207), channel_id=1, source_target_pairs={{0,4},{4,8},{8,12},{1,5},{5,9},{9,13},{2,6},{6,10},{10,14},{3,7},{... | collective-permute-start | bytes 786440 | tf_op jit(solution)/shard_map/ppermute | solution.py:17
  20.2 9.1 %collective-permute-start.9 = (bf16[128,1,4,256]{3,0,2,1:T(8,128)(2,1)S(1)}, bf16[128,1,4,256]{3,0,2,1:T(8,128)(2,1)S(1)}, u32[]{:S(2)}, u32[]{:S(2)}) collective-permute-start(bf16[128,1,4,256]{3,0,2,1:T(8,128)(2,1)S(1)} %copy.207), channel_id=1, source_target_pairs={{4,0},{8,4},{12,8},{5,1},{9,5},{13,9},{6,2},{10,6},{14,10},{7,3},{... | collective-permute-start | bytes 786440 | tf_op jit(solution)/shard_map/ppermute | solution.py:19
  21.5 5.9 %copy-start.6 = (bf16[128,1,4,256]{3,0,2,1:T(8,128)(2,1)}, bf16[128,1,4,256]{3,0,2,1:T(8,128)(2,1)S(1)}, u32[]{:S(2)}) copy-start(bf16[128,1,4,256]{3,0,2,1:T(8,128)(2,1)S(1)} %collective-permute-done) | copy-start | bytes 786436
  23.0 4.4 %copy-start.4 = (bf16[128,1,4,256]{3,0,2,1:T(8,128)(2,1)}, bf16[128,1,4,256]{3,0,2,1:T(8,128)(2,1)S(1)}, u32[]{:S(2)}) copy-start(bf16[128,1,4,256]{3,0,2,1:T(8,128)(2,1)S(1)} %collective-permute-done.1) | copy-start | bytes 786436
  23.1 12.1 %collective-permute-start.3 = (bf16[128,3,1,256]{3,0,2,1:T(8,128)(2,1)S(1)}, bf16[128,3,1,256]{3,0,2,1:T(8,128)(2,1)S(1)}, u32[]{:S(2)}, u32[]{:S(2)}) collective-permute-start(bf16[128,3,1,256]{3,0,2,1:T(8,128)(2,1)S(1)} %get-tuple-element.17), channel_id=1, source_target_pairs={{1,0},{2,1},{3,2},{5,4},{6,5},{7,6},{9,8},{10,9},{11,10},{13,12},{... | collective-permute-start | bytes 589832 | tf_op jit(solution)/shard_map/ppermute | solution.py:19
  24.4 10.8 %collective-permute-start.2 = (bf16[128,3,1,256]{3,0,2,1:T(8,128)(2,1)S(1)}, bf16[128,3,1,256]{3,0,2,1:T(8,128)(2,1)S(1)}, u32[]{:S(2)}, u32[]{:S(2)}) collective-permute-start(bf16[128,3,1,256]{3,0,2,1:T(8,128)(2,1)S(1)} %get-tuple-element.16), channel_id=1, source_target_pairs={{0,1},{1,2},{2,3},{4,5},{5,6},{6,7},{8,9},{9,10},{10,11},{12,13},{... | collective-permute-start | bytes 589832 | tf_op jit(solution)/shard_map/ppermute | solution.py:17
  29.3 8.1 %copy-start.2 = (bf16[128,3,4,256]{3,0,2,1:T(8,128)(2,1)}, bf16[128,3,4,256]{3,0,2,1:T(8,128)(2,1)S(1)}, u32[]{:S(2)}) copy-start(bf16[128,3,4,256]{3,0,2,1:T(8,128)(2,1)S(1)} %constant_dynamic-update-slice_fusion.3) | copy-start | bytes 2359300
  30.2 28.8 %collective-permute-start.11 = (bf16[128,3,1,256]{3,0,2,1:T(8,128)(2,1)}, bf16[128,3,1,256]{3,0,2,1:T(8,128)(2,1)S(1)}, u32[]{:S(2)}, u32[]{:S(2)}) collective-permute-start(bf16[128,3,1,256]{3,0,2,1:T(8,128)(2,1)} %get-tuple-element.13), channel_id=1, source_target_pairs={{1,0},{2,1},{3,2},{5,4},{6,5},{7,6},{9,8},{10,9},{11,10},{13,12},{... | collective-permute-start | bytes 589832 | tf_op jit(solution)/shard_map/ppermute | solution.py:19
  31.5 27.6 %collective-permute-start.10 = (bf16[128,3,1,256]{3,0,2,1:T(8,128)(2,1)}, bf16[128,3,1,256]{3,0,2,1:T(8,128)(2,1)}, u32[]{:S(2)}, u32[]{:S(2)}) collective-permute-start(bf16[128,3,1,256]{3,0,2,1:T(8,128)(2,1)} %get-tuple-element.12), channel_id=1, source_target_pairs={{0,1},{1,2},{2,3},{4,5},{5,6},{6,7},{8,9},{9,10},{10,11},{12,13},{... | collective-permute-start | bytes 589832 | tf_op jit(solution)/shard_map/ppermute | solution.py:17
  53.0 47.6 %collective-permute-start.5 = (bf16[128,1,4,256]{3,0,2,1:T(8,128)(2,1)S(1)}, bf16[128,1,4,256]{3,0,2,1:T(8,128)(2,1)S(1)}, u32[]{:S(2)}, u32[]{:S(2)}) collective-permute-start(bf16[128,1,4,256]{3,0,2,1:T(8,128)(2,1)S(1)} %fusion.107), channel_id=1, source_target_pairs={{4,0},{8,4},{12,8},{5,1},{9,5},{13,9},{6,2},{10,6},{14,10},{7,3},{... | collective-permute-start | bytes 786440 | tf_op jit(solution)/shard_map/ppermute | solution.py:19
  54.3 46.3 %collective-permute-start.4 = (bf16[128,1,4,256]{3,0,2,1:T(8,128)(2,1)S(1)}, bf16[128,1,4,256]{3,0,2,1:T(8,128)(2,1)S(1)}, u32[]{:S(2)}, u32[]{:S(2)}) collective-permute-start(bf16[128,1,4,256]{3,0,2,1:T(8,128)(2,1)S(1)} %fusion.107), channel_id=1, source_target_pairs={{0,4},{4,8},{8,12},{1,5},{5,9},{9,13},{2,6},{6,10},{10,14},{3,7},{... | collective-permute-start | bytes 786440 | tf_op jit(solution)/shard_map/ppermute | solution.py:17
  77.5 3.5 %copy-start.7 = (bf16[128,1,4,256]{3,0,2,1:T(8,128)(2,1)S(1)}, bf16[128,1,4,256]{3,0,2,1:T(8,128)(2,1)}, u32[]{:S(2)}) copy-start(bf16[128,1,4,256]{3,0,2,1:T(8,128)(2,1)} %copy-done.6) | copy-start | bytes 786436
  84.6 4.4 %copy-start.3 = (bf16[128,1,4,256]{3,2,1,0:T(4,128)(2,1)S(1)}, bf16[128,1,4,256]{3,2,1,0:T(4,128)(2,1)}, u32[]{:S(2)}) copy-start(bf16[128,1,4,256]{3,2,1,0:T(4,128)(2,1)} %param.4) | copy-start | bytes 786436
  92.5 4.5 %copy-start.5 = (bf16[128,1,4,256]{3,0,2,1:T(8,128)(2,1)S(1)}, bf16[128,1,4,256]{3,0,2,1:T(8,128)(2,1)}, u32[]{:S(2)}) copy-start(bf16[128,1,4,256]{3,0,2,1:T(8,128)(2,1)} %copy-done.4) | copy-start | bytes 786436
  100.6 9.7 %collective-permute-start.7 = (bf16[128,3,1,256]{3,0,2,1:T(8,128)(2,1)S(1)}, bf16[128,3,1,256]{3,0,2,1:T(8,128)(2,1)S(1)}, u32[]{:S(2)}, u32[]{:S(2)}) collective-permute-start(bf16[128,3,1,256]{3,0,2,1:T(8,128)(2,1)S(1)} %get-tuple-element.15), channel_id=1, source_target_pairs={{1,0},{2,1},{3,2},{5,4},{6,5},{7,6},{9,8},{10,9},{11,10},{13,12},{... | collective-permute-start | bytes 589832 | tf_op jit(solution)/shard_map/ppermute | solution.py:19
  101.9 8.4 %collective-permute-start.6 = (bf16[128,3,1,256]{3,0,2,1:T(8,128)(2,1)S(1)}, bf16[128,3,1,256]{3,0,2,1:T(8,128)(2,1)S(1)}, u32[]{:S(2)}, u32[]{:S(2)}) collective-permute-start(bf16[128,3,1,256]{3,0,2,1:T(8,128)(2,1)S(1)} %get-tuple-element.14), channel_id=1, source_target_pairs={{0,1},{1,2},{2,3},{4,5},{5,6},{6,7},{8,9},{9,10},{10,11},{12,13},{... | collective-permute-start | bytes 589832 | tf_op jit(solution)/shard_map/ppermute | solution.py:17
  109.0 89.6 %reduce-scatter.11.cloned.1.call-start = ((), (), s32[]{:S(2)}) async-start(), calls=%async_computation.5 | async-start | bytes 2621440 | tf_op jit(solution)/shard_map/reduce_scatter | solution.py:92
  121.2 100.5 %reduce-scatter.13.cloned.1.call-start = ((), (), s32[]{:S(2)}) async-start(), calls=%async_computation.6 | async-start | bytes 573440
  160.9 84.3 %reduce-scatter.15.cloned.1.call-start = ((), (), s32[]{:S(2)}) async-start(), calls=%async_computation.7 | async-start | bytes 573440
  (6 other events, 8.0 us)
Sparse Core Ops, SparseCore 0:
  109.1 44.1 reduce-scatter.8
  155.7 42.8 reduce-scatter.10
  201.1 20.4 reduce-scatter.12
  224.0 21.1 reduce-scatter.14
where the time goes:
time: 256 us; the launch traced here: 255 us
  waiting for transfers between devices  95.5 us (37%)
  local copies, waits for them, and re-layouts  63.4 us (25%)
  matrix products  37.5 us (15%)
  starting transfers between devices  32.6 us (13%)
  between operations  14.4 us (6%)
  other arithmetic  11.3 us (4%)
    reduce_scatter x1, waiting for transfers between devices, body(): lax.psum_scatter(second_grads, 'cin', scatter_dimension=2, tiled=True)  37.4 us
    unnamed x51, local copies, waits for them, and re-layouts  37.2 us
    reduce_scatter x1, waiting for transfers between devices, body(): lax.psum_scatter(first_grads, 'cin', scatter_dimension=2, tiled=True)  32.1 us
    dot_general x54, matrix products, tap_products(): jnp.einsum('oc,ic->oi', flat_grad, window, preferred_element_type=jnp.flo...  30.5 us
    ppermute x6, starting transfers between devices, extended(): lax.ppermute(tail, axis, [(i, (i + 1) % count) for i in range(ends)])  24.2 us
    unnamed x6, waiting for transfers between devices  23.8 us
    conv_general_dilated x11, local copies, waits for them, and re-layouts, run_conv(): lax.conv_general_dilated(padded[None], kernel, (1, 1, 1), 'VALID', dimens...  12.7 us
    broadcast_in_dim x3, other arithmetic, run_conv(): padded[None]  8.31 us
  transfers between devices with their start and end apart: 16, of which 6 were waited for; matrix products, arithmetic and copies ran while one was open for 42% of the time, Pallas kernels for 0%

commit v1 on v0

v1 whole, which is shorter than its diff:
```python
import functools
import math

import jax
import jax.numpy as jnp
from jax import lax
from jax.experimental import pallas as pl
from jax.experimental.pallas import tpu as pltpu
from jax.sharding import PartitionSpec as P

VMEM = pl.BlockSpec(memory_space=pltpu.VMEM)
SMEM = pl.BlockSpec(memory_space=pltpu.SMEM)
ANY = pl.BlockSpec(memory_space=pl.ANY)
F32 = jnp.float32
BF16 = jnp.bfloat16


def links(count, odd):
    pairs = []
    for i in range(odd, count - 1, 2):
        pairs += [(i, i + 1), (i + 1, i)]
    return pairs


def swap_planes(values, odd):
    return lax.ppermute(values, "cin", links(lax.axis_size("cin"), odd))


def swap_rows(values, odd):
    return lax.ppermute(values, "cout", links(lax.axis_size("cout"), odd))


def swap_corner(values, odd):
    count = lax.axis_size("cout")
    pairs = [
        (a * count + c, b * count + d)
        for a, b in links(lax.axis_size("cin"), odd)
        for c, d in links(count, 1)
    ]
    return lax.ppermute(values, ("cin", "cout"), pairs)


def shift_up(values):
    lane = lax.broadcasted_iota(jnp.int32, values.shape, 1)
    return jnp.where(lane == 0, 0.0, pltpu.roll(values, 1, 1))


def shift_down(values):
    width = values.shape[1]
    lane = lax.broadcasted_iota(jnp.int32, values.shape, 1)
    return jnp.where(lane == width - 1, 0.0, pltpu.roll(values, width - 1, 1))


def spread(values):
    wide = values.astype(F32)
    return jnp.concatenate(
        [shift_down(wide).astype(BF16), values.astype(BF16), shift_up(wide).astype(BF16)], axis=0
    )


def combine(products):
    chans = products.shape[0] // 3
    return (
        products[chans : 2 * chans]
        + shift_up(products[:chans])
        + shift_down(products[2 * chans :])
    )


def fill(where, slabs, field, sems):
    rows = slabs[0].shape[0]
    plane = where[0]
    row = where[1]
    even_plane = 2 * (1 - plane)
    odd_plane = 2 * plane
    body = pl.ds(1, rows)
    even_row = (1 - row) * (rows + 1)
    odd_row = row * (rows + 1)
    source = row * (rows - 1)
    targets = (1, even_plane, odd_plane)
    copies = []
    for k in range(3):
        copies.append((slabs[k], field.at[body, targets[k]]))
        copies.append((slabs[3 + k].at[source], field.at[even_row, targets[k]]))
        copies.append((slabs[6 + k], field.at[odd_row, targets[k]]))
    started = [
        pltpu.make_async_copy(src, dst, sems.at[n]) for n, (src, dst) in enumerate(copies)
    ]
    for copy in started:
        copy.start()
    for copy in started:
        copy.wait()


def window(field, row):
    block = field[pl.ds(row, 3)]
    return block.reshape(-1, block.shape[-1])


def conv_rows(weights, field, row):
    return combine(
        jnp.dot(weights[...], window(field, row), preferred_element_type=F32)
    )


def first_kernel(where, *refs):
    slabs = refs[:9]
    weights, field, hidden, slope, edge, sems = refs[9:]
    fill(where, slabs, field, sems)
    rows = hidden.shape[0]

    def step(row, carry):
        value = conv_rows(weights, field, row)
        gate = 1.0 / (1.0 + jnp.exp(-value))
        hidden[row] = (value * gate).astype(BF16)
        slope[row] = gate * (1.0 + value * (1.0 - gate))
        return carry

    lax.fori_loop(0, rows, step, 0)
    edge[...] = hidden[where[1] * (rows - 1)]


def second_kernel(where, *refs):
    slabs = refs[:9]
    weights, out, field, sems = refs[9:]
    fill(where, slabs, field, sems)

    def step(row, carry):
        out[row] = conv_rows(weights, field, row).astype(BF16)
        return carry

    lax.fori_loop(0, out.shape[0], step, 0)


def hand_over(where, total, *outs):
    if len(outs) == 1:
        outs[0][...] = total[...]
        return
    send, keep = outs
    width = send.shape[1] // 2
    mine = where[1]
    for half in range(2):
        rows = pl.ds(half * width, width)
        theirs = pl.multiple_of(2 * half * width + (1 - mine) * width, width)
        ours = pl.multiple_of(2 * half * width + mine * width, width)
        send[:, rows] = total[:, pl.ds(theirs, width)].astype(BF16)
        keep[:, rows] = total[:, pl.ds(ours, width)]


def second_grad_kernel(where, *refs):
    slabs = refs[:9]
    hidden, field, *outs = refs[9:-2]
    total, sems = refs[-2:]
    fill(where, slabs, field, sems)
    taps, chans, width = total.shape

    def step(row, carry):
        part = lax.dot_general(
            window(field, row),
            spread(hidden[row]),
            (((1,), (1,)), ((), ())),
            preferred_element_type=F32,
        ).reshape(taps, chans, width)
        total[...] = jnp.where(row == 0, part, total[...] + part)
        return carry

    lax.fori_loop(0, hidden.shape[0], step, 0)
    hand_over(where, total, *outs)


def first_grad_kernel(where, weights, grad_field, slope, field, *refs):
    outs = refs[:-1]
    total = refs[-1]
    taps, chans, width = total.shape

    def step(row, carry):
        grad = conv_rows(weights, grad_field, row) * slope[row]
        part = lax.dot_general(
            spread(grad.astype(BF16)),
            window(field, row),
            (((1,), (1,)), ((), ())),
            preferred_element_type=F32,
        ).reshape(taps, chans, width)
        total[...] = jnp.where(row == 0, part, total[...] + part)
        return carry

    lax.fori_loop(0, slope.shape[0], step, 0)
    hand_over(where, total, *outs)


def add_kernel(where, held, arrived, send, keep):
    width = send.shape[1]
    mine = where[2]
    ours = pl.ds(pl.multiple_of(mine * width, width), width)
    theirs = pl.ds(pl.multiple_of((1 - mine) * width, width), width)
    send[...] = (held[:, theirs] + arrived[:, theirs].astype(F32)).astype(BF16)
    keep[...] = held[:, ours] + arrived[:, ours].astype(F32)


def pack_kernel(where, held, arrived, *refs):
    sends = refs[:-2]
    keep, packed = refs[-2:]
    parts, tiles, outs, lanes = packed.shape
    group = lanes // parts
    per = held.shape[2] // lanes
    sums = {}
    for n in range(held.shape[0] * per):
        at = (n // per, slice(None), slice(n % per * lanes, (n % per + 1) * lanes))
        sums[n] = held[at] + arrived[at].astype(F32)
    lane = lax.broadcasted_iota(jnp.int32, (outs, lanes), 1) // group
    for tile in range(tiles):
        for part in range(parts):
            value = jnp.zeros((outs, lanes), F32)
            for place in range(parts):
                n = tile * parts + place
                if n in sums:
                    turned = sums[n]
                    if place != part:
                        turned = pltpu.roll(turned, (place - part) % parts * group, 1)
                    value = jnp.where(lane == place, turned, value)
            packed[part, tile] = value
    mine = where[3]
    keep[...] = packed[mine]
    for k, send in enumerate(sends):
        send[...] = packed[mine ^ (k + 1)].astype(BF16)


def finish_kernel(tap_of, factor, held, *refs):
    out = refs[-1]
    tiles, outs, lanes = held.shape
    group = out.shape[2]
    places = lanes // group
    for tile in range(tiles):
        total = held[tile]
        for arrived in refs[:-1]:
            total = total + arrived[tile].astype(F32)
        total = total * factor
        for place in range(places):
            n = tile * places + place
            if n < len(tap_of):
                out[:, tap_of[n], :] = total[:, place * group : (place + 1) * group]


def struct(shape, dtype):
    return jax.ShapeDtypeStruct(shape, dtype)


def call(kernel, name, ins, out_shapes, args, scratch=(), flops=0):
    moved = sum(math.prod(a.shape) * a.dtype.itemsize for a in (*args, *out_shapes))
    return pl.pallas_call(
        kernel,
        name=name,
        in_specs=ins,
        out_specs=[VMEM] * len(out_shapes),
        out_shape=out_shapes,
        scratch_shapes=scratch,
        cost_estimate=pl.CostEstimate(flops=flops, bytes_accessed=moved, transcendentals=0),
    )(*args)


def slabs_of(own, edge_own, edge_even, edge_odd):
    planes = (own, swap_planes(own, 0), swap_planes(own, 1))
    return planes + tuple(swap_rows(p, 0) for p in planes) + (edge_own, edge_even, edge_odd)


def by_rows(values):
    return values[:, 0].transpose(1, 0, 2)


def forward_weights(weight):
    outs, taps, ins = weight.shape
    return weight.reshape(outs, 3, 3, 3, ins).transpose(3, 0, 2, 1, 4).reshape(3 * outs, 9 * ins)


def backward_weights(weight):
    outs, taps, ins = weight.shape
    turned = jnp.flip(weight.reshape(outs, 3, 3, 3, ins), axis=(1, 2, 3))
    return turned.transpose(3, 4, 2, 1, 0).reshape(3 * ins, 9 * outs)


def reduced(where, send, keep, tap_of, factor, shape):
    taps, half, width = keep.shape
    parts = lax.axis_size("cin")
    arrived = swap_rows(send, 0)
    quarter = half // 2
    send, keep = call(
        add_kernel,
        "add_halves",
        [SMEM, VMEM, VMEM],
        [struct((taps, quarter, width), BF16), struct((taps, quarter, width), F32)],
        (where, keep, arrived),
    )
    count = lax.axis_size("cout")
    arrived = lax.ppermute(send, "cout", [(i, i ^ 2) for i in range(count)])
    lanes = 128
    tiles = -(-len(tap_of) // parts)
    piece = (tiles, quarter, lanes)
    *sends, keep = call(
        pack_kernel,
        "pack_parts",
        [SMEM, VMEM, VMEM],
        [struct(piece, BF16)] * (parts - 1) + [struct(piece, F32)],
        (where, keep, arrived),
        [pltpu.VMEM((parts, *piece), F32)],
    )
    arrived = [
        lax.ppermute(value, "cin", [(i, i ^ (k + 1)) for i in range(parts)])
        for k, value in enumerate(sends)
    ]
    return call(
        functools.partial(finish_kernel, tap_of, factor),
        "finish_sum",
        [VMEM] * parts,
        [struct(shape, F32)],
        (keep, *arrived),
    )[0]


def scattered(grads, factor):
    part = lax.psum_scatter(grads, "cin", scatter_dimension=2, tiled=True)
    return lax.psum_scatter(part, "cout", scatter_dimension=0, tiled=True) * factor


def body(volume, first_filter, second_filter, cotangent):
    chans, planes, rows, width = volume.shape
    outs, taps, ins = second_filter.shape
    assert planes == 1 and outs == chans == ins
    plane_count = lax.axis_size("cin")
    row_count = lax.axis_size("cout")
    factor = 1.0 / math.sqrt(plane_count * planes * row_count * rows * width)
    plane_at = lax.axis_index("cin")
    row_at = lax.axis_index("cout")
    where = jnp.stack([plane_at % 2, row_at % 2, row_at // 2, plane_at]).astype(jnp.int32)
    pairwise = plane_count == 4 and row_count == 4
    flops = 2 * 27 * chans * chans * rows * width

    own = by_rows(volume)
    grad_own = by_rows(cotangent)
    edge_at = where[1] * (rows - 1)
    edges = jnp.stack(
        [
            lax.dynamic_index_in_dim(own, edge_at, 0, False),
            lax.dynamic_index_in_dim(grad_own, edge_at, 0, False),
        ]
    )
    edge_own = swap_rows(edges, 1)
    edge_even = swap_corner(edges, 0)
    edge_odd = swap_corner(edges, 1)
    slabs = slabs_of(own, edge_own[0], edge_even[0], edge_odd[0])
    grad_slabs = slabs_of(grad_own, edge_own[1], edge_even[1], edge_odd[1])

    field_shape = struct((rows + 2, 3, chans, width), BF16)
    slab_shape = struct((rows, chans, width), BF16)
    sems = pltpu.SemaphoreType.DMA((9,))
    field, hidden, slope, edge = call(
        first_kernel,
        "first_conv",
        [SMEM] + [ANY] * 9 + [VMEM],
        [field_shape, slab_shape, struct((rows, chans, width), F32), struct((chans, width), BF16)],
        (where, *slabs, forward_weights(first_filter)),
        [sems],
        flops,
    )

    def partials(shape):
        if not pairwise:
            return [struct(shape, F32)]
        half = (shape[0], shape[1] // 2, shape[2])
        return [struct(half, BF16), struct(half, F32)]

    second_total = (9, outs, 3 * ins)
    grad_field, *second_part = call(
        second_grad_kernel,
        "second_filter_grad",
        [SMEM] + [ANY] * 9 + [VMEM],
        [field_shape] + partials(second_total),
        (where, *grad_slabs, hidden),
        [pltpu.VMEM(second_total, F32), sems],
        flops,
    )
    first_total = (3, outs, 9 * ins)
    first_part = call(
        first_grad_kernel,
        "first_filter_grad",
        [SMEM] + [VMEM] * 4,
        partials(first_total),
        (where, backward_weights(second_filter), grad_field, slope, field),
        [pltpu.VMEM(first_total, F32)],
        2 * flops,
    )
    hidden_slabs = slabs_of(
        hidden, swap_rows(edge, 1), swap_corner(edge, 0), swap_corner(edge, 1)
    )
    (second_out,) = call(
        second_kernel,
        "second_conv",
        [SMEM] + [ANY] * 9 + [VMEM],
        [slab_shape],
        (where, *hidden_slabs, forward_weights(second_filter)),
        [pltpu.VMEM(field_shape.shape, BF16), sems],
        flops,
    )
    second_out = second_out.transpose(1, 0, 2)[:, None]

    shape = (outs // row_count, taps, ins // plane_count)
    if pairwise:
        second_taps = [26 - (a * 9 + b * 3 + e) for b in range(3) for a in range(3) for e in range(3)]
        first_taps = [a * 9 + b * 3 + e for e in range(3) for b in range(3) for a in range(3)]
        second_sum = reduced(where, *second_part, second_taps, factor, shape)
        first_sum = reduced(where, *first_part, first_taps, factor, shape)
    else:
        second_grads = second_part[0].reshape(3, 3, outs, 3, ins).transpose(2, 1, 0, 3, 4)
        second_grads = jnp.flip(second_grads, axis=(1, 2, 3)).reshape(outs, taps, ins)
        first_grads = first_part[0].reshape(3, outs, 3, 3, ins).transpose(1, 3, 2, 0, 4)
        first_grads = first_grads.reshape(outs, taps, ins)
        second_sum = scattered(second_grads, factor)
        first_sum = scattered(first_grads, factor)
    return (second_out, first_sum, second_sum)


def solution(mesh):
    return jax.shard_map(
        body,
        mesh=mesh,
        in_specs=(
            P(None, ("grp", "cin"), "cout", None),
            P(),
            P(),
            P(None, ("grp", "cin"), "cout", None),
        ),
        out_specs=(
            P(None, ("grp", "cin"), "cout", None),
            P("cout", "grp", "cin"),
            P("cout", "grp", "cin"),
        ),
        check_vma=False,
    )
```

time: 256 us -> 122 us (0.48)
  waiting for transfers between devices: 95.5 us -> 6.04 us
  Pallas kernels: 0 us -> 39.3 us
  matrix products: 37.5 us -> 0 us
  local copies, waits for them, and re-layouts: 63.4 us -> 30.6 us
  between operations: 14.4 us -> 1.01 us
  starting transfers between devices: 32.6 us -> 43 us
  other arithmetic: 11.3 us -> 1.32 us
    reduce_scatter x2 -> x0, waiting for transfers between devices: 69.5 us -> none  [the longest x1 37.4 us: body(): lax.psum_scatter(second_grads, 'cin', scatter_dimension=2, tiled=True)]
    pallas_call x0 -> x10, Pallas kernels: none -> 39.3 us  [call(): pl.pallas_call(kernel, name=name, in_specs=ins, out_specs=[VMEM] * len(ou...]
    dot_general x54 -> x0, matrix products: 30.5 us -> none  [tap_products(): jnp.einsum('oc,ic->oi', flat_grad, window, preferred_element_type=jnp.flo...]
    unnamed x51 -> x63, local copies, waits for them, and re-layouts: 37.2 us -> 11.8 us
    unnamed x6 -> x0, waiting for transfers between devices: 23.8 us -> none
    conv_general_dilated x11 -> x0, local copies, waits for them, and re-layouts: 12.7 us -> none  [run_conv(): lax.conv_general_dilated(padded[None], kernel, (1, 1, 1), 'VALID', dimens...]
    ppermute x12 -> x31, starting transfers between devices: 31.9 us -> 43 us  [the longest x6 11.4 us: swap_planes(): return lax.ppermute(values, 'cin', links(lax.axis_size('cin'), odd))]
    broadcast_in_dim x3 -> x0, other arithmetic: 8.31 us -> none  [run_conv(): padded[None]]
  transfers between devices with their start and end apart: 16 -> 31, of which waited for: 6 -> 3; matrix products, arithmetic and copies ran while one was open for 42% -> 19% of each run, Pallas kernels for 0% -> 26%
where the time goes in v1:
time: 122 us; the launch traced here: 121 us
  starting transfers between devices  43 us (35%)
  Pallas kernels  39.3 us (32%)
  local copies, waits for them, and re-layouts  30.6 us (25%)
  waiting for transfers between devices  6.04 us (5%)
  other arithmetic  1.32 us (1%)
    pallas_call x10, Pallas kernels, call(): pl.pallas_call(kernel, name=name, in_specs=ins, out_specs=[VMEM] * len(ou...  39.3 us
    unnamed x63, local copies, waits for them, and re-layouts  11.8 us
    ppermute x6, starting transfers between devices, swap_planes(): return lax.ppermute(values, 'cin', links(lax.axis_size('cin'), odd))  11.4 us
    ppermute x13, starting transfers between devices, swap_rows(): return lax.ppermute(values, 'cout', links(lax.axis_size('cout'), odd))  9.98 us
    ppermute x6, starting transfers between devices, reduced(): lax.ppermute(value, 'cin', [(i, i ^ k + 1) for i in range(parts)])  8.9 us
    ppermute x2, starting transfers between devices, reduced(): arrived = lax.ppermute(send, 'cout', [(i, i ^ 2) for i in range(count)])  7.55 us
    reshape x5, local copies, waits for them, and re-layouts, forward_weights(): weight.reshape(outs, 3, 3, 3, ins).transpose(3, 0, 2, 1, 4)  6.22 us
    rev x1, local copies, waits for them, and re-layouts, backward_weights(): turned = jnp.flip(weight.reshape(outs, 3, 3, 3, ins), axis=(1, 2, 3))  5.28 us
  transfers between devices with their start and end apart: 31, of which 3 were waited for; matrix products, arithmetic and copies ran while one was open for 19% of the time, Pallas kernels for 26%

profile of v1, /device:TPU:0, one launch (start us, length us, event | category | flops | bytes accessed | tf_op | source)
XLA Modules:
  0.0 121.3 jit_solution(1005061647423558549)
XLA Ops:
  9.0 3.0 %collective-permute-start = (bf16[4,128,256]{2,1,0:T(8,128)(2,1)}, bf16[4,128,256]{2,1,0:T(8,128)(2,1)}, u32[]{:S(2)}, u32[]{:S(2)}) collective-permute-start(bf16[4,128,256]{2,1,0:T(8,128)(2,1)} %bitcast.37.clone.2.refs_0_), channel_id=1, source_target_pairs={{0,4},{4,0},{8,12},{12,8},{1,5},{5,1},{9,13},{13,9},{2,6},{6,2},{1... | collective-permute-start | bytes 786440 | tf_op jit(solution)/shard_map/ppermute | solution.py:26
  17.6 5.3 %rev.4 = bf16[128,3,3,3,128]{0,1,2,4,3:T(4,128)(2,1)S(1)} reverse(bf16[128,3,3,3,128]{0,1,2,4,3:T(4,128)(2,1)S(1)} %copy.20), dimensions={1,2,3} | reverse | bytes 1769472 | tf_op jit(solution)/shard_map/jit(_flip)/rev | solution.py:277
  24.8 5.7 %collective-permute-start.2 = (bf16[4,128,256]{2,1,0:T(8,128)(2,1)}, bf16[4,128,256]{2,1,0:T(8,128)(2,1)S(1)}, u32[]{:S(2)}, u32[]{:S(2)}) collective-permute-start(bf16[4,128,256]{2,1,0:T(8,128)(2,1)} %bitcast.37.clone.2.refs_0_), channel_id=1, source_target_pairs={{0,1},{1,0},{2,3},{3,2},{4,5},{5,4},{6,7},{7,6},{8,9},{9,8},{10,11... | collective-permute-start | bytes 786440 | tf_op jit(solution)/shard_map/ppermute | solution.py:30
  30.5 2.4 %collective-permute-start.16 = (bf16[4,128,256]{2,1,0:T(8,128)(2,1)S(1)}, bf16[4,128,256]{2,1,0:T(8,128)(2,1)S(1)}, u32[]{:S(2)}, u32[]{:S(2)}) collective-permute-start(bf16[4,128,256]{2,1,0:T(8,128)(2,1)S(1)} %bitcast.47), channel_id=1, source_target_pairs={{0,4},{4,0},{8,12},{12,8},{1,5},{5,1},{9,13},{13,9},{2,6},{6,2},{1... | collective-permute-start | bytes 786440 | tf_op jit(solution)/shard_map/ppermute | solution.py:26
  37.3 2.1 %collective-permute-done.16.refs_1_ = bf16[4,128,256]{2,1,0:T(8,128)(2,1)S(1)} collective-permute-done((bf16[4,128,256]{2,1,0:T(8,128)(2,1)S(1)}, bf16[4,128,256]{2,1,0:T(8,128)(2,1)S(1)}, u32[]{:S(2)}, u32[]{:S(2)}) %collective-permute-start.16) | collective-permute-done | bytes 262176 | tf_op jit(solution)/shard_map/ppermute | solution.py:26
  42.3 5.5 %first_conv.1 = (bf16[6,3,128,256]{3,2,1,0:T(8,128)(2,1)}, bf16[4,128,256]{2,1,0:T(8,128)(2,1)}, f32[4,128,256]{2,1,0:T(8,128)}, bf16[128,256]{1,0:T(8,128)(2,1)}) custom-call(s32[4]{0:T(128)} %pad_add_fusion.where, bf16[4,128,256]{2,1,0:T(8,128)(2,1)} %bitcast.37.clone.2.refs_0_, bf16[4,128,256]{2,1,0:T(8,128)(2,1)} %collective-permute-done.refs_1_, ...), custom_call_target="tpu_custom_call" | custom-call | flops 905969664 | bytes 4685840 | tf_op jit(solution)/shard_map/first_conv/pallas_call | solution.py:250
  48.8 5.7 %second_filter_grad.1 = (bf16[6,3,128,256]{3,2,1,0:T(8,128)(2,1)}, bf16[9,64,384]{2,1,0:T(8,128)(2,1)}, f32[9,64,384]{2,1,0:T(8,128)}) custom-call(s32[4]{0:T(128)} %pad_add_fusion.where, bf16[4,128,256]{2,1,0:T(8,128)(2,1)} %bitcast.50, bf16[4,128,256]{2,1,0:T(8,128)(2,1)} %copy-done.16, bf16[4,128,256]{2,1,0:T(8,128)(2,1)} %copy-done.18, ...), custom_call_target="tpu_custom_call" | custom-call | flops 905969664 | bytes 4538384 | tf_op jit(solution)/shard_map/second_filter_grad/pallas_call | solution.py:250
  54.6 9.1 %first_filter_grad.1 = (bf16[3,64,1152]{2,1,0:T(8,128)(2,1)}, f32[3,64,1152]{2,1,0:T(8,128)}) custom-call(s32[4]{0:T(128)} %pad_add_fusion.where, bf16[384,1152]{1,0:T(8,128)(2,1)} %reshape.32.weights, bf16[6,3,128,256]{3,2,1,0:T(8,128)(2,1)} %get-tuple-element.26.grad_field, f32[4,128,256]{2,1,0:T(8,128)} %get-tuple-element.27.slope, ...), custom_call_target="tpu_custom_call" | custom-call | flops 1811939328 | bytes 5095440 | tf_op jit(solution)/shard_map/first_filter_grad/pallas_call | solution.py:250
  64.1 3.2 %collective-permute-start.8 = (bf16[4,128,256]{2,1,0:T(8,128)(2,1)S(1)}, bf16[4,128,256]{2,1,0:T(8,128)(2,1)S(1)}, u32[]{:S(2)}, u32[]{:S(2)}) collective-permute-start(bf16[4,128,256]{2,1,0:T(8,128)(2,1)S(1)} %copy-done.13), channel_id=1, source_target_pairs={{0,4},{4,0},{8,12},{12,8},{1,5},{5,1},{9,13},{13,9},{2,6},{6,2},{1... | collective-permute-start | bytes 786440 | tf_op jit(solution)/shard_map/ppermute | solution.py:26
  70.0 2.2 %add_halves.3 = (bf16[9,32,384]{2,1,0:T(8,128)(2,1)}, f32[9,32,384]{2,1,0:T(8,128)}) custom-call(s32[4]{0:T(128)} %pad_add_fusion.where, f32[9,64,384]{2,1,0:T(8,128)} %get-tuple-element.37.held, bf16[9,64,384]{2,1,0:T(8,128)(2,1)} %copy-done.3), custom_call_target="tpu_custom_call" | custom-call | bytes 1990672 | tf_op jit(solution)/shard_map/add_halves/pallas_call | solution.py:250
  72.2 6.8 %collective-permute-start.27 = (bf16[9,32,384]{2,1,0:T(8,128)(2,1)}, bf16[9,32,384]{2,1,0:T(8,128)(2,1)S(1)}, u32[]{:S(2)}, u32[]{:S(2)}) collective-permute-start(bf16[9,32,384]{2,1,0:T(8,128)(2,1)} %get-tuple-element.40), channel_id=1, source_target_pairs={{0,2},{1,3},{2,0},{3,1},{4,6},{5,7},{6,4},{7,5},{8,10},{9,11},{10,... | collective-permute-start | bytes 663560 | tf_op jit(solution)/shard_map/ppermute | solution.py:294
  79.0 2.2 %add_halves.2 = (bf16[3,32,1152]{2,1,0:T(8,128)(2,1)}, f32[3,32,1152]{2,1,0:T(8,128)}) custom-call(s32[4]{0:T(128)} %pad_add_fusion.where, f32[3,64,1152]{2,1,0:T(8,128)} %get-tuple-element.29.held, bf16[3,64,1152]{2,1,0:T(8,128)(2,1)} %copy-done.2), custom_call_target="tpu_custom_call" | custom-call | bytes 1990672 | tf_op jit(solution)/shard_map/add_halves/pallas_call | solution.py:250
  82.6 2.6 %collective-permute-done.27.arrived = bf16[9,32,384]{2,1,0:T(8,128)(2,1)S(1)} collective-permute-done((bf16[9,32,384]{2,1,0:T(8,128)(2,1)}, bf16[9,32,384]{2,1,0:T(8,128)(2,1)S(1)}, u32[]{:S(2)}, u32[]{:S(2)}) %collective-permute-start.27) | collective-permute-done | bytes 221216 | tf_op jit(solution)/shard_map/ppermute | solution.py:294
  86.5 2.2 %pack_parts.3 = (bf16[7,32,128]{2,1,0:T(8,128)(2,1)}, bf16[7,32,128]{2,1,0:T(8,128)(2,1)}, bf16[7,32,128]{2,1,0:T(8,128)(2,1)}, f32[7,32,128]{2,1,0:T(8,128)}) custom-call(s32[4]{0:T(128)} %pad_add_fusion.where, f32[9,32,384]{2,1,0:T(8,128)} %get-tuple-element.39.held, bf16[9,32,384]{2,1,0:T(8,128)(2,1)} %copy-done.6), custom_call_target="tpu_custom_call" | custom-call | bytes 950288 | tf_op jit(solution)/shard_map/pack_parts/pallas_call | solution.py:250
  92.7 2.2 %pack_parts.2 = (bf16[7,32,128]{2,1,0:T(8,128)(2,1)}, bf16[7,32,128]{2,1,0:T(8,128)(2,1)}, bf16[7,32,128]{2,1,0:T(8,128)(2,1)}, f32[7,32,128]{2,1,0:T(8,128)}) custom-call(s32[4]{0:T(128)} %pad_add_fusion.where, f32[3,32,1152]{2,1,0:T(8,128)} %get-tuple-element.31.held, bf16[3,32,1152]{2,1,0:T(8,128)(2,1)} %copy-done.5), custom_call_target="tpu_custom_call" | custom-call | bytes 950288 | tf_op jit(solution)/shard_map/pack_parts/pallas_call | solution.py:250
  94.9 2.2 %collective-permute-start.29 = (bf16[7,32,128]{2,1,0:T(8,128)(2,1)S(1)}, bf16[7,32,128]{2,1,0:T(8,128)(2,1)S(1)}, u32[]{:S(2)}, u32[]{:S(2)}) collective-permute-start(bf16[7,32,128]{2,1,0:T(8,128)(2,1)S(1)} %copy-done.28), channel_id=1, source_target_pairs={{0,8},{4,12},{8,0},{12,4},{1,9},{5,13},{9,1},{13,5},{2,10},{6,14},... | collective-permute-start | bytes 172040 | tf_op jit(solution)/shard_map/ppermute | solution.py:307
  97.1 2.3 %collective-permute-start.30 = (bf16[7,32,128]{2,1,0:T(8,128)(2,1)S(1)}, bf16[7,32,128]{2,1,0:T(8,128)(2,1)S(1)}, u32[]{:S(2)}, u32[]{:S(2)}) collective-permute-start(bf16[7,32,128]{2,1,0:T(8,128)(2,1)S(1)} %copy-done.27), channel_id=1, source_target_pairs={{0,12},{4,8},{8,4},{12,0},{1,13},{5,9},{9,5},{13,1},{2,14},{6,10},... | collective-permute-start | bytes 172040 | tf_op jit(solution)/shard_map/ppermute | solution.py:307
  99.5 2.1 %collective-permute-start.24 = (bf16[7,32,128]{2,1,0:T(8,128)(2,1)}, bf16[7,32,128]{2,1,0:T(8,128)(2,1)S(1)}, u32[]{:S(2)}, u32[]{:S(2)}) collective-permute-start(bf16[7,32,128]{2,1,0:T(8,128)(2,1)} %get-tuple-element.35), channel_id=1, source_target_pairs={{0,8},{4,12},{8,0},{12,4},{1,9},{5,13},{9,1},{13,5},{2,10},{6,14},... | collective-permute-start | bytes 172040 | tf_op jit(solution)/shard_map/ppermute | solution.py:307
  101.6 2.3 %collective-permute-start.25 = (bf16[7,32,128]{2,1,0:T(8,128)(2,1)}, bf16[7,32,128]{2,1,0:T(8,128)(2,1)S(1)}, u32[]{:S(2)}, u32[]{:S(2)}) collective-permute-start(bf16[7,32,128]{2,1,0:T(8,128)(2,1)} %get-tuple-element.36), channel_id=1, source_target_pairs={{0,12},{4,8},{8,4},{12,0},{1,13},{5,9},{9,5},{13,1},{2,14},{6,10},... | collective-permute-start | bytes 172040 | tf_op jit(solution)/shard_map/ppermute | solution.py:307
  103.9 5.2 %second_conv.1 = bf16[4,128,256]{2,1,0:T(8,128)(2,1)} custom-call(s32[4]{0:T(128)} %pad_add_fusion.where, bf16[4,128,256]{2,1,0:T(8,128)(2,1)} %get-tuple-element.24.refs_0_.refs_9_, bf16[4,128,256]{2,1,0:T(8,128)(2,1)} %copy-done.14, bf16[4,128,256]{2,1,0:T(8,128)(2,1)} %copy-done.15, bf16[4,128,256]{2,1,0:T(8,128)(2,1)} %copy-done.17, ...), custom_call_target="tpu_custom_call" | custom-call | flops 905969664 | bytes 2916368 | tf_op jit(solution)/shard_map/second_conv/pallas_call | solution.py:250
  111.5 2.5 %finish_sum.3 = f32[32,27,32]{2,1,0:T(8,128)} custom-call(f32[7,32,128]{2,1,0:T(8,128)} %get-tuple-element.41.held, bf16[7,32,128]{2,1,0:T(8,128)(2,1)} %copy-done.7, bf16[7,32,128]{2,1,0:T(8,128)(2,1)} %copy-done.9, bf16[7,32,128]{2,1,0:T(8,128)(2,1)} %copy-done.11), custom_call_target="tpu_custom_call" | custom-call | bytes 397312 | tf_op jit(solution)/shard_map/finish_sum/pallas_call | solution.py:250
  114.0 2.1 %copy.24 = f32[32,27,32]{2,0,1:T(8,128)} copy(f32[32,27,32]{2,1,0:T(8,128)} %finish_sum.3) | data formatting | bytes 221184
  116.8 2.5 %finish_sum.2 = f32[32,27,32]{2,1,0:T(8,128)} custom-call(f32[7,32,128]{2,1,0:T(8,128)} %get-tuple-element.33.held, bf16[7,32,128]{2,1,0:T(8,128)(2,1)} %copy-done.8, bf16[7,32,128]{2,1,0:T(8,128)(2,1)} %copy-done.10, bf16[7,32,128]{2,1,0:T(8,128)(2,1)} %copy-done.12), custom_call_target="tpu_custom_call" | custom-call | bytes 397312 | tf_op jit(solution)/shard_map/finish_sum/pallas_call | solution.py:250
  119.3 2.1 %copy.23 = f32[32,27,32]{2,0,1:T(8,128)} copy(f32[32,27,32]{2,1,0:T(8,128)} %finish_sum.2) | data formatting | bytes 221184
  (125 shorter events, 36.8 us)
Async XLA Ops:
  5.0 19.8 %collective-permute-start.7 = (bf16[2,128,256]{2,1,0:T(8,128)(2,1)}, bf16[2,128,256]{2,1,0:T(8,128)(2,1)}, u32[]{:S(2)}, u32[]{:S(2)}) collective-permute-start(bf16[2,128,256]{2,1,0:T(8,128)(2,1)} %pad_maximum_fusion), channel_id=1, source_target_pairs={{5,10},{6,9},{9,6},{10,5},{21,26},{22,25},{25,22},{26,21}} | collective-permute-start | bytes 393224 | tf_op jit(solution)/shard_map/ppermute | solution.py:40
  6.3 24.2 %collective-permute-start.6 = (bf16[2,128,256]{2,1,0:T(8,128)(2,1)}, bf16[2,128,256]{2,1,0:T(8,128)(2,1)}, u32[]{:S(2)}, u32[]{:S(2)}) collective-permute-start(bf16[2,128,256]{2,1,0:T(8,128)(2,1)} %pad_maximum_fusion), channel_id=1, source_target_pairs={{1,6},{2,5},{5,2},{6,1},{9,14},{10,13},{13,10},{14,9},{17,22},{18,... | collective-permute-start | bytes 393224 | tf_op jit(solution)/shard_map/ppermute | solution.py:40
  7.6 25.3 %collective-permute-start.5 = (bf16[2,128,256]{2,1,0:T(8,128)(2,1)}, bf16[2,128,256]{2,1,0:T(8,128)(2,1)}, u32[]{:S(2)}, u32[]{:S(2)}) collective-permute-start(bf16[2,128,256]{2,1,0:T(8,128)(2,1)} %pad_maximum_fusion), channel_id=1, source_target_pairs={{1,2},{2,1},{5,6},{6,5},{9,10},{10,9},{13,14},{14,13},{17,18},{18,... | collective-permute-start | bytes 393224 | tf_op jit(solution)/shard_map/ppermute | solution.py:30
  9.0 26.2 %collective-permute-start = (bf16[4,128,256]{2,1,0:T(8,128)(2,1)}, bf16[4,128,256]{2,1,0:T(8,128)(2,1)}, u32[]{:S(2)}, u32[]{:S(2)}) collective-permute-start(bf16[4,128,256]{2,1,0:T(8,128)(2,1)} %bitcast.37.clone.2.refs_0_), channel_id=1, source_target_pairs={{0,4},{4,0},{8,12},{12,8},{1,5},{5,1},{9,13},{13,9},{2,6},{6,2},{1... | collective-permute-start | bytes 786440 | tf_op jit(solution)/shard_map/ppermute | solution.py:26
  12.0 23.2 %collective-permute-start.1 = (bf16[4,128,256]{2,1,0:T(8,128)(2,1)}, bf16[4,128,256]{2,1,0:T(8,128)(2,1)}, u32[]{:S(2)}, u32[]{:S(2)}) collective-permute-start(bf16[4,128,256]{2,1,0:T(8,128)(2,1)} %bitcast.37.clone.2.refs_0_), channel_id=1, source_target_pairs={{4,8},{8,4},{5,9},{9,5},{6,10},{10,6},{7,11},{11,7},{20,24},{24,20... | collective-permute-start | bytes 786440 | tf_op jit(solution)/shard_map/ppermute | solution.py:26
  24.8 12.4 %collective-permute-start.2 = (bf16[4,128,256]{2,1,0:T(8,128)(2,1)}, bf16[4,128,256]{2,1,0:T(8,128)(2,1)S(1)}, u32[]{:S(2)}, u32[]{:S(2)}) collective-permute-start(bf16[4,128,256]{2,1,0:T(8,128)(2,1)} %bitcast.37.clone.2.refs_0_), channel_id=1, source_target_pairs={{0,1},{1,0},{2,3},{3,2},{4,5},{5,4},{6,7},{7,6},{8,9},{9,8},{10,11... | collective-permute-start | bytes 786440 | tf_op jit(solution)/shard_map/ppermute | solution.py:30
  30.5 9.0 %collective-permute-start.16 = (bf16[4,128,256]{2,1,0:T(8,128)(2,1)S(1)}, bf16[4,128,256]{2,1,0:T(8,128)(2,1)S(1)}, u32[]{:S(2)}, u32[]{:S(2)}) collective-permute-start(bf16[4,128,256]{2,1,0:T(8,128)(2,1)S(1)} %bitcast.47), channel_id=1, source_target_pairs={{0,4},{4,0},{8,12},{12,8},{1,5},{5,1},{9,13},{13,9},{2,6},{6,2},{1... | collective-permute-start | bytes 786440 | tf_op jit(solution)/shard_map/ppermute | solution.py:26
  37.2 10.7 %collective-permute-start.18 = (bf16[4,128,256]{2,1,0:T(8,128)(2,1)S(1)}, bf16[4,128,256]{2,1,0:T(8,128)(2,1)S(1)}, u32[]{:S(2)}, u32[]{:S(2)}) collective-permute-start(bf16[4,128,256]{2,1,0:T(8,128)(2,1)S(1)} %bitcast.49), channel_id=1, source_target_pairs={{0,1},{1,0},{2,3},{3,2},{4,5},{5,4},{6,7},{7,6},{8,9},{9,8},{10,11... | collective-permute-start | bytes 786440 | tf_op jit(solution)/shard_map/ppermute | solution.py:30
  54.5 14.2 %collective-permute-start.26 = (bf16[9,64,384]{2,1,0:T(8,128)(2,1)}, bf16[9,64,384]{2,1,0:T(8,128)(2,1)S(1)}, u32[]{:S(2)}, u32[]{:S(2)}) collective-permute-start(bf16[9,64,384]{2,1,0:T(8,128)(2,1)} %get-tuple-element.38), channel_id=1, source_target_pairs={{0,1},{1,0},{2,3},{3,2},{4,5},{5,4},{6,7},{7,6},{8,9},{9,8},{10,11... | collective-permute-start | bytes 1327112 | tf_op jit(solution)/shard_map/ppermute | solution.py:30
  64.1 17.9 %collective-permute-start.8 = (bf16[4,128,256]{2,1,0:T(8,128)(2,1)S(1)}, bf16[4,128,256]{2,1,0:T(8,128)(2,1)S(1)}, u32[]{:S(2)}, u32[]{:S(2)}) collective-permute-start(bf16[4,128,256]{2,1,0:T(8,128)(2,1)S(1)} %copy-done.13), channel_id=1, source_target_pairs={{0,4},{4,0},{8,12},{12,8},{1,5},{5,1},{9,13},{13,9},{2,6},{6,2},{1... | collective-permute-start | bytes 786440 | tf_op jit(solution)/shard_map/ppermute | solution.py:26
  67.3 15.2 %collective-permute-start.9 = (bf16[4,128,256]{2,1,0:T(8,128)(2,1)S(1)}, bf16[4,128,256]{2,1,0:T(8,128)(2,1)S(1)}, u32[]{:S(2)}, u32[]{:S(2)}) collective-permute-start(bf16[4,128,256]{2,1,0:T(8,128)(2,1)S(1)} %copy-done.13), channel_id=1, source_target_pairs={{4,8},{8,4},{5,9},{9,5},{6,10},{10,6},{7,11},{11,7},{20,24},{24,20... | collective-permute-start | bytes 786440 | tf_op jit(solution)/shard_map/ppermute | solution.py:26
  68.0 13.2 %collective-permute-start.13 = (bf16[128,256]{1,0:T(8,128)(2,1)S(1)}, bf16[128,256]{1,0:T(8,128)(2,1)S(1)}, u32[]{:S(2)}, u32[]{:S(2)}) collective-permute-start(bf16[128,256]{1,0:T(8,128)(2,1)S(1)} %copy-done.25), channel_id=1, source_target_pairs={{1,2},{2,1},{5,6},{6,5},{9,10},{10,9},{13,14},{14,13},{17,18},{18,... | collective-permute-start | bytes 196616 | tf_op jit(solution)/shard_map/ppermute | solution.py:30
  68.7 13.3 %collective-permute-start.14 = (bf16[128,256]{1,0:T(8,128)(2,1)S(1)}, bf16[128,256]{1,0:T(8,128)(2,1)}, u32[]{:S(2)}, u32[]{:S(2)}) collective-permute-start(bf16[128,256]{1,0:T(8,128)(2,1)S(1)} %copy-done.25), channel_id=1, source_target_pairs={{1,6},{2,5},{5,2},{6,1},{9,14},{10,13},{13,10},{14,9},{17,22},{18,... | collective-permute-start | bytes 196616 | tf_op jit(solution)/shard_map/ppermute | solution.py:40
  72.2 13.0 %collective-permute-start.27 = (bf16[9,32,384]{2,1,0:T(8,128)(2,1)}, bf16[9,32,384]{2,1,0:T(8,128)(2,1)S(1)}, u32[]{:S(2)}, u32[]{:S(2)}) collective-permute-start(bf16[9,32,384]{2,1,0:T(8,128)(2,1)} %get-tuple-element.40), channel_id=1, source_target_pairs={{0,2},{1,3},{2,0},{3,1},{4,6},{5,7},{6,4},{7,5},{8,10},{9,11},{10,... | collective-permute-start | bytes 663560 | tf_op jit(solution)/shard_map/ppermute | solution.py:294
  82.0 15.1 %collective-permute-start.10 = (bf16[4,128,256]{2,1,0:T(8,128)(2,1)S(1)}, bf16[4,128,256]{2,1,0:T(8,128)(2,1)S(1)}, u32[]{:S(2)}, u32[]{:S(2)}) collective-permute-start(bf16[4,128,256]{2,1,0:T(8,128)(2,1)S(1)} %copy-done.13), channel_id=1, source_target_pairs={{0,1},{1,0},{2,3},{3,2},{4,5},{5,4},{6,7},{7,6},{8,9},{9,8},{10,11... | collective-permute-start | bytes 786440 | tf_op jit(solution)/shard_map/ppermute | solution.py:30
  82.0 17.4 %collective-permute-start.11 = (bf16[4,128,256]{2,1,0:T(8,128)(2,1)S(1)}, bf16[4,128,256]{2,1,0:T(8,128)(2,1)}, u32[]{:S(2)}, u32[]{:S(2)}) collective-permute-start(bf16[4,128,256]{2,1,0:T(8,128)(2,1)S(1)} %collective-permute-done.8.refs_1_), channel_id=1, source_target_pairs={{0,1},{1,0},{2,3},{3,2},{4,5},{5,4},{6,7},{7,6},{8,9},{9,8},{10,11... | collective-permute-start | bytes 786440 | tf_op jit(solution)/shard_map/ppermute | solution.py:30
  82.5 16.9 %collective-permute-start.12 = (bf16[4,128,256]{2,1,0:T(8,128)(2,1)S(1)}, bf16[4,128,256]{2,1,0:T(8,128)(2,1)}, u32[]{:S(2)}, u32[]{:S(2)}) collective-permute-start(bf16[4,128,256]{2,1,0:T(8,128)(2,1)S(1)} %collective-permute-done.9.refs_2_), channel_id=1, source_target_pairs={{0,1},{1,0},{2,3},{3,2},{4,5},{5,4},{6,7},{7,6},{8,9},{9,8},{10,11... | collective-permute-start | bytes 786440 | tf_op jit(solution)/shard_map/ppermute | solution.py:30
  85.2 9.7 %collective-permute-start.15 = (bf16[128,256]{1,0:T(8,128)(2,1)S(1)}, bf16[128,256]{1,0:T(8,128)(2,1)}, u32[]{:S(2)}, u32[]{:S(2)}) collective-permute-start(bf16[128,256]{1,0:T(8,128)(2,1)S(1)} %copy-done.25), channel_id=1, source_target_pairs={{5,10},{6,9},{9,6},{10,5},{21,26},{22,25},{25,22},{26,21}} | collective-permute-start | bytes 196616 | tf_op jit(solution)/shard_map/ppermute | solution.py:40
  90.0 11.6 %collective-permute-start.28 = (bf16[7,32,128]{2,1,0:T(8,128)(2,1)}, bf16[7,32,128]{2,1,0:T(8,128)(2,1)S(1)}, u32[]{:S(2)}, u32[]{:S(2)}) collective-permute-start(bf16[7,32,128]{2,1,0:T(8,128)(2,1)} %get-tuple-element.42), channel_id=1, source_target_pairs={{0,4},{4,0},{8,12},{12,8},{1,5},{5,1},{9,13},{13,9},{2,6},{6,2},{1... | collective-permute-start | bytes 172040 | tf_op jit(solution)/shard_map/ppermute | solution.py:307
  94.9 16.0 %collective-permute-start.29 = (bf16[7,32,128]{2,1,0:T(8,128)(2,1)S(1)}, bf16[7,32,128]{2,1,0:T(8,128)(2,1)S(1)}, u32[]{:S(2)}, u32[]{:S(2)}) collective-permute-start(bf16[7,32,128]{2,1,0:T(8,128)(2,1)S(1)} %copy-done.28), channel_id=1, source_target_pairs={{0,8},{4,12},{8,0},{12,4},{1,9},{5,13},{9,1},{13,5},{2,10},{6,14},... | collective-permute-start | bytes 172040 | tf_op jit(solution)/shard_map/ppermute | solution.py:307
  97.1 13.8 %collective-permute-start.30 = (bf16[7,32,128]{2,1,0:T(8,128)(2,1)S(1)}, bf16[7,32,128]{2,1,0:T(8,128)(2,1)S(1)}, u32[]{:S(2)}, u32[]{:S(2)}) collective-permute-start(bf16[7,32,128]{2,1,0:T(8,128)(2,1)S(1)} %copy-done.27), channel_id=1, source_target_pairs={{0,12},{4,8},{8,4},{12,0},{1,13},{5,9},{9,5},{13,1},{2,14},{6,10},... | collective-permute-start | bytes 172040 | tf_op jit(solution)/shard_map/ppermute | solution.py:307
  99.4 16.7 %collective-permute-start.23 = (bf16[7,32,128]{2,1,0:T(8,128)(2,1)}, bf16[7,32,128]{2,1,0:T(8,128)(2,1)S(1)}, u32[]{:S(2)}, u32[]{:S(2)}) collective-permute-start(bf16[7,32,128]{2,1,0:T(8,128)(2,1)} %get-tuple-element.34), channel_id=1, source_target_pairs={{0,4},{4,0},{8,12},{12,8},{1,5},{5,1},{9,13},{13,9},{2,6},{6,2},{1... | collective-permute-start | bytes 172040 | tf_op jit(solution)/shard_map/ppermute | solution.py:307
  99.5 16.7 %collective-permute-start.24 = (bf16[7,32,128]{2,1,0:T(8,128)(2,1)}, bf16[7,32,128]{2,1,0:T(8,128)(2,1)S(1)}, u32[]{:S(2)}, u32[]{:S(2)}) collective-permute-start(bf16[7,32,128]{2,1,0:T(8,128)(2,1)} %get-tuple-element.35), channel_id=1, source_target_pairs={{0,8},{4,12},{8,0},{12,4},{1,9},{5,13},{9,1},{13,5},{2,10},{6,14},... | collective-permute-start | bytes 172040 | tf_op jit(solution)/shard_map/ppermute | solution.py:307
  101.6 14.5 %collective-permute-start.25 = (bf16[7,32,128]{2,1,0:T(8,128)(2,1)}, bf16[7,32,128]{2,1,0:T(8,128)(2,1)S(1)}, u32[]{:S(2)}, u32[]{:S(2)}) collective-permute-start(bf16[7,32,128]{2,1,0:T(8,128)(2,1)} %get-tuple-element.36), channel_id=1, source_target_pairs={{0,12},{4,8},{8,4},{12,0},{1,13},{5,9},{9,5},{13,1},{2,14},{6,10},... | collective-permute-start | bytes 172040 | tf_op jit(solution)/shard_map/ppermute | solution.py:307
  (36 other events, 257.8 us)

commit v2 on v1

v2 whole, which is shorter than its diff:
```python
import functools
import math

import jax
import jax.numpy as jnp
from jax import lax
from jax.experimental import pallas as pl
from jax.experimental.pallas import tpu as pltpu
from jax.sharding import PartitionSpec as P

VMEM = pl.BlockSpec(memory_space=pltpu.VMEM)
SMEM = pl.BlockSpec(memory_space=pltpu.SMEM)
F32 = jnp.float32
BF16 = jnp.bfloat16
LIMIT = 14 * 1024 * 1024


def links(count, odd):
    pairs = []
    for i in range(odd, count - 1, 2):
        pairs += [(i, i + 1), (i + 1, i)]
    return pairs


def swap_planes(values, odd):
    return lax.ppermute(values, "cin", links(lax.axis_size("cin"), odd))


def swap_rows(values, odd):
    return lax.ppermute(values, "cout", links(lax.axis_size("cout"), odd))


def swap_corner(values, odd):
    count = lax.axis_size("cout")
    pairs = [
        (a * count + c, b * count + d)
        for a, b in links(lax.axis_size("cin"), odd)
        for c, d in links(count, 1)
    ]
    return lax.ppermute(values, ("cin", "cout"), pairs)


def shift_up(values):
    lane = lax.broadcasted_iota(jnp.int32, values.shape, 1)
    return jnp.where(lane == 0, 0.0, pltpu.roll(values, 1, 1))


def shift_down(values):
    width = values.shape[1]
    lane = lax.broadcasted_iota(jnp.int32, values.shape, 1)
    return jnp.where(lane == width - 1, 0.0, pltpu.roll(values, width - 1, 1))


def spread(values):
    wide = values.astype(F32)
    return jnp.concatenate(
        [shift_down(wide).astype(BF16), values, shift_up(wide).astype(BF16)], axis=0
    )


def combine(products):
    chans = products.shape[0] // 3
    return (
        products[chans : 2 * chans]
        + shift_up(products[:chans])
        + shift_down(products[2 * chans :])
    )


def planes_of(where):
    return (1, 2 * (1 - where[0]), 2 * where[0])


def fill(where, slabs, edges, field):
    rows = slabs[0].shape[0]
    row = where[1]
    for k, plane in enumerate(planes_of(where)):
        for r in range(rows):
            field[1 + r, plane] = slabs[k][r]
        field[(1 - row) * (rows + 1), plane] = slabs[3 + k][row * (rows - 1)]
        field[row * (rows + 1), plane] = edges[k][...]


def halves(where, quarter):
    mine = where[1]
    return [pl.ds(pl.multiple_of(2 * h * quarter + mine * quarter, quarter), quarter) for h in range(2)]


def fill_pair(where, slabs, edges, pair_edges, field, split):
    rows = slabs[0].shape[0]
    row = where[1]

    def put(at, plane, value):
        if not split:
            field[at, plane] = value[...]
            return
        quarter = field.shape[2] // 2
        for h, part in enumerate(halves(where, quarter)):
            field[at, plane, h * quarter : (h + 1) * quarter] = value[part]

    for k, plane in enumerate(planes_of(where)):
        for r in range(rows):
            put(1 + row * rows + r, plane, slabs[k].at[r])
            put(1 + (1 - row) * rows + r, plane, slabs[3 + k].at[r])
        put(row * (2 * rows + 1), plane, edges[k])
        put((1 - row) * (2 * rows + 1), plane, pair_edges[k])


def window(field, row):
    block = field[row : row + 3]
    return block.reshape(-1, block.shape[-1])


def conv_rows(weights, field, row):
    return combine(jnp.dot(weights[...], window(field, row), preferred_element_type=F32))


def prepare_kernel(values, out):
    out[...] = jnp.transpose(values[:, 0], (1, 0, 2))


def prepare_pair_kernel(where, values, other, out, edges):
    out[...] = jnp.transpose(values[:, 0], (1, 0, 2))
    at = where[1] * (out.shape[0] - 1)
    edges[0] = other[at]
    edges[1] = out[at]


def edge_kernel(where, *refs):
    out = refs[-1]
    for k, slab in enumerate(refs[:-1]):
        out[k] = slab[where[1] * (slab.shape[0] - 1)]


def weights_kernel(first, second, first_out, second_out, back_out):
    chans = first.shape[1]
    for b in range(3):
        for a in range(3):
            for e in range(3):
                tap = a * 9 + b * 3 + e
                at = (
                    slice(e * chans, (e + 1) * chans),
                    slice((b * 3 + a) * chans, (b * 3 + a + 1) * chans),
                )
                first_out[at] = first[tap]
                second_out[at] = second[tap]
                back_out[at] = second[26 - tap].T


def first_kernel(where, *refs):
    slabs = refs[:6]
    edges = [ref.at[0] for ref in refs[6:9]]
    weights, hidden, slope, field = refs[9:]
    fill(where, slabs, edges, field)
    for row in range(hidden.shape[0]):
        value = conv_rows(weights, field, row)
        gate = 1.0 / (1.0 + jnp.exp(-value))
        hidden[row] = (value * gate).astype(BF16)
        slope[row] = gate * (1.0 + value * (1.0 - gate))


def second_kernel(where, *refs):
    slabs = refs[:6]
    packed, weights, out, field, held = refs[6:]
    fill(where, slabs, [packed.at[k] for k in range(3)], field)
    for row in range(held.shape[0]):
        held[row] = conv_rows(weights, field, row).astype(BF16)
    out[:, 0] = jnp.transpose(held[...], (1, 0, 2))


def grad_kernel(where, *refs):
    slabs = refs[:6]
    edges = [ref.at[1] for ref in refs[6:9]]
    weights, slope, keep, *rest = refs[9:]
    *send, field, whole = rest
    fill(where, slabs, edges, field)
    for row in range(slope.shape[0]):
        grad = (conv_rows(weights, field, row) * slope[row]).astype(BF16)
        if not send:
            keep[row] = grad
        else:
            whole[...] = grad
            quarter = keep.shape[1] // 2
            for h in range(2):
                at = pl.ds(h * quarter, quarter)
                mine = pl.ds(pl.multiple_of((2 * h + where[1]) * quarter, quarter), quarter)
                theirs = pl.ds(pl.multiple_of((2 * h + 1 - where[1]) * quarter, quarter), quarter)
                keep[row, at] = whole[mine]
                send[0][row, at] = whole[theirs]


def pair_off(where, total, send, keep):
    width = send.shape[1]
    mine = pl.multiple_of(where[2] * width, width)
    theirs = pl.multiple_of((1 - where[2]) * width, width)
    send[...] = total[:, pl.ds(theirs, width)].astype(BF16)
    keep[...] = total[:, pl.ds(mine, width)]


def ordered(where, own, pair, both):
    rows = own.shape[0]
    for r in range(rows):
        both[where[1] * rows + r] = own[r]
        both[(1 - where[1]) * rows + r] = pair[r]


def second_grad_kernel(where, *refs):
    slabs = refs[:6]
    edges = [ref.at[1] for ref in refs[6:9]]
    pair_edges = [ref.at[1] for ref in refs[9:12]]
    hidden, pair_hidden, send, keep, field, both, total = refs[12:]
    fill_pair(where, slabs, edges, pair_edges, field, True)
    ordered(where, hidden, pair_hidden, both)
    for row in range(both.shape[0]):
        part = lax.dot_general(
            window(field, row),
            spread(both[row]),
            (((1,), (1,)), ((), ())),
            preferred_element_type=F32,
        ).reshape(total.shape)
        total[...] = part if row == 0 else total[...] + part
    pair_off(where, total, send, keep)


def first_grad_kernel(where, *refs):
    slabs = refs[:6]
    edges = [ref.at[0] for ref in refs[6:9]]
    pair_edges = [ref.at[0] for ref in refs[9:12]]
    grad, pair_grad, send, keep, field, both, total = refs[12:]
    fill_pair(where, slabs, edges, pair_edges, field, False)
    ordered(where, grad, pair_grad, both)
    for row in range(both.shape[0]):
        part = lax.dot_general(
            spread(both[row]),
            window(field, row),
            (((1,), (1,)), ((), ())),
            preferred_element_type=F32,
        ).reshape(total.shape)
        total[...] = part if row == 0 else total[...] + part
    pair_off(where, total, send, keep)


def second_total_kernel(where, *refs):
    slabs = refs[:6]
    edges = [ref.at[1] for ref in refs[6:9]]
    hidden, total, field = refs[9:]
    fill(where, slabs, edges, field)
    for row in range(hidden.shape[0]):
        part = lax.dot_general(
            window(field, row),
            spread(hidden[row]),
            (((1,), (1,)), ((), ())),
            preferred_element_type=F32,
        ).reshape(total.shape)
        total[...] = part if row == 0 else total[...] + part


def first_total_kernel(where, *refs):
    slabs = refs[:6]
    edges = [ref.at[0] for ref in refs[6:9]]
    grad, total, field = refs[9:]
    fill(where, slabs, edges, field)
    for row in range(grad.shape[0]):
        part = lax.dot_general(
            spread(grad[row]),
            window(field, row),
            (((1,), (1,)), ((), ())),
            preferred_element_type=F32,
        ).reshape(total.shape)
        total[...] = part if row == 0 else total[...] + part


def pack_kernel(where, held, arrived, *refs):
    sends = refs[:-2]
    keep, packed = refs[-2:]
    parts, tiles, outs, lanes = packed.shape
    group = lanes // parts
    per = held.shape[2] // lanes
    sums = {}
    for n in range(held.shape[0] * per):
        at = (n // per, slice(None), slice(n % per * lanes, (n % per + 1) * lanes))
        sums[n] = held[at] + arrived[at].astype(F32)
    lane = lax.broadcasted_iota(jnp.int32, (outs, lanes), 1) // group
    for tile in range(tiles):
        for part in range(parts):
            value = jnp.zeros((outs, lanes), F32)
            for place in range(parts):
                n = tile * parts + place
                if n in sums:
                    turned = sums[n]
                    if place != part:
                        turned = pltpu.roll(turned, (place - part) % parts * group, 1)
                    value = jnp.where(lane == place, turned, value)
            packed[part, tile] = value
    mine = where[3]
    keep[...] = packed[mine]
    for k, send in enumerate(sends):
        send[...] = packed[mine ^ (k + 1)].astype(BF16)


def finish_kernel(tap_of, factor, held, *refs):
    out = refs[-1]
    tiles, outs, lanes = held.shape
    group = out.shape[2]
    places = lanes // group
    for tile in range(tiles):
        total = held[tile]
        for arrived in refs[:-1]:
            total = total + arrived[tile].astype(F32)
        total = total * factor
        for place in range(places):
            n = tile * places + place
            if n < len(tap_of):
                out[tap_of[n]] = total[:, place * group : (place + 1) * group]


def struct(shape, dtype):
    return jax.ShapeDtypeStruct(shape, dtype)


def call(kernel, name, out_shapes, args, scratch=(), flops=0, scalars=True):
    moved = sum(math.prod(a.shape) * a.dtype.itemsize for a in (*args, *out_shapes))
    return pl.pallas_call(
        kernel,
        name=name,
        in_specs=[SMEM] * scalars + [VMEM] * (len(args) - scalars),
        out_specs=[VMEM] * len(out_shapes),
        out_shape=out_shapes,
        scratch_shapes=[pltpu.VMEM(s.shape, s.dtype) for s in scratch],
        cost_estimate=pl.CostEstimate(flops=flops, bytes_accessed=moved, transcendentals=0),
        compiler_params=pltpu.CompilerParams(vmem_limit_bytes=LIMIT),
    )(*args)


def slabs_of(own):
    planes = (own, swap_planes(own, 0), swap_planes(own, 1))
    return planes + tuple(swap_rows(p, 0) for p in planes)


def reduced(where, send, keep, tap_of, factor, shape):
    taps, outs, width = keep.shape
    parts = lax.axis_size("cin")
    count = lax.axis_size("cout")
    arrived = lax.ppermute(send, "cout", [(i, i ^ 2) for i in range(count)])
    lanes = 128
    tiles = -(-len(tap_of) // parts)
    piece = (tiles, outs, lanes)
    *sends, keep = call(
        pack_kernel,
        "pack_parts",
        [struct(piece, BF16)] * (parts - 1) + [struct(piece, F32)],
        (where, keep, arrived),
        [struct((parts, *piece), F32)],
    )
    arrived = [
        lax.ppermute(value, "cin", [(i, i ^ (k + 1)) for i in range(parts)])
        for k, value in enumerate(sends)
    ]
    (total,) = call(
        functools.partial(finish_kernel, tap_of, factor),
        "finish_sum",
        [struct((shape[1], shape[0], shape[2]), F32)],
        (keep, *arrived),
        scalars=False,
    )
    return total.transpose(1, 0, 2)


def scattered(grads, factor):
    part = lax.psum_scatter(grads, "cin", scatter_dimension=2, tiled=True)
    return lax.psum_scatter(part, "cout", scatter_dimension=0, tiled=True) * factor


def body(volume, first_filter, second_filter, cotangent):
    chans, planes, rows, width = volume.shape
    outs, taps, ins = second_filter.shape
    assert planes == 1 and outs == chans == ins
    plane_count = lax.axis_size("cin")
    row_count = lax.axis_size("cout")
    factor = 1.0 / math.sqrt(plane_count * planes * row_count * rows * width)
    plane_at = lax.axis_index("cin")
    row_at = lax.axis_index("cout")
    where = jnp.stack([plane_at % 2, row_at % 2, row_at // 2, plane_at]).astype(jnp.int32)
    pairwise = plane_count == 4 and row_count == 4
    flops = 2 * 27 * chans * chans * rows * width
    slab = struct((rows, chans, width), BF16)
    field = struct((rows + 2, 3, chans, width), BF16)
    matrix = struct((3 * chans, 9 * chans), BF16)

    (own,) = call(prepare_kernel, "prepare_volume", [slab], (volume,), scalars=False)
    grad_own, edge = call(
        prepare_pair_kernel,
        "prepare_cotangent",
        [slab, struct((2, chans, width), BF16)],
        (where, cotangent, own),
    )
    slabs = slabs_of(own)
    edges = (swap_rows(edge, 1), swap_corner(edge, 0), swap_corner(edge, 1))
    grad_slabs = slabs_of(grad_own)
    first_weights, second_weights, back_weights = call(
        weights_kernel,
        "weights",
        [matrix] * 3,
        (first_filter.transpose(1, 0, 2), second_filter.transpose(1, 0, 2)),
        scalars=False,
    )
    hidden, slope = call(
        first_kernel,
        "first_conv",
        [slab, struct(slab.shape, F32)],
        (where, *slabs, *edges, first_weights),
        [field],
        flops,
    )
    half = struct((rows, chans // 2, width), BF16)
    grads = call(
        grad_kernel,
        "hidden_grad",
        [half, half] if pairwise else [slab],
        (where, *grad_slabs, *edges, back_weights, slope),
        [field, struct((chans, width), BF16)],
        flops,
    )
    shape = (outs // row_count, taps, ins // plane_count)
    hidden_slabs = slabs_of(hidden)
    if pairwise:
        pair_edges = tuple(swap_rows(e, 0) for e in edges)
        wide = 2 * rows + 2
        block = shape[0]
        second_part = call(
            second_grad_kernel,
            "second_filter_grad",
            [struct((9, block, 3 * ins), BF16), struct((9, block, 3 * ins), F32)],
            (where, *grad_slabs, *edges, *pair_edges, hidden, hidden_slabs[3]),
            [
                struct((wide, 3, 2 * block, width), BF16),
                struct((2 * rows, chans, width), BF16),
                struct((9, 2 * block, 3 * ins), F32),
            ],
            flops,
        )
        first_part = call(
            first_grad_kernel,
            "first_filter_grad",
            [struct((3, block, 9 * ins), BF16), struct((3, block, 9 * ins), F32)],
            (where, *slabs, *edges, *pair_edges, grads[0], swap_rows(grads[1], 0)),
            [
                struct((wide, 3, chans, width), BF16),
                struct((2 * rows, 2 * block, width), BF16),
                struct((3, 2 * block, 9 * ins), F32),
            ],
            flops,
        )
        steps = range(3)
        second_taps = [26 - (a * 9 + b * 3 + e) for b in steps for a in steps for e in steps]
        first_taps = [a * 9 + b * 3 + e for e in steps for b in steps for a in steps]
        second_sum = reduced(where, *second_part, second_taps, factor, shape)
        first_sum = reduced(where, *first_part, first_taps, factor, shape)
    else:
        (second_total,) = call(
            second_total_kernel,
            "second_filter_grad",
            [struct((9, outs, 3 * ins), F32)],
            (where, *grad_slabs, *edges, hidden),
            [field],
            flops,
        )
        (first_total,) = call(
            first_total_kernel,
            "first_filter_grad",
            [struct((3, outs, 9 * ins), F32)],
            (where, *slabs, *edges, *grads),
            [field],
            flops,
        )
        second_total = second_total.reshape(3, 3, outs, 3, ins).transpose(2, 1, 0, 3, 4)
        second_total = jnp.flip(second_total, axis=(1, 2, 3)).reshape(outs, taps, ins)
        first_total = first_total.reshape(3, outs, 3, 3, ins).transpose(1, 3, 2, 0, 4)
        second_sum = scattered(second_total, factor)
        first_sum = scattered(first_total.reshape(outs, taps, ins), factor)

    (packed,) = call(
        edge_kernel, "hidden_edges", [struct((3, chans, width), BF16)], (where, *hidden_slabs[:3])
    )
    (second_out,) = call(
        second_kernel,
        "second_conv",
        [struct(volume.shape, BF16)],
        (where, *hidden_slabs, swap_rows(packed, 1), second_weights),
        [field, slab],
        flops,
    )
    return (second_out, first_sum, second_sum)


def solution(mesh):
    return jax.shard_map(
        body,
        mesh=mesh,
        in_specs=(
            P(None, ("grp", "cin"), "cout", None),
            P(),
            P(),
            P(None, ("grp", "cin"), "cout", None),
        ),
        out_specs=(
            P(None, ("grp", "cin"), "cout", None),
            P("cout", "grp", "cin"),
            P("cout", "grp", "cin"),
        ),
        check_vma=False,
    )
```

time: 122 us -> 78.6 us (0.64)
  local copies, waits for them, and re-layouts: 30.6 us -> 3.14 us
  Pallas kernels: 39.3 us -> 16.6 us
  waiting for transfers between devices: 6.04 us -> 19 us
  starting transfers between devices: 43 us -> 38.6 us
  other arithmetic: 1.32 us -> 0.08 us
    pallas_call x10 -> x13, Pallas kernels: 39.3 us -> 16.6 us  [call(): pl.pallas_call(kernel, name=name, in_specs=[SMEM] * scalars + [VMEM] * (l...]
    ppermute x6, waiting for transfers between devices: 0.02 us -> 10.9 us  [reduced(): lax.ppermute(value, 'cin', [(i, i ^ k + 1) for i in range(parts)])]
    unnamed x63 -> x8, local copies, waits for them, and re-layouts: 11.8 us -> 3.14 us
    reshape x6 -> x0, local copies, waits for them, and re-layouts: 8.15 us -> none  [the longest x5 6.22 us: forward_weights(): weight.reshape(outs, 3, 3, 3, ins).transpose(3, 0, 2, 1, 4)]
    ppermute x6, waiting for transfers between devices: 2.16 us -> 7.97 us  [swap_planes(): return lax.ppermute(values, 'cin', links(lax.axis_size('cin'), odd))]
    ppermute x2, starting transfers between devices: 7.55 us -> 1.86 us  [reduced(): arrived = lax.ppermute(send, 'cout', [(i, i ^ 2) for i in range(count)])]
    rev x1 -> x0, local copies, waits for them, and re-layouts: 5.28 us -> none  [backward_weights(): turned = jnp.flip(weight.reshape(outs, 3, 3, 3, ins), axis=(1, 2, 3))]
    squeeze x3 -> x0, local copies, waits for them, and re-layouts: 4.58 us -> none  [body(): grad_slabs = slabs_of(grad_own, edge_own[1], edge_even[1], edge_odd[1])]
  transfers between devices with their start and end apart: 31 -> 31, of which waited for: 3 -> 6; matrix products, arithmetic and copies ran while one was open for 19% -> 0% of each run, Pallas kernels for 26% -> 19%
where the time goes in v2:
time: 78.6 us; the launch traced here: 78.3 us
  starting transfers between devices  38.6 us (49%)
  waiting for transfers between devices  19 us (24%)
  Pallas kernels  16.6 us (21%)
  local copies, waits for them, and re-layouts  3.14 us (4%)
  between operations  0.91 us (1%)
    pallas_call x13, Pallas kernels, call(): pl.pallas_call(kernel, name=name, in_specs=[SMEM] * scalars + [VMEM] * (l...  16.6 us
    ppermute x15, starting transfers between devices, swap_rows(): return lax.ppermute(values, 'cout', links(lax.axis_size('cout'), odd))  14 us
    ppermute x6, starting transfers between devices, reduced(): lax.ppermute(value, 'cin', [(i, i ^ k + 1) for i in range(parts)])  11.6 us
    ppermute x6, waiting for transfers between devices, reduced(): lax.ppermute(value, 'cin', [(i, i ^ k + 1) for i in range(parts)])  10.9 us
    ppermute x6, starting transfers between devices, swap_planes(): return lax.ppermute(values, 'cin', links(lax.axis_size('cin'), odd))  9.85 us
    ppermute x6, waiting for transfers between devices, swap_planes(): return lax.ppermute(values, 'cin', links(lax.axis_size('cin'), odd))  7.97 us
    unnamed x8, local copies, waits for them, and re-layouts  3.14 us
    ppermute x2, starting transfers between devices, reduced(): arrived = lax.ppermute(send, 'cout', [(i, i ^ 2) for i in range(count)])  1.86 us
  transfers between devices with their start and end apart: 31, of which 6 were waited for; matrix products, arithmetic and copies ran while one was open for 0% of the time, Pallas kernels for 19%

profile of v2, /device:TPU:0, one launch (start us, length us, event | category | flops | bytes accessed | tf_op | source)
XLA Modules:
  0.0 78.3 jit_solution(10675329788641341500)
XLA Ops:
  0.7 1.0 %copy-done.3 = bf16[128,1,4,256]{3,2,1,0:T(4,128)(2,1)S(1)} copy-done((bf16[128,1,4,256]{3,2,1,0:T(4,128)(2,1)S(1)}, bf16[128,1,4,256]{3,2,1,0:T(4,128)(2,1)}, u32[]{:S(2)}) %copy-start.3) | copy-done | bytes 262168
  5.5 3.1 %collective-permute-start = (bf16[4,128,256]{2,1,0:T(8,128)(2,1)S(1)}, bf16[4,128,256]{2,1,0:T(8,128)(2,1)S(1)}, u32[]{:S(2)}, u32[]{:S(2)}) collective-permute-start(bf16[4,128,256]{2,1,0:T(8,128)(2,1)S(1)} %prepare_volume.1.other.refs_0_), channel_id=1, source_target_pairs={{0,4},{4,0},{8,12},{12,8},{1,5},{5,1},{9,13},{13,9},{2,6},{6,2},{1... | collective-permute-start | bytes 786440 | tf_op jit(solution)/shard_map/ppermute | solution.py:26
  9.3 8.9 %collective-permute-start.2 = (bf16[4,128,256]{2,1,0:T(8,128)(2,1)S(1)}, bf16[4,128,256]{2,1,0:T(8,128)(2,1)S(1)}, u32[]{:S(2)}, u32[]{:S(2)}) collective-permute-start(bf16[4,128,256]{2,1,0:T(8,128)(2,1)S(1)} %prepare_volume.1.other.refs_0_), channel_id=1, source_target_pairs={{0,1},{1,0},{2,3},{3,2},{4,5},{5,4},{6,7},{7,6},{8,9},{9,8},{10,11... | collective-permute-start | bytes 786440 | tf_op jit(solution)/shard_map/ppermute | solution.py:30
  18.2 1.5 %collective-permute-start.17 = (bf16[4,128,256]{2,1,0:T(8,128)(2,1)S(1)}, bf16[4,128,256]{2,1,0:T(8,128)(2,1)S(1)}, u32[]{:S(2)}, u32[]{:S(2)}) collective-permute-start(bf16[4,128,256]{2,1,0:T(8,128)(2,1)S(1)} %get-tuple-element.28.refs_0_), channel_id=1, source_target_pairs={{0,4},{4,0},{8,12},{12,8},{1,5},{5,1},{9,13},{13,9},{2,6},{6,2},{1... | collective-permute-start | bytes 786440 | tf_op jit(solution)/shard_map/ppermute | solution.py:26
  21.7 5.3 %collective-permute-done.17.refs_1_ = bf16[4,128,256]{2,1,0:T(8,128)(2,1)S(1)} collective-permute-done((bf16[4,128,256]{2,1,0:T(8,128)(2,1)S(1)}, bf16[4,128,256]{2,1,0:T(8,128)(2,1)S(1)}, u32[]{:S(2)}, u32[]{:S(2)}) %collective-permute-start.17) | collective-permute-done | bytes 262176 | tf_op jit(solution)/shard_map/ppermute | solution.py:26
  27.5 1.2 %copy-done.1 = bf16[128,27,128]{2,0,1:T(8,128)(2,1)S(1)} copy-done((bf16[128,27,128]{2,0,1:T(8,128)(2,1)S(1)}, bf16[128,27,128]{2,0,1:T(8,128)(2,1)}, u32[]{:S(2)}) %copy-start.1) | copy-done | bytes 884760
  29.8 2.0 %first_conv.1 = (bf16[4,128,256]{2,1,0:T(8,128)(2,1)S(1)}, f32[4,128,256]{2,1,0:T(8,128)S(1)}) custom-call(s32[4]{0:T(128)S(1)} %pad_add_fusion.where, bf16[4,128,256]{2,1,0:T(8,128)(2,1)S(1)} %prepare_volume.1.other.refs_0_, bf16[4,128,256]{2,1,0:T(8,128)(2,1)S(1)} %collective-permute-done.refs_1_, bf16[4,128,256]{2,1,0:T(8,128)(2,1)S(1)} %collective-permute-done.1.refs_2_, ...), custom_call_target="tpu_custom_call" | custom-call | flops 905969664 | bytes 3637264 | tf_op jit(solution)/shard_map/first_conv/pallas_call | solution.py:323
  31.9 1.9 %hidden_grad.1 = (bf16[4,64,256]{2,1,0:T(8,128)(2,1)S(1)}, bf16[4,64,256]{2,1,0:T(8,128)(2,1)S(1)}) custom-call(s32[4]{0:T(128)S(1)} %pad_add_fusion.where, bf16[4,128,256]{2,1,0:T(8,128)(2,1)S(1)} %get-tuple-element.28.refs_0_, bf16[4,128,256]{2,1,0:T(8,128)(2,1)S(1)} %collective-permute-done.17.refs_1_, ...), custom_call_target="tpu_custom_call" | custom-call | flops 905969664 | bytes 3637264 | tf_op jit(solution)/shard_map/hidden_grad/pallas_call | solution.py:323
  34.4 3.2 %collective-permute-start.8 = (bf16[4,128,256]{2,1,0:T(8,128)(2,1)S(1)}, bf16[4,128,256]{2,1,0:T(8,128)(2,1)S(1)}, u32[]{:S(2)}, u32[]{:S(2)}) collective-permute-start(bf16[4,128,256]{2,1,0:T(8,128)(2,1)S(1)} %get-tuple-element.26.refs_0_.refs_12_), channel_id=1, source_target_pairs={{0,4},{4,0},{8,12},{12,8},{1,5},{5,1},{9,13},{13,9},{2,6},{6,2},{1... | collective-permute-start | bytes 786440 | tf_op jit(solution)/shard_map/ppermute | solution.py:26
  38.5 2.3 %first_filter_grad.1 = (bf16[3,32,1152]{2,1,0:T(8,128)(2,1)S(1)}, f32[3,32,1152]{2,1,0:T(8,128)S(1)}) custom-call(s32[4]{0:T(128)S(1)} %pad_add_fusion.where, bf16[4,128,256]{2,1,0:T(8,128)(2,1)S(1)} %prepare_volume.1.other.refs_0_, bf16[4,128,256]{2,1,0:T(8,128)(2,1)S(1)} %collective-permute-done.refs_1_, ...), custom_call_target="tpu_custom_call" | custom-call | flops 905969664 | bytes 3285008 | tf_op jit(solution)/shard_map/first_filter_grad/pallas_call | solution.py:323
  41.8 2.7 %collective-permute-done.8.refs_1_ = bf16[4,128,256]{2,1,0:T(8,128)(2,1)S(1)} collective-permute-done((bf16[4,128,256]{2,1,0:T(8,128)(2,1)S(1)}, bf16[4,128,256]{2,1,0:T(8,128)(2,1)S(1)}, u32[]{:S(2)}, u32[]{:S(2)}) %collective-permute-start.8) | collective-permute-done | bytes 262176 | tf_op jit(solution)/shard_map/ppermute | solution.py:26
  45.0 2.1 %second_filter_grad.1 = (bf16[9,32,384]{2,1,0:T(8,128)(2,1)S(1)}, f32[9,32,384]{2,1,0:T(8,128)S(1)}) custom-call(s32[4]{0:T(128)S(1)} %pad_add_fusion.where, bf16[4,128,256]{2,1,0:T(8,128)(2,1)S(1)} %get-tuple-element.28.refs_0_, bf16[4,128,256]{2,1,0:T(8,128)(2,1)S(1)} %collective-permute-done.17.refs_1_, ...), custom_call_target="tpu_custom_call" | custom-call | flops 905969664 | bytes 3547152 | tf_op jit(solution)/shard_map/second_filter_grad/pallas_call | solution.py:323
  49.3 1.0 %pack_parts.2 = (bf16[7,32,128]{2,1,0:T(8,128)(2,1)S(1)}, bf16[7,32,128]{2,1,0:T(8,128)(2,1)S(1)}, bf16[7,32,128]{2,1,0:T(8,128)(2,1)S(1)}, f32[7,32,128]{2,1,0:T(8,128)S(1)}) custom-call(s32[4]{0:T(128)S(1)} %pad_add_fusion.where, f32[3,32,1152]{2,1,0:T(8,128)S(1)} %get-tuple-element.33.held, bf16[3,32,1152]{2,1,0:T(8,128)(2,1)S(1)} %collective-permute-done.23.arrived), custom_call_target="tpu_custom_call" | custom-call | bytes 950288 | tf_op jit(solution)/shard_map/pack_parts/pallas_call | solution.py:323
  50.3 3.2 %collective-permute-start.24 = (bf16[7,32,128]{2,1,0:T(8,128)(2,1)S(1)}, bf16[7,32,128]{2,1,0:T(8,128)(2,1)S(1)}, u32[]{:S(2)}, u32[]{:S(2)}) collective-permute-start(bf16[7,32,128]{2,1,0:T(8,128)(2,1)S(1)} %get-tuple-element.36), channel_id=1, source_target_pairs={{0,4},{4,0},{8,12},{12,8},{1,5},{5,1},{9,13},{13,9},{2,6},{6,2},{1... | collective-permute-start | bytes 172040 | tf_op jit(solution)/shard_map/ppermute | solution.py:356
  53.5 2.2 %collective-permute-done.24.refs_0_ = bf16[7,32,128]{2,1,0:T(8,128)(2,1)S(1)} collective-permute-done((bf16[7,32,128]{2,1,0:T(8,128)(2,1)S(1)}, bf16[7,32,128]{2,1,0:T(8,128)(2,1)S(1)}, u32[]{:S(2)}, u32[]{:S(2)}) %collective-permute-start.24) | collective-permute-done | bytes 57376 | tf_op jit(solution)/shard_map/ppermute | solution.py:356
  55.6 2.2 %collective-permute-start.25 = (bf16[7,32,128]{2,1,0:T(8,128)(2,1)S(1)}, bf16[7,32,128]{2,1,0:T(8,128)(2,1)S(1)}, u32[]{:S(2)}, u32[]{:S(2)}) collective-permute-start(bf16[7,32,128]{2,1,0:T(8,128)(2,1)S(1)} %get-tuple-element.37), channel_id=1, source_target_pairs={{0,8},{4,12},{8,0},{12,4},{1,9},{5,13},{9,1},{13,5},{2,10},{6,14},... | collective-permute-start | bytes 172040 | tf_op jit(solution)/shard_map/ppermute | solution.py:356
  57.9 2.9 %collective-permute-done.25.refs_1_ = bf16[7,32,128]{2,1,0:T(8,128)(2,1)S(1)} collective-permute-done((bf16[7,32,128]{2,1,0:T(8,128)(2,1)S(1)}, bf16[7,32,128]{2,1,0:T(8,128)(2,1)S(1)}, u32[]{:S(2)}, u32[]{:S(2)}) %collective-permute-start.25) | collective-permute-done | bytes 57376 | tf_op jit(solution)/shard_map/ppermute | solution.py:356
  60.7 1.7 %collective-permute-start.26 = (bf16[7,32,128]{2,1,0:T(8,128)(2,1)S(1)}, bf16[7,32,128]{2,1,0:T(8,128)(2,1)S(1)}, u32[]{:S(2)}, u32[]{:S(2)}) collective-permute-start(bf16[7,32,128]{2,1,0:T(8,128)(2,1)S(1)} %get-tuple-element.38), channel_id=1, source_target_pairs={{0,12},{4,8},{8,4},{12,0},{1,13},{5,9},{9,5},{13,1},{2,14},{6,10},... | collective-permute-start | bytes 172040 | tf_op jit(solution)/shard_map/ppermute | solution.py:356
  62.4 4.6 %collective-permute-done.26.refs_2_ = bf16[7,32,128]{2,1,0:T(8,128)(2,1)S(1)} collective-permute-done((bf16[7,32,128]{2,1,0:T(8,128)(2,1)S(1)}, bf16[7,32,128]{2,1,0:T(8,128)(2,1)S(1)}, u32[]{:S(2)}, u32[]{:S(2)}) %collective-permute-start.26) | collective-permute-done | bytes 57376 | tf_op jit(solution)/shard_map/ppermute | solution.py:356
  67.9 1.0 %pack_parts.3 = (bf16[7,32,128]{2,1,0:T(8,128)(2,1)S(1)}, bf16[7,32,128]{2,1,0:T(8,128)(2,1)S(1)}, bf16[7,32,128]{2,1,0:T(8,128)(2,1)S(1)}, f32[7,32,128]{2,1,0:T(8,128)S(1)}) custom-call(s32[4]{0:T(128)S(1)} %pad_add_fusion.where, f32[9,32,384]{2,1,0:T(8,128)S(1)} %get-tuple-element.39.held, bf16[9,32,384]{2,1,0:T(8,128)(2,1)S(1)} %collective-permute-done.27.arrived), custom_call_target="tpu_custom_call" | custom-call | bytes 950288 | tf_op jit(solution)/shard_map/pack_parts/pallas_call | solution.py:323
  68.9 1.4 %collective-permute-start.28 = (bf16[7,32,128]{2,1,0:T(8,128)(2,1)S(1)}, bf16[7,32,128]{2,1,0:T(8,128)(2,1)S(1)}, u32[]{:S(2)}, u32[]{:S(2)}) collective-permute-start(bf16[7,32,128]{2,1,0:T(8,128)(2,1)S(1)} %get-tuple-element.42), channel_id=1, source_target_pairs={{0,4},{4,0},{8,12},{12,8},{1,5},{5,1},{9,13},{13,9},{2,6},{6,2},{1... | collective-permute-start | bytes 172040 | tf_op jit(solution)/shard_map/ppermute | solution.py:356
  71.0 2.3 %collective-permute-start.30 = (bf16[7,32,128]{2,1,0:T(8,128)(2,1)S(1)}, bf16[7,32,128]{2,1,0:T(8,128)(2,1)S(1)}, u32[]{:S(2)}, u32[]{:S(2)}) collective-permute-start(bf16[7,32,128]{2,1,0:T(8,128)(2,1)S(1)} %get-tuple-element.44), channel_id=1, source_target_pairs={{0,12},{4,8},{8,4},{12,0},{1,13},{5,9},{9,5},{13,1},{2,14},{6,10},... | collective-permute-start | bytes 172040 | tf_op jit(solution)/shard_map/ppermute | solution.py:356
  73.3 2.7 %second_conv.1 = bf16[128,1,4,256]{3,2,1,0:T(4,128)(2,1)} custom-call(s32[4]{0:T(128)S(1)} %pad_add_fusion.where, bf16[4,128,256]{2,1,0:T(8,128)(2,1)S(1)} %get-tuple-element.26.refs_0_.refs_12_, bf16[4,128,256]{2,1,0:T(8,128)(2,1)S(1)} %collective-permute-done.8.refs_1_, bf16[4,128,256]{2,1,0:T(8,128)(2,1)S(1)} %collective-permute-done.9.refs_2_, ...), custom_call_target="tpu_custom_call" | custom-call | flops 905969664 | bytes 2916368 | tf_op jit(solution)/shard_map/second_conv/pallas_call | solution.py:323
  76.0 1.4 %collective-permute-done.29.refs_1_ = bf16[7,32,128]{2,1,0:T(8,128)(2,1)S(1)} collective-permute-done((bf16[7,32,128]{2,1,0:T(8,128)(2,1)S(1)}, bf16[7,32,128]{2,1,0:T(8,128)(2,1)S(1)}, u32[]{:S(2)}, u32[]{:S(2)}) %collective-permute-start.29) | collective-permute-done | bytes 57376 | tf_op jit(solution)/shard_map/ppermute | solution.py:356
  (60 shorter events, 15.8 us)
Async XLA Ops:
  4.1 14.0 %collective-permute-start.6 = (bf16[2,128,256]{2,1,0:T(8,128)(2,1)S(1)}, bf16[2,128,256]{2,1,0:T(8,128)(2,1)S(1)}, u32[]{:S(2)}, u32[]{:S(2)}) collective-permute-start(bf16[2,128,256]{2,1,0:T(8,128)(2,1)S(1)} %get-tuple-element.24), channel_id=1, source_target_pairs={{1,6},{2,5},{5,2},{6,1},{9,14},{10,13},{13,10},{14,9},{17,22},{18,... | collective-permute-start | bytes 393224 | tf_op jit(solution)/shard_map/ppermute | solution.py:40
  4.8 14.9 %collective-permute-start.7 = (bf16[2,128,256]{2,1,0:T(8,128)(2,1)S(1)}, bf16[2,128,256]{2,1,0:T(8,128)(2,1)S(1)}, u32[]{:S(2)}, u32[]{:S(2)}) collective-permute-start(bf16[2,128,256]{2,1,0:T(8,128)(2,1)S(1)} %get-tuple-element.24), channel_id=1, source_target_pairs={{5,10},{6,9},{9,6},{10,5},{21,26},{22,25},{25,22},{26,21}} | collective-permute-start | bytes 393224 | tf_op jit(solution)/shard_map/ppermute | solution.py:40
  5.5 14.9 %collective-permute-start = (bf16[4,128,256]{2,1,0:T(8,128)(2,1)S(1)}, bf16[4,128,256]{2,1,0:T(8,128)(2,1)S(1)}, u32[]{:S(2)}, u32[]{:S(2)}) collective-permute-start(bf16[4,128,256]{2,1,0:T(8,128)(2,1)S(1)} %prepare_volume.1.other.refs_0_), channel_id=1, source_target_pairs={{0,4},{4,0},{8,12},{12,8},{1,5},{5,1},{9,13},{13,9},{2,6},{6,2},{1... | collective-permute-start | bytes 786440 | tf_op jit(solution)/shard_map/ppermute | solution.py:26
  8.6 12.6 %collective-permute-start.1 = (bf16[4,128,256]{2,1,0:T(8,128)(2,1)S(1)}, bf16[4,128,256]{2,1,0:T(8,128)(2,1)S(1)}, u32[]{:S(2)}, u32[]{:S(2)}) collective-permute-start(bf16[4,128,256]{2,1,0:T(8,128)(2,1)S(1)} %prepare_volume.1.other.refs_0_), channel_id=1, source_target_pairs={{4,8},{8,4},{5,9},{9,5},{6,10},{10,6},{7,11},{11,7},{20,24},{24,20... | collective-permute-start | bytes 786440 | tf_op jit(solution)/shard_map/ppermute | solution.py:26
  9.3 11.9 %collective-permute-start.2 = (bf16[4,128,256]{2,1,0:T(8,128)(2,1)S(1)}, bf16[4,128,256]{2,1,0:T(8,128)(2,1)S(1)}, u32[]{:S(2)}, u32[]{:S(2)}) collective-permute-start(bf16[4,128,256]{2,1,0:T(8,128)(2,1)S(1)} %prepare_volume.1.other.refs_0_), channel_id=1, source_target_pairs={{0,1},{1,0},{2,3},{3,2},{4,5},{5,4},{6,7},{7,6},{8,9},{9,8},{10,11... | collective-permute-start | bytes 786440 | tf_op jit(solution)/shard_map/ppermute | solution.py:30
  18.2 8.8 %collective-permute-start.17 = (bf16[4,128,256]{2,1,0:T(8,128)(2,1)S(1)}, bf16[4,128,256]{2,1,0:T(8,128)(2,1)S(1)}, u32[]{:S(2)}, u32[]{:S(2)}) collective-permute-start(bf16[4,128,256]{2,1,0:T(8,128)(2,1)S(1)} %get-tuple-element.28.refs_0_), channel_id=1, source_target_pairs={{0,4},{4,0},{8,12},{12,8},{1,5},{5,1},{9,13},{13,9},{2,6},{6,2},{1... | collective-permute-start | bytes 786440 | tf_op jit(solution)/shard_map/ppermute | solution.py:26
  19.7 7.3 %collective-permute-start.18 = (bf16[4,128,256]{2,1,0:T(8,128)(2,1)S(1)}, bf16[4,128,256]{2,1,0:T(8,128)(2,1)S(1)}, u32[]{:S(2)}, u32[]{:S(2)}) collective-permute-start(bf16[4,128,256]{2,1,0:T(8,128)(2,1)S(1)} %get-tuple-element.28.refs_0_), channel_id=1, source_target_pairs={{4,8},{8,4},{5,9},{9,5},{6,10},{10,6},{7,11},{11,7},{20,24},{24,20... | collective-permute-start | bytes 786440 | tf_op jit(solution)/shard_map/ppermute | solution.py:26
  20.4 8.8 %collective-permute-start.3 = (bf16[4,128,256]{2,1,0:T(8,128)(2,1)S(1)}, bf16[4,128,256]{2,1,0:T(8,128)(2,1)S(1)}, u32[]{:S(2)}, u32[]{:S(2)}) collective-permute-start(bf16[4,128,256]{2,1,0:T(8,128)(2,1)S(1)} %collective-permute-done.refs_1_), channel_id=1, source_target_pairs={{0,1},{1,0},{2,3},{3,2},{4,5},{5,4},{6,7},{7,6},{8,9},{9,8},{10,11... | collective-permute-start | bytes 786440 | tf_op jit(solution)/shard_map/ppermute | solution.py:30
  21.2 8.1 %collective-permute-start.4 = (bf16[4,128,256]{2,1,0:T(8,128)(2,1)S(1)}, bf16[4,128,256]{2,1,0:T(8,128)(2,1)S(1)}, u32[]{:S(2)}, u32[]{:S(2)}) collective-permute-start(bf16[4,128,256]{2,1,0:T(8,128)(2,1)S(1)} %collective-permute-done.1.refs_2_), channel_id=1, source_target_pairs={{0,1},{1,0},{2,3},{3,2},{4,5},{5,4},{6,7},{7,6},{8,9},{9,8},{10,11... | collective-permute-start | bytes 786440 | tf_op jit(solution)/shard_map/ppermute | solution.py:30
  21.2 10.6 %collective-permute-start.19 = (bf16[4,128,256]{2,1,0:T(8,128)(2,1)S(1)}, bf16[4,128,256]{2,1,0:T(8,128)(2,1)S(1)}, u32[]{:S(2)}, u32[]{:S(2)}) collective-permute-start(bf16[4,128,256]{2,1,0:T(8,128)(2,1)S(1)} %get-tuple-element.28.refs_0_), channel_id=1, source_target_pairs={{0,1},{1,0},{2,3},{3,2},{4,5},{5,4},{6,7},{7,6},{8,9},{9,8},{10,11... | collective-permute-start | bytes 786440 | tf_op jit(solution)/shard_map/ppermute | solution.py:30
  29.2 8.4 %collective-permute-start.14 = (bf16[2,128,256]{2,1,0:T(8,128)(2,1)S(1)}, bf16[2,128,256]{2,1,0:T(8,128)(2,1)S(1)}, u32[]{:S(2)}, u32[]{:S(2)}) collective-permute-start(bf16[2,128,256]{2,1,0:T(8,128)(2,1)S(1)} %collective-permute-done.5.refs_6_), channel_id=1, source_target_pairs={{0,1},{1,0},{2,3},{3,2},{4,5},{5,4},{6,7},{7,6},{8,9},{9,8},{10,11... | collective-permute-start | bytes 393224 | tf_op jit(solution)/shard_map/ppermute | solution.py:30
  29.3 9.0 %collective-permute-start.15 = (bf16[2,128,256]{2,1,0:T(8,128)(2,1)S(1)}, bf16[2,128,256]{2,1,0:T(8,128)(2,1)S(1)}, u32[]{:S(2)}, u32[]{:S(2)}) collective-permute-start(bf16[2,128,256]{2,1,0:T(8,128)(2,1)S(1)} %collective-permute-done.6.refs_7_), channel_id=1, source_target_pairs={{0,1},{1,0},{2,3},{3,2},{4,5},{5,4},{6,7},{7,6},{8,9},{9,8},{10,11... | collective-permute-start | bytes 393224 | tf_op jit(solution)/shard_map/ppermute | solution.py:30
  31.8 6.7 %collective-permute-start.16 = (bf16[2,128,256]{2,1,0:T(8,128)(2,1)S(1)}, bf16[2,128,256]{2,1,0:T(8,128)(2,1)S(1)}, u32[]{:S(2)}, u32[]{:S(2)}) collective-permute-start(bf16[2,128,256]{2,1,0:T(8,128)(2,1)S(1)} %collective-permute-done.7.refs_8_), channel_id=1, source_target_pairs={{0,1},{1,0},{2,3},{3,2},{4,5},{5,4},{6,7},{7,6},{8,9},{9,8},{10,11... | collective-permute-start | bytes 393224 | tf_op jit(solution)/shard_map/ppermute | solution.py:30
  34.4 10.1 %collective-permute-start.8 = (bf16[4,128,256]{2,1,0:T(8,128)(2,1)S(1)}, bf16[4,128,256]{2,1,0:T(8,128)(2,1)S(1)}, u32[]{:S(2)}, u32[]{:S(2)}) collective-permute-start(bf16[4,128,256]{2,1,0:T(8,128)(2,1)S(1)} %get-tuple-element.26.refs_0_.refs_12_), channel_id=1, source_target_pairs={{0,4},{4,0},{8,12},{12,8},{1,5},{5,1},{9,13},{13,9},{2,6},{6,2},{1... | collective-permute-start | bytes 786440 | tf_op jit(solution)/shard_map/ppermute | solution.py:26
  37.6 6.9 %collective-permute-start.9 = (bf16[4,128,256]{2,1,0:T(8,128)(2,1)S(1)}, bf16[4,128,256]{2,1,0:T(8,128)(2,1)S(1)}, u32[]{:S(2)}, u32[]{:S(2)}) collective-permute-start(bf16[4,128,256]{2,1,0:T(8,128)(2,1)S(1)} %get-tuple-element.26.refs_0_.refs_12_), channel_id=1, source_target_pairs={{4,8},{8,4},{5,9},{9,5},{6,10},{10,6},{7,11},{11,7},{20,24},{24,20... | collective-permute-start | bytes 786440 | tf_op jit(solution)/shard_map/ppermute | solution.py:26
  38.3 6.7 %collective-permute-start.10 = (bf16[4,128,256]{2,1,0:T(8,128)(2,1)S(1)}, bf16[4,128,256]{2,1,0:T(8,128)(2,1)S(1)}, u32[]{:S(2)}, u32[]{:S(2)}) collective-permute-start(bf16[4,128,256]{2,1,0:T(8,128)(2,1)S(1)} %get-tuple-element.26.refs_0_.refs_12_), channel_id=1, source_target_pairs={{0,1},{1,0},{2,3},{3,2},{4,5},{5,4},{6,7},{7,6},{8,9},{9,8},{10,11... | collective-permute-start | bytes 786440 | tf_op jit(solution)/shard_map/ppermute | solution.py:30
  40.8 8.4 %collective-permute-start.23 = (bf16[3,32,1152]{2,1,0:T(8,128)(2,1)S(1)}, bf16[3,32,1152]{2,1,0:T(8,128)(2,1)S(1)}, u32[]{:S(2)}, u32[]{:S(2)}) collective-permute-start(bf16[3,32,1152]{2,1,0:T(8,128)(2,1)S(1)} %get-tuple-element.34), channel_id=1, source_target_pairs={{0,2},{1,3},{2,0},{3,1},{4,6},{5,7},{6,4},{7,5},{8,10},{9,11},{10,... | collective-permute-start | bytes 663560 | tf_op jit(solution)/shard_map/ppermute | solution.py:344
  44.5 28.9 %collective-permute-start.11 = (bf16[4,128,256]{2,1,0:T(8,128)(2,1)S(1)}, bf16[4,128,256]{2,1,0:T(8,128)(2,1)S(1)}, u32[]{:S(2)}, u32[]{:S(2)}) collective-permute-start(bf16[4,128,256]{2,1,0:T(8,128)(2,1)S(1)} %collective-permute-done.8.refs_1_), channel_id=1, source_target_pairs={{0,1},{1,0},{2,3},{3,2},{4,5},{5,4},{6,7},{7,6},{8,9},{9,8},{10,11... | collective-permute-start | bytes 786440 | tf_op jit(solution)/shard_map/ppermute | solution.py:30
  44.5 28.8 %collective-permute-start.12 = (bf16[4,128,256]{2,1,0:T(8,128)(2,1)S(1)}, bf16[4,128,256]{2,1,0:T(8,128)(2,1)S(1)}, u32[]{:S(2)}, u32[]{:S(2)}) collective-permute-start(bf16[4,128,256]{2,1,0:T(8,128)(2,1)S(1)} %collective-permute-done.9.refs_2_), channel_id=1, source_target_pairs={{0,1},{1,0},{2,3},{3,2},{4,5},{5,4},{6,7},{7,6},{8,9},{9,8},{10,11... | collective-permute-start | bytes 786440 | tf_op jit(solution)/shard_map/ppermute | solution.py:30
  47.1 20.8 %collective-permute-start.27 = (bf16[9,32,384]{2,1,0:T(8,128)(2,1)S(1)}, bf16[9,32,384]{2,1,0:T(8,128)(2,1)S(1)}, u32[]{:S(2)}, u32[]{:S(2)}) collective-permute-start(bf16[9,32,384]{2,1,0:T(8,128)(2,1)S(1)} %get-tuple-element.40), channel_id=1, source_target_pairs={{0,2},{1,3},{2,0},{3,1},{4,6},{5,7},{6,4},{7,5},{8,10},{9,11},{10,... | collective-permute-start | bytes 663560 | tf_op jit(solution)/shard_map/ppermute | solution.py:344
  48.6 22.4 %collective-permute-start.13 = (bf16[3,128,256]{2,1,0:T(8,128)(2,1)S(1)}, bf16[3,128,256]{2,1,0:T(8,128)(2,1)S(1)}, u32[]{:S(2)}, u32[]{:S(2)}) collective-permute-start(bf16[3,128,256]{2,1,0:T(8,128)(2,1)S(1)} %hidden_edges.1), channel_id=1, source_target_pairs={{1,2},{2,1},{5,6},{6,5},{9,10},{10,9},{13,14},{14,13},{17,18},{18,... | collective-permute-start | bytes 589832 | tf_op jit(solution)/shard_map/ppermute | solution.py:30
  68.9 7.1 %collective-permute-start.28 = (bf16[7,32,128]{2,1,0:T(8,128)(2,1)S(1)}, bf16[7,32,128]{2,1,0:T(8,128)(2,1)S(1)}, u32[]{:S(2)}, u32[]{:S(2)}) collective-permute-start(bf16[7,32,128]{2,1,0:T(8,128)(2,1)S(1)} %get-tuple-element.42), channel_id=1, source_target_pairs={{0,4},{4,0},{8,12},{12,8},{1,5},{5,1},{9,13},{13,9},{2,6},{6,2},{1... | collective-permute-start | bytes 172040 | tf_op jit(solution)/shard_map/ppermute | solution.py:356
  70.2 7.2 %collective-permute-start.29 = (bf16[7,32,128]{2,1,0:T(8,128)(2,1)S(1)}, bf16[7,32,128]{2,1,0:T(8,128)(2,1)S(1)}, u32[]{:S(2)}, u32[]{:S(2)}) collective-permute-start(bf16[7,32,128]{2,1,0:T(8,128)(2,1)S(1)} %get-tuple-element.43), channel_id=1, source_target_pairs={{0,8},{4,12},{8,0},{12,4},{1,9},{5,13},{9,1},{13,5},{2,10},{6,14},... | collective-permute-start | bytes 172040 | tf_op jit(solution)/shard_map/ppermute | solution.py:356
  71.0 6.3 %collective-permute-start.30 = (bf16[7,32,128]{2,1,0:T(8,128)(2,1)S(1)}, bf16[7,32,128]{2,1,0:T(8,128)(2,1)S(1)}, u32[]{:S(2)}, u32[]{:S(2)}) collective-permute-start(bf16[7,32,128]{2,1,0:T(8,128)(2,1)S(1)} %get-tuple-element.44), channel_id=1, source_target_pairs={{0,12},{4,8},{8,4},{12,0},{1,13},{5,9},{9,5},{13,1},{2,14},{6,10},... | collective-permute-start | bytes 172040 | tf_op jit(solution)/shard_map/ppermute | solution.py:356
  (11 other events, 67.0 us)

commit v3 on v2

--- a/solution.py
+++ b/solution.py
@@ -30,16 +30,6 @@
     return lax.ppermute(values, "cout", links(lax.axis_size("cout"), odd))
 
 
-def swap_corner(values, odd):
-    count = lax.axis_size("cout")
-    pairs = [
-        (a * count + c, b * count + d)
-        for a, b in links(lax.axis_size("cin"), odd)
-        for c, d in links(count, 1)
-    ]
-    return lax.ppermute(values, ("cin", "cout"), pairs)
-
-
 def shift_up(values):
     lane = lax.broadcasted_iota(jnp.int32, values.shape, 1)
     return jnp.where(lane == 0, 0.0, pltpu.roll(values, 1, 1))
@@ -77,8 +67,9 @@
     for k, plane in enumerate(planes_of(where)):
         for r in range(rows):
             field[1 + r, plane] = slabs[k][r]
-        field[(1 - row) * (rows + 1), plane] = slabs[3 + k][row * (rows - 1)]
-        field[row * (rows + 1), plane] = edges[k][...]
+        inside = slabs[3 + k][row * (rows - 1)] if len(slabs) == 6 else slabs[3][k]
+        field[(1 - row) * (rows + 1), plane] = inside
+        field[row * (rows + 1), plane] = edges[k]
 
 
 def halves(where, quarter):
@@ -102,8 +93,8 @@
         for r in range(rows):
             put(1 + row * rows + r, plane, slabs[k].at[r])
             put(1 + (1 - row) * rows + r, plane, slabs[3 + k].at[r])
-        put(row * (2 * rows + 1), plane, edges[k])
-        put((1 - row) * (2 * rows + 1), plane, pair_edges[k])
+        put(row * (2 * rows + 1), plane, edges.at[k])
+        put((1 - row) * (2 * rows + 1), plane, pair_edges.at[k])
 
 
 def window(field, row):
@@ -119,17 +110,12 @@
     out[...] = jnp.transpose(values[:, 0], (1, 0, 2))
 
 
-def prepare_pair_kernel(where, values, other, out, edges):
-    out[...] = jnp.transpose(values[:, 0], (1, 0, 2))
-    at = where[1] * (out.shape[0] - 1)
-    edges[0] = other[at]
-    edges[1] = out[at]
-
-
-def edge_kernel(where, *refs):
-    out = refs[-1]
-    for k, slab in enumerate(refs[:-1]):
-        out[k] = slab[where[1] * (slab.shape[0] - 1)]
+def edge_kernel(where, own, even, odd, across, *inside):
+    last = own.shape[0] - 1
+    for k, slab in enumerate((own, even, odd)):
+        across[k] = slab[where[1] * last]
+        for out in inside:
+            out[k] = slab[(1 - where[1]) * last]
 
 
 def weights_kernel(first, second, first_out, second_out, back_out):
@@ -149,8 +135,7 @@
 
 def first_kernel(where, *refs):
     slabs = refs[:6]
-    edges = [ref.at[0] for ref in refs[6:9]]
-    weights, hidden, slope, field = refs[9:]
+    edges, weights, hidden, slope, field = refs[6:]
     fill(where, slabs, edges, field)
     for row in range(hidden.shape[0]):
         value = conv_rows(weights, field, row)
@@ -160,9 +145,9 @@
 
 
 def second_kernel(where, *refs):
-    slabs = refs[:6]
-    packed, weights, out, field, held = refs[6:]
-    fill(where, slabs, [packed.at[k] for k in range(3)], field)
+    slabs = refs[:4]
+    packed, weights, out, field, held = refs[4:]
+    fill(where, slabs, packed, field)
     for row in range(held.shape[0]):
         held[row] = conv_rows(weights, field, row).astype(BF16)
     out[:, 0] = jnp.transpose(held[...], (1, 0, 2))
@@ -170,8 +155,7 @@
 
 def grad_kernel(where, *refs):
     slabs = refs[:6]
-    edges = [ref.at[1] for ref in refs[6:9]]
-    weights, slope, keep, *rest = refs[9:]
+    edges, weights, slope, keep, *rest = refs[6:]
     *send, field, whole = rest
     fill(where, slabs, edges, field)
     for row in range(slope.shape[0]):
@@ -206,9 +190,7 @@
 
 def second_grad_kernel(where, *refs):
     slabs = refs[:6]
-    edges = [ref.at[1] for ref in refs[6:9]]
-    pair_edges = [ref.at[1] for ref in refs[9:12]]
-    hidden, pair_hidden, send, keep, field, both, total = refs[12:]
+    edges, pair_edges, hidden, pair_hidden, send, keep, field, both, total = refs[6:]
     fill_pair(where, slabs, edges, pair_edges, field, True)
     ordered(where, hidden, pair_hidden, both)
     for row in range(both.shape[0]):
@@ -224,9 +206,7 @@
 
 def first_grad_kernel(where, *refs):
     slabs = refs[:6]
-    edges = [ref.at[0] for ref in refs[6:9]]
-    pair_edges = [ref.at[0] for ref in refs[9:12]]
-    grad, pair_grad, send, keep, field, both, total = refs[12:]
+    edges, pair_edges, grad, pair_grad, send, keep, field, both, total = refs[6:]
     fill_pair(where, slabs, edges, pair_edges, field, False)
     ordered(where, grad, pair_grad, both)
     for row in range(both.shape[0]):
@@ -242,8 +222,7 @@
 
 def second_total_kernel(where, *refs):
     slabs = refs[:6]
-    edges = [ref.at[1] for ref in refs[6:9]]
-    hidden, total, field = refs[9:]
+    edges, hidden, total, field = refs[6:]
     fill(where, slabs, edges, field)
     for row in range(hidden.shape[0]):
         part = lax.dot_general(
@@ -257,8 +236,7 @@
 
 def first_total_kernel(where, *refs):
     slabs = refs[:6]
-    edges = [ref.at[0] for ref in refs[6:9]]
-    grad, total, field = refs[9:]
+    edges, grad, total, field = refs[6:]
     fill(where, slabs, edges, field)
     for row in range(grad.shape[0]):
         part = lax.dot_general(
@@ -332,30 +310,34 @@
     )(*args)
 
 
-def slabs_of(own):
-    planes = (own, swap_planes(own, 0), swap_planes(own, 1))
-    return planes + tuple(swap_rows(p, 0) for p in planes)
-
-
-def reduced(where, send, keep, tap_of, factor, shape):
+def after(value, *others):
+    return lax.optimization_barrier((value, *others))[0]
+
+
+def packed_parts(where, keep, arrived):
     taps, outs, width = keep.shape
     parts = lax.axis_size("cin")
-    count = lax.axis_size("cout")
-    arrived = lax.ppermute(send, "cout", [(i, i ^ 2) for i in range(count)])
     lanes = 128
-    tiles = -(-len(tap_of) // parts)
+    tiles = -(-taps * width // (lanes * parts))
     piece = (tiles, outs, lanes)
-    *sends, keep = call(
+    return call(
         pack_kernel,
         "pack_parts",
         [struct(piece, BF16)] * (parts - 1) + [struct(piece, F32)],
         (where, keep, arrived),
         [struct((parts, *piece), F32)],
     )
-    arrived = [
+
+
+def exchanged(sends):
+    parts = lax.axis_size("cin")
+    return [
         lax.ppermute(value, "cin", [(i, i ^ (k + 1)) for i in range(parts)])
         for k, value in enumerate(sends)
     ]
+
+
+def finished(keep, arrived, tap_of, factor, shape):
     (total,) = call(
         functools.partial(finish_kernel, tap_of, factor),
         "finish_sum",
@@ -364,6 +346,10 @@
         scalars=False,
     )
     return total.transpose(1, 0, 2)
+
+
+def cross(values):
+    return lax.ppermute(values, "cout", [(i, i ^ 2) for i in range(lax.axis_size("cout"))])
 
 
 def scattered(grads, factor):
@@ -388,15 +374,11 @@
     matrix = struct((3 * chans, 9 * chans), BF16)
 
     (own,) = call(prepare_kernel, "prepare_volume", [slab], (volume,), scalars=False)
-    grad_own, edge = call(
-        prepare_pair_kernel,
-        "prepare_cotangent",
-        [slab, struct((2, chans, width), BF16)],
-        (where, cotangent, own),
-    )
-    slabs = slabs_of(own)
-    edges = (swap_rows(edge, 1), swap_corner(edge, 0), swap_corner(edge, 1))
-    grad_slabs = slabs_of(grad_own)
+    own_even, own_odd, own_pair = swap_planes(own, 0), swap_planes(own, 1), swap_rows(own, 0)
+    (grad_own,) = call(
+        prepare_kernel, "prepare_cotangent", [slab], (cotangent,), scalars=False
+    )
+    grad_even, grad_odd = swap_planes(grad_own, 0), swap_planes(grad_own, 1)
     first_weights, second_weights, back_weights = call(
         weights_kernel,
         "weights",
@@ -404,34 +386,78 @@
         (first_filter.transpose(1, 0, 2), second_filter.transpose(1, 0, 2)),
         scalars=False,
     )
+
+    def across(own, even, odd):
+        (out,) = call(
+            edge_kernel,
+            "edges",
+            [struct((3, chans, width), BF16)],
+            (where, own, even, odd),
+        )
+        return swap_rows(out, 1)
+
+    edges = across(own, after(own_even, first_weights), own_odd)
+    slabs = (own, own_even, own_odd, own_pair, swap_rows(own_even, 0), swap_rows(own_odd, 0))
     hidden, slope = call(
         first_kernel,
         "first_conv",
         [slab, struct(slab.shape, F32)],
-        (where, *slabs, *edges, first_weights),
+        (where, *slabs, edges, first_weights),
         [field],
         flops,
+    )
+    hidden_pair = swap_rows(hidden, 0)
+    hidden_even, hidden_odd = swap_planes(hidden, 0), swap_planes(hidden, 1)
+    grad_edges = across(grad_own, grad_even, grad_odd)
+    grad_slabs = (
+        grad_own,
+        grad_even,
+        grad_odd,
+        swap_rows(grad_own, 0),
+        swap_rows(grad_even, 0),
+        swap_rows(grad_odd, 0),
     )
     half = struct((rows, chans // 2, width), BF16)
     grads = call(
         grad_kernel,
         "hidden_grad",
         [half, half] if pairwise else [slab],
-        (where, *grad_slabs, *edges, back_weights, slope),
+        (where, *grad_slabs, grad_edges, back_weights, slope),
         [field, struct((chans, width), BF16)],
         flops,
     )
     shape = (outs // row_count, taps, ins // plane_count)
-    hidden_slabs = slabs_of(hidden)
+
+    def hidden_rows(even, odd, *others):
+        across, inside = call(
+            edge_kernel,
+            "hidden_edges",
+            [struct((3, chans, width), BF16)] * 2,
+            (where, hidden, even, odd),
+        )
+        across, inside, *_ = lax.optimization_barrier((across, inside, *others))
+        return swap_rows(inside, 0), swap_rows(across, 1)
+
+    def convolved(inside, across):
+        (out,) = call(
+            second_kernel,
+            "second_conv",
+            [struct(volume.shape, BF16)],
+            (where, hidden, hidden_even, hidden_odd, inside, across, second_weights),
+            [field, slab],
+            flops,
+        )
+        return out
+
     if pairwise:
-        pair_edges = tuple(swap_rows(e, 0) for e in edges)
+        pair_edges, pair_grad_edges = swap_rows(edges, 0), swap_rows(grad_edges, 0)
         wide = 2 * rows + 2
         block = shape[0]
-        second_part = call(
+        second_send, second_keep = call(
             second_grad_kernel,
             "second_filter_grad",
             [struct((9, block, 3 * ins), BF16), struct((9, block, 3 * ins), F32)],
-            (where, *grad_slabs, *edges, *pair_edges, hidden, hidden_slabs[3]),
+            (where, *grad_slabs, grad_edges, pair_grad_edges, hidden, hidden_pair),
             [
                 struct((wide, 3, 2 * block, width), BF16),
                 struct((2 * rows, chans, width), BF16),
@@ -439,11 +465,19 @@
             ],
             flops,
         )
-        first_part = call(
+        second_arrived = cross(second_send)
+        first_send, first_keep = call(
             first_grad_kernel,
             "first_filter_grad",
             [struct((3, block, 9 * ins), BF16), struct((3, block, 9 * ins), F32)],
-            (where, *slabs, *edges, *pair_edges, grads[0], swap_rows(grads[1], 0)),
+            (
+                where,
+                *slabs,
+                edges,
+                pair_edges,
+                after(grads[0], second_send),
+                swap_rows(grads[1], 0),
+            ),
             [
                 struct((wide, 3, chans, width), BF16),
                 struct((2 * rows, 2 * block, width), BF16),
@@ -451,17 +485,31 @@
             ],
             flops,
         )
+        first_arrived = cross(first_send)
+        inside, across = hidden_rows(after(hidden_even, first_send), hidden_odd, second_arrived)
         steps = range(3)
         second_taps = [26 - (a * 9 + b * 3 + e) for b in steps for a in steps for e in steps]
         first_taps = [a * 9 + b * 3 + e for e in steps for b in steps for a in steps]
-        second_sum = reduced(where, *second_part, second_taps, factor, shape)
-        first_sum = reduced(where, *first_part, first_taps, factor, shape)
+        *second_parts, second_keep = packed_parts(
+            where, after(second_keep, inside), second_arrived
+        )
+        second_parts = exchanged(second_parts)
+        *first_parts, first_keep = packed_parts(
+            where, after(first_keep, second_keep), first_arrived
+        )
+        first_parts = exchanged(first_parts)
+        second_sum = finished(
+            after(second_keep, first_keep), second_parts, second_taps, factor, shape
+        )
+        first_sum = finished(first_keep, first_parts, first_taps, factor, shape)
+        second_out = convolved(after(inside, first_keep), across)
     else:
+        second_out = convolved(*hidden_rows(hidden_even, hidden_odd))
         (second_total,) = call(
             second_total_kernel,
             "second_filter_grad",
             [struct((9, outs, 3 * ins), F32)],
-            (where, *grad_slabs, *edges, hidden),
+            (where, *grad_slabs, grad_edges, hidden),
             [field],
             flops,
         )
@@ -469,7 +517,7 @@
             first_total_kernel,
             "first_filter_grad",
             [struct((3, outs, 9 * ins), F32)],
-            (where, *slabs, *edges, *grads),
+            (where, *slabs, edges, *grads),
             [field],
             flops,
         )
@@ -478,18 +526,6 @@
         first_total = first_total.reshape(3, outs, 3, 3, ins).transpose(1, 3, 2, 0, 4)
         second_sum = scattered(second_total, factor)
         first_sum = scattered(first_total.reshape(outs, taps, ins), factor)
-
-    (packed,) = call(
-        edge_kernel, "hidden_edges", [struct((3, chans, width), BF16)], (where, *hidden_slabs[:3])
-    )
-    (second_out,) = call(
-        second_kernel,
-        "second_conv",
-        [struct(volume.shape, BF16)],
-        (where, *hidden_slabs, swap_rows(packed, 1), second_weights),
-        [field, slab],
-        flops,
-    )
     return (second_out, first_sum, second_sum)
 
 

time: 78.6 us -> 65.7 us (0.84)
  waiting for transfers between devices: 19 us -> 9.28 us
  starting transfers between devices: 38.6 us -> 34.8 us
    ppermute x6, waiting for transfers between devices: 7.97 us -> 2.05 us  [swap_planes(): return lax.ppermute(values, 'cin', links(lax.axis_size('cin'), odd))]
    ppermute x10 -> x8, waiting for transfers between devices: 10.9 us -> 6.42 us  [the longest x2 4.96 us: cross(): lax.ppermute(values, 'cout', [(i, i ^ 2) for i in range(lax.axis_size('co...]
    ppermute x15 -> x14, starting transfers between devices: 14 us -> 10.2 us  [swap_rows(): return lax.ppermute(values, 'cout', links(lax.axis_size('cout'), odd))]
    ppermute x10 -> x8, starting transfers between devices: 14.8 us -> 13.4 us  [the longest x6 11.3 us: exchanged(): lax.ppermute(value, 'cin', [(i, i ^ k + 1) for i in range(parts)])]
    ppermute x6, starting transfers between devices: 9.85 us -> 11.2 us  [swap_planes(): return lax.ppermute(values, 'cin', links(lax.axis_size('cin'), odd))]
    pallas_call x13 -> x15, Pallas kernels: 16.6 us -> 17.2 us  [call(): pl.pallas_call(kernel, name=name, in_specs=[SMEM] * scalars + [VMEM] * (l...]
  transfers between devices with their start and end apart: 31 -> 28, of which waited for: 6 -> 5; matrix products, arithmetic and copies ran while one was open for 0% -> 0% of each run, Pallas kernels for 19% -> 25%
where the time goes in v3:
time: 65.7 us; the launch traced here: 65.4 us
  starting transfers between devices  34.8 us (53%)
  Pallas kernels  17.2 us (26%)
  waiting for transfers between devices  9.28 us (14%)
  local copies, waits for them, and re-layouts  3.13 us (5%)
  between operations  0.89 us (1%)
    pallas_call x15, Pallas kernels, call(): pl.pallas_call(kernel, name=name, in_specs=[SMEM] * scalars + [VMEM] * (l...  17.2 us
    ppermute x6, starting transfers between devices, exchanged(): lax.ppermute(value, 'cin', [(i, i ^ k + 1) for i in range(parts)])  11.3 us
    ppermute x6, starting transfers between devices, swap_planes(): return lax.ppermute(values, 'cin', links(lax.axis_size('cin'), odd))  11.2 us
    ppermute x14, starting transfers between devices, swap_rows(): return lax.ppermute(values, 'cout', links(lax.axis_size('cout'), odd))  10.2 us
    ppermute x2, waiting for transfers between devices, cross(): lax.ppermute(values, 'cout', [(i, i ^ 2) for i in range(lax.axis_size('co...  4.96 us
    unnamed x8, local copies, waits for them, and re-layouts  3.13 us
    ppermute x2, starting transfers between devices, cross(): lax.ppermute(values, 'cout', [(i, i ^ 2) for i in range(lax.axis_size('co...  2.15 us
    ppermute x6, waiting for transfers between devices, swap_planes(): return lax.ppermute(values, 'cin', links(lax.axis_size('cin'), odd))  2.05 us
  transfers between devices with their start and end apart: 28, of which 5 were waited for; matrix products, arithmetic and copies ran while one was open for 0% of the time, Pallas kernels for 25%

profile of v3, /device:TPU:0, one launch (start us, length us, event | category | flops | bytes accessed | tf_op | source)
XLA Modules:
  0.0 65.4 jit_solution(17204737943517466181)
XLA Ops:
  0.6 1.0 %copy-done.2 = bf16[128,1,4,256]{3,2,1,0:T(4,128)(2,1)S(1)} copy-done((bf16[128,1,4,256]{3,2,1,0:T(4,128)(2,1)S(1)}, bf16[128,1,4,256]{3,2,1,0:T(4,128)(2,1)}, u32[]{:S(2)}) %copy-start.2) | copy-done | bytes 262168
  1.7 3.1 %collective-permute-start = (bf16[4,128,256]{2,1,0:T(8,128)(2,1)S(1)}, bf16[4,128,256]{2,1,0:T(8,128)(2,1)S(1)}, u32[]{:S(2)}, u32[]{:S(2)}) collective-permute-start(bf16[4,128,256]{2,1,0:T(8,128)(2,1)S(1)} %prepare_volume.1.own.refs_0_), channel_id=1, source_target_pairs={{0,4},{4,0},{8,12},{12,8},{1,5},{5,1},{9,13},{13,9},{2,6},{6,2},{1... | collective-permute-start | bytes 786440 | tf_op jit(solution)/shard_map/ppermute | solution.py:26
  5.5 0.9 %copy-done.3 = bf16[128,1,4,256]{3,2,1,0:T(4,128)(2,1)S(1)} copy-done((bf16[128,1,4,256]{3,2,1,0:T(4,128)(2,1)S(1)}, bf16[128,1,4,256]{3,2,1,0:T(4,128)(2,1)}, u32[]{:S(2)}) %copy-start.3) | copy-done | bytes 262168
  6.5 4.4 %collective-permute-start.9 = (bf16[4,128,256]{2,1,0:T(8,128)(2,1)S(1)}, bf16[4,128,256]{2,1,0:T(8,128)(2,1)S(1)}, u32[]{:S(2)}, u32[]{:S(2)}) collective-permute-start(bf16[4,128,256]{2,1,0:T(8,128)(2,1)S(1)} %prepare_cotangent.1.own.refs_0_), channel_id=1, source_target_pairs={{0,4},{4,0},{8,12},{12,8},{1,5},{5,1},{9,13},{13,9},{2,6},{6,2},{1... | collective-permute-start | bytes 786440 | tf_op jit(solution)/shard_map/ppermute | solution.py:26
  11.7 1.2 %copy-done.1 = bf16[128,27,128]{2,0,1:T(8,128)(2,1)S(1)} copy-done((bf16[128,27,128]{2,0,1:T(8,128)(2,1)S(1)}, bf16[128,27,128]{2,0,1:T(8,128)(2,1)}, u32[]{:S(2)}) %copy-start.1) | copy-done | bytes 884760
  14.7 2.0 %collective-permute-done.9.even.refs_1_ = bf16[4,128,256]{2,1,0:T(8,128)(2,1)S(1)} collective-permute-done((bf16[4,128,256]{2,1,0:T(8,128)(2,1)S(1)}, bf16[4,128,256]{2,1,0:T(8,128)(2,1)S(1)}, u32[]{:S(2)}, u32[]{:S(2)}) %collective-permute-start.9) | collective-permute-done | bytes 262176 | tf_op jit(solution)/shard_map/ppermute | solution.py:26
  18.7 4.3 %collective-permute-start.11 = (bf16[4,128,256]{2,1,0:T(8,128)(2,1)S(1)}, bf16[4,128,256]{2,1,0:T(8,128)(2,1)S(1)}, u32[]{:S(2)}, u32[]{:S(2)}) collective-permute-start(bf16[4,128,256]{2,1,0:T(8,128)(2,1)S(1)} %prepare_cotangent.1.own.refs_0_), channel_id=1, source_target_pairs={{0,1},{1,0},{2,3},{3,2},{4,5},{5,4},{6,7},{7,6},{8,9},{9,8},{10,11... | collective-permute-start | bytes 786440 | tf_op jit(solution)/shard_map/ppermute | solution.py:30
  23.8 2.0 %first_conv.1 = (bf16[4,128,256]{2,1,0:T(8,128)(2,1)S(1)}, f32[4,128,256]{2,1,0:T(8,128)S(1)}) custom-call(s32[4]{0:T(128)S(1)} %pad_add_fusion.where, bf16[4,128,256]{2,1,0:T(8,128)(2,1)S(1)} %prepare_volume.1.own.refs_0_, bf16[4,128,256]{2,1,0:T(8,128)(2,1)S(1)} %collective-permute-done.even.refs_1_, ...), custom_call_target="tpu_custom_call" | custom-call | flops 905969664 | bytes 3440656 | tf_op jit(solution)/shard_map/first_conv/pallas_call | solution.py:301
  26.3 1.7 %collective-permute-start.15 = (bf16[3,128,256]{2,1,0:T(8,128)(2,1)S(1)}, bf16[3,128,256]{2,1,0:T(8,128)(2,1)S(1)}, u32[]{:S(2)}, u32[]{:S(2)}) collective-permute-start(bf16[3,128,256]{2,1,0:T(8,128)(2,1)S(1)} %collective-permute-done.14.refs_6_), channel_id=1, source_target_pairs={{0,1},{1,0},{2,3},{3,2},{4,5},{5,4},{6,7},{7,6},{8,9},{9,8},{10,11... | collective-permute-start | bytes 589832 | tf_op jit(solution)/shard_map/ppermute | solution.py:30
  28.0 1.6 %collective-permute-start.6 = (bf16[4,128,256]{2,1,0:T(8,128)(2,1)S(1)}, bf16[4,128,256]{2,1,0:T(8,128)(2,1)S(1)}, u32[]{:S(2)}, u32[]{:S(2)}) collective-permute-start(bf16[4,128,256]{2,1,0:T(8,128)(2,1)S(1)} %get-tuple-element.35.refs_8_.own.refs_0_), channel_id=1, source_target_pairs={{0,4},{4,0},{8,12},{12,8},{1,5},{5,1},{9,13},{13,9},{2,6},{6,2},{1... | collective-permute-start | bytes 786440 | tf_op jit(solution)/shard_map/ppermute | solution.py:26
  30.3 1.9 %hidden_grad.1 = (bf16[4,64,256]{2,1,0:T(8,128)(2,1)S(1)}, bf16[4,64,256]{2,1,0:T(8,128)(2,1)S(1)}) custom-call(s32[4]{0:T(128)S(1)} %pad_add_fusion.where, bf16[4,128,256]{2,1,0:T(8,128)(2,1)S(1)} %prepare_cotangent.1.own.refs_0_, bf16[4,128,256]{2,1,0:T(8,128)(2,1)S(1)} %collective-permute-done.9.even.refs_1_, ...), custom_call_target="tpu_custom_call" | custom-call | flops 905969664 | bytes 3440656 | tf_op jit(solution)/shard_map/hidden_grad/pallas_call | solution.py:301
  32.5 2.1 %second_filter_grad.1 = (bf16[9,32,384]{2,1,0:T(8,128)(2,1)S(1)}, f32[9,32,384]{2,1,0:T(8,128)S(1)}) custom-call(s32[4]{0:T(128)S(1)} %pad_add_fusion.where, bf16[4,128,256]{2,1,0:T(8,128)(2,1)S(1)} %prepare_cotangent.1.own.refs_0_, bf16[4,128,256]{2,1,0:T(8,128)(2,1)S(1)} %collective-permute-done.9.even.refs_1_, ...), custom_call_target="tpu_custom_call" | custom-call | flops 905969664 | bytes 3153936 | tf_op jit(solution)/shard_map/second_filter_grad/pallas_call | solution.py:301
  34.6 1.5 %collective-permute-start.18 = (bf16[9,32,384]{2,1,0:T(8,128)(2,1)S(1)}, bf16[9,32,384]{2,1,0:T(8,128)(2,1)S(1)}, u32[]{:S(2)}, u32[]{:S(2)}) collective-permute-start(bf16[9,32,384]{2,1,0:T(8,128)(2,1)S(1)} %get-tuple-element.39), channel_id=1, source_target_pairs={{0,2},{1,3},{2,0},{3,1},{4,6},{5,7},{6,4},{7,5},{8,10},{9,11},{10,... | collective-permute-start | bytes 663560 | tf_op jit(solution)/shard_map/ppermute | solution.py:352
  36.2 2.3 %first_filter_grad.1 = (bf16[3,32,1152]{2,1,0:T(8,128)(2,1)S(1)}, f32[3,32,1152]{2,1,0:T(8,128)S(1)}) custom-call(s32[4]{0:T(128)S(1)} %pad_add_fusion.where, bf16[4,128,256]{2,1,0:T(8,128)(2,1)S(1)} %prepare_volume.1.own.refs_0_, bf16[4,128,256]{2,1,0:T(8,128)(2,1)S(1)} %collective-permute-done.even.refs_1_, ...), custom_call_target="tpu_custom_call" | custom-call | flops 905969664 | bytes 2891792 | tf_op jit(solution)/shard_map/first_filter_grad/pallas_call | solution.py:301
  39.7 3.2 %collective-permute-done.18.arrived = bf16[9,32,384]{2,1,0:T(8,128)(2,1)S(1)} collective-permute-done((bf16[9,32,384]{2,1,0:T(8,128)(2,1)S(1)}, bf16[9,32,384]{2,1,0:T(8,128)(2,1)S(1)}, u32[]{:S(2)}, u32[]{:S(2)}) %collective-permute-start.18) | collective-permute-done | bytes 221216 | tf_op jit(solution)/shard_map/ppermute | solution.py:352
  44.4 1.0 %pack_parts.2 = (bf16[7,32,128]{2,1,0:T(8,128)(2,1)S(1)}, bf16[7,32,128]{2,1,0:T(8,128)(2,1)S(1)}, bf16[7,32,128]{2,1,0:T(8,128)(2,1)S(1)}, f32[7,32,128]{2,1,0:T(8,128)S(1)}) custom-call(s32[4]{0:T(128)S(1)} %pad_add_fusion.where, f32[9,32,384]{2,1,0:T(8,128)S(1)} %get-tuple-element.49.held, bf16[9,32,384]{2,1,0:T(8,128)(2,1)S(1)} %collective-permute-done.18.arrived), custom_call_target="tpu_custom_call" | custom-call | bytes 950288 | tf_op jit(solution)/shard_map/pack_parts/pallas_call | solution.py:301
  45.4 1.8 %collective-permute-done.20.arrived = bf16[3,32,1152]{2,1,0:T(8,128)(2,1)S(1)} collective-permute-done((bf16[3,32,1152]{2,1,0:T(8,128)(2,1)S(1)}, bf16[3,32,1152]{2,1,0:T(8,128)(2,1)S(1)}, u32[]{:S(2)}, u32[]{:S(2)}) %collective-permute-start.20) | collective-permute-done | bytes 221216 | tf_op jit(solution)/shard_map/ppermute | solution.py:352
  47.1 1.0 %pack_parts.3 = (bf16[7,32,128]{2,1,0:T(8,128)(2,1)S(1)}, bf16[7,32,128]{2,1,0:T(8,128)(2,1)S(1)}, bf16[7,32,128]{2,1,0:T(8,128)(2,1)S(1)}, f32[7,32,128]{2,1,0:T(8,128)S(1)}) custom-call(s32[4]{0:T(128)S(1)} %pad_add_fusion.where, f32[3,32,1152]{2,1,0:T(8,128)S(1)} %get-tuple-element.51.held, bf16[3,32,1152]{2,1,0:T(8,128)(2,1)S(1)} %collective-permute-done.20.arrived), custom_call_target="tpu_custom_call" | custom-call | bytes 950288 | tf_op jit(solution)/shard_map/pack_parts/pallas_call | solution.py:301
  48.1 4.4 %collective-permute-start.22 = (bf16[7,32,128]{2,1,0:T(8,128)(2,1)S(1)}, bf16[7,32,128]{2,1,0:T(8,128)(2,1)S(1)}, u32[]{:S(2)}, u32[]{:S(2)}) collective-permute-start(bf16[7,32,128]{2,1,0:T(8,128)(2,1)S(1)} %get-tuple-element.56), channel_id=1, source_target_pairs={{0,4},{4,0},{8,12},{12,8},{1,5},{5,1},{9,13},{13,9},{2,6},{6,2},{1... | collective-permute-start | bytes 172040 | tf_op jit(solution)/shard_map/ppermute | solution.py:335
  52.6 2.4 %collective-permute-start.24 = (bf16[7,32,128]{2,1,0:T(8,128)(2,1)S(1)}, bf16[7,32,128]{2,1,0:T(8,128)(2,1)S(1)}, u32[]{:S(2)}, u32[]{:S(2)}) collective-permute-start(bf16[7,32,128]{2,1,0:T(8,128)(2,1)S(1)} %get-tuple-element.58), channel_id=1, source_target_pairs={{0,12},{4,8},{8,4},{12,0},{1,13},{5,9},{9,5},{13,1},{2,14},{6,10},... | collective-permute-start | bytes 172040 | tf_op jit(solution)/shard_map/ppermute | solution.py:335
  55.0 1.0 %collective-permute-start.25 = (bf16[7,32,128]{2,1,0:T(8,128)(2,1)S(1)}, bf16[7,32,128]{2,1,0:T(8,128)(2,1)S(1)}, u32[]{:S(2)}, u32[]{:S(2)}) collective-permute-start(bf16[7,32,128]{2,1,0:T(8,128)(2,1)S(1)} %get-tuple-element.60), channel_id=1, source_target_pairs={{0,4},{4,0},{8,12},{12,8},{1,5},{5,1},{9,13},{13,9},{2,6},{6,2},{1... | collective-permute-start | bytes 172040 | tf_op jit(solution)/shard_map/ppermute | solution.py:335
  57.0 2.4 %collective-permute-start.27 = (bf16[7,32,128]{2,1,0:T(8,128)(2,1)S(1)}, bf16[7,32,128]{2,1,0:T(8,128)(2,1)S(1)}, u32[]{:S(2)}, u32[]{:S(2)}) collective-permute-start(bf16[7,32,128]{2,1,0:T(8,128)(2,1)S(1)} %get-tuple-element.62), channel_id=1, source_target_pairs={{0,12},{4,8},{8,4},{12,0},{1,13},{5,9},{9,5},{13,1},{2,14},{6,10},... | collective-permute-start | bytes 172040 | tf_op jit(solution)/shard_map/ppermute | solution.py:335
  59.4 2.7 %second_conv.1 = bf16[128,1,4,256]{3,2,1,0:T(4,128)(2,1)} custom-call(s32[4]{0:T(128)S(1)} %pad_add_fusion.where, bf16[4,128,256]{2,1,0:T(8,128)(2,1)S(1)} %get-tuple-element.35.refs_8_.own.refs_0_, bf16[4,128,256]{2,1,0:T(8,128)(2,1)S(1)} %collective-permute-done.6.even.refs_1_, bf16[4,128,256]{2,1,0:T(8,128)(2,1)S(1)} %collective-permute-done.7.odd.refs_2_, ...), custom_call_target="tpu_custom_call" | custom-call | flops 905969664 | bytes 2326544 | tf_op jit(solution)/shard_map/second_conv/pallas_call | solution.py:301
  63.0 1.4 %collective-permute-done.26.refs_1_ = bf16[7,32,128]{2,1,0:T(8,128)(2,1)S(1)} collective-permute-done((bf16[7,32,128]{2,1,0:T(8,128)(2,1)S(1)}, bf16[7,32,128]{2,1,0:T(8,128)(2,1)S(1)}, u32[]{:S(2)}, u32[]{:S(2)}) %collective-permute-start.26) | collective-permute-done | bytes 57376 | tf_op jit(solution)/shard_map/ppermute | solution.py:335
  (56 shorter events, 12.9 us)
Async XLA Ops:
  1.7 11.7 %collective-permute-start = (bf16[4,128,256]{2,1,0:T(8,128)(2,1)S(1)}, bf16[4,128,256]{2,1,0:T(8,128)(2,1)S(1)}, u32[]{:S(2)}, u32[]{:S(2)}) collective-permute-start(bf16[4,128,256]{2,1,0:T(8,128)(2,1)S(1)} %prepare_volume.1.own.refs_0_), channel_id=1, source_target_pairs={{0,4},{4,0},{8,12},{12,8},{1,5},{5,1},{9,13},{13,9},{2,6},{6,2},{1... | collective-permute-start | bytes 786440 | tf_op jit(solution)/shard_map/ppermute | solution.py:26
  4.8 9.2 %collective-permute-start.1 = (bf16[4,128,256]{2,1,0:T(8,128)(2,1)S(1)}, bf16[4,128,256]{2,1,0:T(8,128)(2,1)S(1)}, u32[]{:S(2)}, u32[]{:S(2)}) collective-permute-start(bf16[4,128,256]{2,1,0:T(8,128)(2,1)S(1)} %prepare_volume.1.own.refs_0_), channel_id=1, source_target_pairs={{4,8},{8,4},{5,9},{9,5},{6,10},{10,6},{7,11},{11,7},{20,24},{24,20... | collective-permute-start | bytes 786440 | tf_op jit(solution)/shard_map/ppermute | solution.py:26
  6.5 10.2 %collective-permute-start.9 = (bf16[4,128,256]{2,1,0:T(8,128)(2,1)S(1)}, bf16[4,128,256]{2,1,0:T(8,128)(2,1)S(1)}, u32[]{:S(2)}, u32[]{:S(2)}) collective-permute-start(bf16[4,128,256]{2,1,0:T(8,128)(2,1)S(1)} %prepare_cotangent.1.own.refs_0_), channel_id=1, source_target_pairs={{0,4},{4,0},{8,12},{12,8},{1,5},{5,1},{9,13},{13,9},{2,6},{6,2},{1... | collective-permute-start | bytes 786440 | tf_op jit(solution)/shard_map/ppermute | solution.py:26
  11.0 7.7 %collective-permute-start.2 = (bf16[4,128,256]{2,1,0:T(8,128)(2,1)S(1)}, bf16[4,128,256]{2,1,0:T(8,128)(2,1)S(1)}, u32[]{:S(2)}, u32[]{:S(2)}) collective-permute-start(bf16[4,128,256]{2,1,0:T(8,128)(2,1)S(1)} %prepare_volume.1.own.refs_0_), channel_id=1, source_target_pairs={{0,1},{1,0},{2,3},{3,2},{4,5},{5,4},{6,7},{7,6},{8,9},{9,8},{10,11... | collective-permute-start | bytes 786440 | tf_op jit(solution)/shard_map/ppermute | solution.py:30
  11.0 6.4 %collective-permute-start.10 = (bf16[4,128,256]{2,1,0:T(8,128)(2,1)S(1)}, bf16[4,128,256]{2,1,0:T(8,128)(2,1)S(1)}, u32[]{:S(2)}, u32[]{:S(2)}) collective-permute-start(bf16[4,128,256]{2,1,0:T(8,128)(2,1)S(1)} %prepare_cotangent.1.own.refs_0_), channel_id=1, source_target_pairs={{4,8},{8,4},{5,9},{9,5},{6,10},{10,6},{7,11},{11,7},{20,24},{24,20... | collective-permute-start | bytes 786440 | tf_op jit(solution)/shard_map/ppermute | solution.py:26
  13.4 10.4 %collective-permute-start.3 = (bf16[4,128,256]{2,1,0:T(8,128)(2,1)S(1)}, bf16[4,128,256]{2,1,0:T(8,128)(2,1)S(1)}, u32[]{:S(2)}, u32[]{:S(2)}) collective-permute-start(bf16[4,128,256]{2,1,0:T(8,128)(2,1)S(1)} %collective-permute-done.even.refs_1_), channel_id=1, source_target_pairs={{0,1},{1,0},{2,3},{3,2},{4,5},{5,4},{6,7},{7,6},{8,9},{9,8},{10,11... | collective-permute-start | bytes 786440 | tf_op jit(solution)/shard_map/ppermute | solution.py:30
  14.0 9.8 %collective-permute-start.4 = (bf16[4,128,256]{2,1,0:T(8,128)(2,1)S(1)}, bf16[4,128,256]{2,1,0:T(8,128)(2,1)S(1)}, u32[]{:S(2)}, u32[]{:S(2)}) collective-permute-start(bf16[4,128,256]{2,1,0:T(8,128)(2,1)S(1)} %collective-permute-done.1.odd.refs_2_), channel_id=1, source_target_pairs={{0,1},{1,0},{2,3},{3,2},{4,5},{5,4},{6,7},{7,6},{8,9},{9,8},{10,11... | collective-permute-start | bytes 786440 | tf_op jit(solution)/shard_map/ppermute | solution.py:30
  16.8 6.3 %collective-permute-start.5 = (bf16[3,128,256]{2,1,0:T(8,128)(2,1)S(1)}, bf16[3,128,256]{2,1,0:T(8,128)(2,1)S(1)}, u32[]{:S(2)}, u32[]{:S(2)}) collective-permute-start(bf16[3,128,256]{2,1,0:T(8,128)(2,1)S(1)} %edges.2), channel_id=1, source_target_pairs={{1,2},{2,1},{5,6},{6,5},{9,10},{10,9},{13,14},{14,13},{17,18},{18,... | collective-permute-start | bytes 589832 | tf_op jit(solution)/shard_map/ppermute | solution.py:30
  18.0 8.3 %collective-permute-start.14 = (bf16[3,128,256]{2,1,0:T(8,128)(2,1)S(1)}, bf16[3,128,256]{2,1,0:T(8,128)(2,1)S(1)}, u32[]{:S(2)}, u32[]{:S(2)}) collective-permute-start(bf16[3,128,256]{2,1,0:T(8,128)(2,1)S(1)} %edges.3), channel_id=1, source_target_pairs={{1,2},{2,1},{5,6},{6,5},{9,10},{10,9},{13,14},{14,13},{17,18},{18,... | collective-permute-start | bytes 589832 | tf_op jit(solution)/shard_map/ppermute | solution.py:30
  18.7 9.3 %collective-permute-start.11 = (bf16[4,128,256]{2,1,0:T(8,128)(2,1)S(1)}, bf16[4,128,256]{2,1,0:T(8,128)(2,1)S(1)}, u32[]{:S(2)}, u32[]{:S(2)}) collective-permute-start(bf16[4,128,256]{2,1,0:T(8,128)(2,1)S(1)} %prepare_cotangent.1.own.refs_0_), channel_id=1, source_target_pairs={{0,1},{1,0},{2,3},{3,2},{4,5},{5,4},{6,7},{7,6},{8,9},{9,8},{10,11... | collective-permute-start | bytes 786440 | tf_op jit(solution)/shard_map/ppermute | solution.py:30
  25.8 6.8 %collective-permute-start.16 = (bf16[4,128,256]{2,1,0:T(8,128)(2,1)S(1)}, bf16[4,128,256]{2,1,0:T(8,128)(2,1)S(1)}, u32[]{:S(2)}, u32[]{:S(2)}) collective-permute-start(bf16[4,128,256]{2,1,0:T(8,128)(2,1)S(1)} %get-tuple-element.35.refs_8_.own.refs_0_), channel_id=1, source_target_pairs={{0,1},{1,0},{2,3},{3,2},{4,5},{5,4},{6,7},{7,6},{8,9},{9,8},{10,11... | collective-permute-start | bytes 786440 | tf_op jit(solution)/shard_map/ppermute | solution.py:30
  26.3 6.0 %collective-permute-start.15 = (bf16[3,128,256]{2,1,0:T(8,128)(2,1)S(1)}, bf16[3,128,256]{2,1,0:T(8,128)(2,1)S(1)}, u32[]{:S(2)}, u32[]{:S(2)}) collective-permute-start(bf16[3,128,256]{2,1,0:T(8,128)(2,1)S(1)} %collective-permute-done.14.refs_6_), channel_id=1, source_target_pairs={{0,1},{1,0},{2,3},{3,2},{4,5},{5,4},{6,7},{7,6},{8,9},{9,8},{10,11... | collective-permute-start | bytes 589832 | tf_op jit(solution)/shard_map/ppermute | solution.py:30
  28.0 8.2 %collective-permute-start.8 = (bf16[3,128,256]{2,1,0:T(8,128)(2,1)S(1)}, bf16[3,128,256]{2,1,0:T(8,128)(2,1)S(1)}, u32[]{:S(2)}, u32[]{:S(2)}) collective-permute-start(bf16[3,128,256]{2,1,0:T(8,128)(2,1)S(1)} %collective-permute-done.5.refs_6_), channel_id=1, source_target_pairs={{0,1},{1,0},{2,3},{3,2},{4,5},{5,4},{6,7},{7,6},{8,9},{9,8},{10,11... | collective-permute-start | bytes 589832 | tf_op jit(solution)/shard_map/ppermute | solution.py:30
  28.0 11.2 %collective-permute-start.6 = (bf16[4,128,256]{2,1,0:T(8,128)(2,1)S(1)}, bf16[4,128,256]{2,1,0:T(8,128)(2,1)S(1)}, u32[]{:S(2)}, u32[]{:S(2)}) collective-permute-start(bf16[4,128,256]{2,1,0:T(8,128)(2,1)S(1)} %get-tuple-element.35.refs_8_.own.refs_0_), channel_id=1, source_target_pairs={{0,4},{4,0},{8,12},{12,8},{1,5},{5,1},{9,13},{13,9},{2,6},{6,2},{1... | collective-permute-start | bytes 786440 | tf_op jit(solution)/shard_map/ppermute | solution.py:26
  29.7 9.5 %collective-permute-start.7 = (bf16[4,128,256]{2,1,0:T(8,128)(2,1)S(1)}, bf16[4,128,256]{2,1,0:T(8,128)(2,1)S(1)}, u32[]{:S(2)}, u32[]{:S(2)}) collective-permute-start(bf16[4,128,256]{2,1,0:T(8,128)(2,1)S(1)} %get-tuple-element.35.refs_8_.own.refs_0_), channel_id=1, source_target_pairs={{4,8},{8,4},{5,9},{9,5},{6,10},{10,6},{7,11},{11,7},{20,24},{24,20... | collective-permute-start | bytes 786440 | tf_op jit(solution)/shard_map/ppermute | solution.py:26
  34.6 8.3 %collective-permute-start.18 = (bf16[9,32,384]{2,1,0:T(8,128)(2,1)S(1)}, bf16[9,32,384]{2,1,0:T(8,128)(2,1)S(1)}, u32[]{:S(2)}, u32[]{:S(2)}) collective-permute-start(bf16[9,32,384]{2,1,0:T(8,128)(2,1)S(1)} %get-tuple-element.39), channel_id=1, source_target_pairs={{0,2},{1,3},{2,0},{3,1},{4,6},{5,7},{6,4},{7,5},{8,10},{9,11},{10,... | collective-permute-start | bytes 663560 | tf_op jit(solution)/shard_map/ppermute | solution.py:352
  38.5 8.6 %collective-permute-start.20 = (bf16[3,32,1152]{2,1,0:T(8,128)(2,1)S(1)}, bf16[3,32,1152]{2,1,0:T(8,128)(2,1)S(1)}, u32[]{:S(2)}, u32[]{:S(2)}) collective-permute-start(bf16[3,32,1152]{2,1,0:T(8,128)(2,1)S(1)} %get-tuple-element.42), channel_id=1, source_target_pairs={{0,2},{1,3},{2,0},{3,1},{4,6},{5,7},{6,4},{7,5},{8,10},{9,11},{10,... | collective-permute-start | bytes 663560 | tf_op jit(solution)/shard_map/ppermute | solution.py:352
  43.0 13.1 %collective-permute-start.21 = (bf16[3,128,256]{2,1,0:T(8,128)(2,1)S(1)}, bf16[3,128,256]{2,1,0:T(8,128)(2,1)S(1)}, u32[]{:S(2)}, u32[]{:S(2)}) collective-permute-start(bf16[3,128,256]{2,1,0:T(8,128)(2,1)S(1)} %get-tuple-element.54), channel_id=1, source_target_pairs={{1,2},{2,1},{5,6},{6,5},{9,10},{10,9},{13,14},{14,13},{17,18},{18,... | collective-permute-start | bytes 589832 | tf_op jit(solution)/shard_map/ppermute | solution.py:30
  48.1 8.8 %collective-permute-start.22 = (bf16[7,32,128]{2,1,0:T(8,128)(2,1)S(1)}, bf16[7,32,128]{2,1,0:T(8,128)(2,1)S(1)}, u32[]{:S(2)}, u32[]{:S(2)}) collective-permute-start(bf16[7,32,128]{2,1,0:T(8,128)(2,1)S(1)} %get-tuple-element.56), channel_id=1, source_target_pairs={{0,4},{4,0},{8,12},{12,8},{1,5},{5,1},{9,13},{13,9},{2,6},{6,2},{1... | collective-permute-start | bytes 172040 | tf_op jit(solution)/shard_map/ppermute | solution.py:335
  52.6 9.5 %collective-permute-start.23 = (bf16[7,32,128]{2,1,0:T(8,128)(2,1)S(1)}, bf16[7,32,128]{2,1,0:T(8,128)(2,1)S(1)}, u32[]{:S(2)}, u32[]{:S(2)}) collective-permute-start(bf16[7,32,128]{2,1,0:T(8,128)(2,1)S(1)} %get-tuple-element.57), channel_id=1, source_target_pairs={{0,8},{4,12},{8,0},{12,4},{1,9},{5,13},{9,1},{13,5},{2,10},{6,14},... | collective-permute-start | bytes 172040 | tf_op jit(solution)/shard_map/ppermute | solution.py:335
  52.6 9.5 %collective-permute-start.24 = (bf16[7,32,128]{2,1,0:T(8,128)(2,1)S(1)}, bf16[7,32,128]{2,1,0:T(8,128)(2,1)S(1)}, u32[]{:S(2)}, u32[]{:S(2)}) collective-permute-start(bf16[7,32,128]{2,1,0:T(8,128)(2,1)S(1)} %get-tuple-element.58), channel_id=1, source_target_pairs={{0,12},{4,8},{8,4},{12,0},{1,13},{5,9},{9,5},{13,1},{2,14},{6,10},... | collective-permute-start | bytes 172040 | tf_op jit(solution)/shard_map/ppermute | solution.py:335
  55.0 8.0 %collective-permute-start.25 = (bf16[7,32,128]{2,1,0:T(8,128)(2,1)S(1)}, bf16[7,32,128]{2,1,0:T(8,128)(2,1)S(1)}, u32[]{:S(2)}, u32[]{:S(2)}) collective-permute-start(bf16[7,32,128]{2,1,0:T(8,128)(2,1)S(1)} %get-tuple-element.60), channel_id=1, source_target_pairs={{0,4},{4,0},{8,12},{12,8},{1,5},{5,1},{9,13},{13,9},{2,6},{6,2},{1... | collective-permute-start | bytes 172040 | tf_op jit(solution)/shard_map/ppermute | solution.py:335
  56.1 8.4 %collective-permute-start.26 = (bf16[7,32,128]{2,1,0:T(8,128)(2,1)S(1)}, bf16[7,32,128]{2,1,0:T(8,128)(2,1)S(1)}, u32[]{:S(2)}, u32[]{:S(2)}) collective-permute-start(bf16[7,32,128]{2,1,0:T(8,128)(2,1)S(1)} %get-tuple-element.61), channel_id=1, source_target_pairs={{0,8},{4,12},{8,0},{12,4},{1,9},{5,13},{9,1},{13,5},{2,10},{6,14},... | collective-permute-start | bytes 172040 | tf_op jit(solution)/shard_map/ppermute | solution.py:335
  57.0 7.5 %collective-permute-start.27 = (bf16[7,32,128]{2,1,0:T(8,128)(2,1)S(1)}, bf16[7,32,128]{2,1,0:T(8,128)(2,1)S(1)}, u32[]{:S(2)}, u32[]{:S(2)}) collective-permute-start(bf16[7,32,128]{2,1,0:T(8,128)(2,1)S(1)} %get-tuple-element.62), channel_id=1, source_target_pairs={{0,12},{4,8},{8,4},{12,0},{1,13},{5,9},{9,5},{13,1},{2,14},{6,10},... | collective-permute-start | bytes 172040 | tf_op jit(solution)/shard_map/ppermute | solution.py:335
  (8 other events, 30.4 us)

commit v4 on v3

--- a/solution.py
+++ b/solution.py
@@ -61,15 +61,14 @@
     return (1, 2 * (1 - where[0]), 2 * where[0])
 
 
-def fill(where, slabs, edges, field):
-    rows = slabs[0].shape[0]
+def fill(where, stack, inside, edges, field):
+    rows = field.shape[0] - 2
     row = where[1]
-    for k, plane in enumerate(planes_of(where)):
+    for plane in range(3):
         for r in range(rows):
-            field[1 + r, plane] = slabs[k][r]
-        inside = slabs[3 + k][row * (rows - 1)] if len(slabs) == 6 else slabs[3][k]
-        field[(1 - row) * (rows + 1), plane] = inside
-        field[row * (rows + 1), plane] = edges[k]
+            field[1 + r, plane] = stack[plane, r]
+        field[(1 - row) * (rows + 1), plane] = inside[plane]
+        field[row * (rows + 1), plane] = edges[plane]
 
 
 def halves(where, quarter):
@@ -77,8 +76,8 @@
     return [pl.ds(pl.multiple_of(2 * h * quarter + mine * quarter, quarter), quarter) for h in range(2)]
 
 
-def fill_pair(where, slabs, edges, pair_edges, field, split):
-    rows = slabs[0].shape[0]
+def fill_pair(where, stack, pair, edges, pair_edges, field, split):
+    rows = (field.shape[0] - 2) // 2
     row = where[1]
 
     def put(at, plane, value):
@@ -89,12 +88,12 @@
         for h, part in enumerate(halves(where, quarter)):
             field[at, plane, h * quarter : (h + 1) * quarter] = value[part]
 
-    for k, plane in enumerate(planes_of(where)):
+    for plane in range(3):
         for r in range(rows):
-            put(1 + row * rows + r, plane, slabs[k].at[r])
-            put(1 + (1 - row) * rows + r, plane, slabs[3 + k].at[r])
-        put(row * (2 * rows + 1), plane, edges.at[k])
-        put((1 - row) * (2 * rows + 1), plane, pair_edges.at[k])
+            put(1 + row * rows + r, plane, stack.at[plane, r])
+            put(1 + (1 - row) * rows + r, plane, pair(plane, r))
+        put(row * (2 * rows + 1), plane, edges.at[plane])
+        put((1 - row) * (2 * rows + 1), plane, pair_edges.at[plane])
 
 
 def window(field, row):
@@ -106,16 +105,20 @@
     return combine(jnp.dot(weights[...], window(field, row), preferred_element_type=F32))
 
 
-def prepare_kernel(values, out):
-    out[...] = jnp.transpose(values[:, 0], (1, 0, 2))
-
-
-def edge_kernel(where, own, even, odd, across, *inside):
+def gather_kernel(where, own, even, odd, *refs):
+    stack, across, inside = refs
+    for plane, slab in zip(planes_of(where), (own, even, odd)):
+        stack[plane] = jnp.transpose(slab[:, 0], (1, 0, 2))
+        across[plane] = stack[plane, where[1] * (stack.shape[1] - 1)]
+        inside[plane] = stack[plane, (1 - where[1]) * (stack.shape[1] - 1)]
+
+
+def gather_hidden_kernel(where, own, even, odd, stack, across, inside):
     last = own.shape[0] - 1
-    for k, slab in enumerate((own, even, odd)):
-        across[k] = slab[where[1] * last]
-        for out in inside:
-            out[k] = slab[(1 - where[1]) * last]
+    for plane, slab in zip(planes_of(where), (own, even, odd)):
+        stack[plane] = slab[...]
+        across[plane] = slab[where[1] * last]
+        inside[plane] = slab[(1 - where[1]) * last]
 
 
 def weights_kernel(first, second, first_out, second_out, back_out):
@@ -134,30 +137,32 @@
 
 
 def first_kernel(where, *refs):
-    slabs = refs[:6]
-    edges, weights, hidden, slope, field = refs[6:]
-    fill(where, slabs, edges, field)
+    stack, inside, edges, weights, hidden, slope, shared, field = refs
+    fill(where, stack, inside, edges, field)
+    rows = hidden.shape[0]
+    for plane in range(3):
+        shared[plane * rows : (plane + 1) * rows] = stack[plane]
+    shared[3 * rows : 3 * rows + 3] = edges[...]
     for row in range(hidden.shape[0]):
         value = conv_rows(weights, field, row)
         gate = 1.0 / (1.0 + jnp.exp(-value))
         hidden[row] = (value * gate).astype(BF16)
+        shared[3 * rows + 3 + row] = hidden[row]
         slope[row] = gate * (1.0 + value * (1.0 - gate))
 
 
 def second_kernel(where, *refs):
-    slabs = refs[:4]
-    packed, weights, out, field, held = refs[4:]
-    fill(where, slabs, packed, field)
+    stack, inside, edges, weights, out, field, held = refs
+    fill(where, stack, inside, edges, field)
     for row in range(held.shape[0]):
         held[row] = conv_rows(weights, field, row).astype(BF16)
     out[:, 0] = jnp.transpose(held[...], (1, 0, 2))
 
 
 def grad_kernel(where, *refs):
-    slabs = refs[:6]
-    edges, weights, slope, keep, *rest = refs[6:]
+    weights, slope, keep, *rest = refs[3:]
     *send, field, whole = rest
-    fill(where, slabs, edges, field)
+    fill(where, *refs[:3], field)
     for row in range(slope.shape[0]):
         grad = (conv_rows(weights, field, row) * slope[row]).astype(BF16)
         if not send:
@@ -189,10 +194,10 @@
 
 
 def second_grad_kernel(where, *refs):
-    slabs = refs[:6]
-    edges, pair_edges, hidden, pair_hidden, send, keep, field, both, total = refs[6:]
-    fill_pair(where, slabs, edges, pair_edges, field, True)
-    ordered(where, hidden, pair_hidden, both)
+    stack, pair, edges, pair_edges, hidden, pair_shared, send, keep, field, both, total = refs
+    rows = hidden.shape[0]
+    fill_pair(where, stack, lambda p, r: pair.at[p, r], edges, pair_edges, field, True)
+    ordered(where, hidden, pair_shared.at[pl.ds(3 * rows + 3, rows)], both)
     for row in range(both.shape[0]):
         part = lax.dot_general(
             window(field, row),
@@ -205,9 +210,12 @@
 
 
 def first_grad_kernel(where, *refs):
-    slabs = refs[:6]
-    edges, pair_edges, grad, pair_grad, send, keep, field, both, total = refs[6:]
-    fill_pair(where, slabs, edges, pair_edges, field, False)
+    stack, edges, pair_shared, grad, pair_grad, send, keep, field, both, total = refs
+    rows = grad.shape[0]
+    pair_edges = pair_shared.at[pl.ds(3 * rows, 3)]
+    fill_pair(
+        where, stack, lambda p, r: pair_shared.at[p * rows + r], edges, pair_edges, field, False
+    )
     ordered(where, grad, pair_grad, both)
     for row in range(both.shape[0]):
         part = lax.dot_general(
@@ -221,9 +229,8 @@
 
 
 def second_total_kernel(where, *refs):
-    slabs = refs[:6]
-    edges, hidden, total, field = refs[6:]
-    fill(where, slabs, edges, field)
+    hidden, total, field = refs[3:]
+    fill(where, *refs[:3], field)
     for row in range(hidden.shape[0]):
         part = lax.dot_general(
             window(field, row),
@@ -235,9 +242,8 @@
 
 
 def first_total_kernel(where, *refs):
-    slabs = refs[:6]
-    edges, grad, total, field = refs[6:]
-    fill(where, slabs, edges, field)
+    grad, total, field = refs[3:]
+    fill(where, *refs[:3], field)
     for row in range(grad.shape[0]):
         part = lax.dot_general(
             spread(grad[row]),
@@ -296,7 +302,7 @@
     return jax.ShapeDtypeStruct(shape, dtype)
 
 
-def call(kernel, name, out_shapes, args, scratch=(), flops=0, scalars=True):
+def call(kernel, name, out_shapes, args, scratch=(), flops=0, scalars=True, busy=1):
     moved = sum(math.prod(a.shape) * a.dtype.itemsize for a in (*args, *out_shapes))
     return pl.pallas_call(
         kernel,
@@ -305,7 +311,9 @@
         out_specs=[VMEM] * len(out_shapes),
         out_shape=out_shapes,
         scratch_shapes=[pltpu.VMEM(s.shape, s.dtype) for s in scratch],
-        cost_estimate=pl.CostEstimate(flops=flops, bytes_accessed=moved, transcendentals=0),
+        cost_estimate=pl.CostEstimate(
+            flops=flops * busy, bytes_accessed=moved * busy, transcendentals=0
+        ),
         compiler_params=pltpu.CompilerParams(vmem_limit_bytes=LIMIT),
     )(*args)
 
@@ -373,12 +381,11 @@
     field = struct((rows + 2, 3, chans, width), BF16)
     matrix = struct((3 * chans, 9 * chans), BF16)
 
-    (own,) = call(prepare_kernel, "prepare_volume", [slab], (volume,), scalars=False)
-    own_even, own_odd, own_pair = swap_planes(own, 0), swap_planes(own, 1), swap_rows(own, 0)
-    (grad_own,) = call(
-        prepare_kernel, "prepare_cotangent", [slab], (cotangent,), scalars=False
-    )
-    grad_even, grad_odd = swap_planes(grad_own, 0), swap_planes(grad_own, 1)
+    stack = struct((3, rows, chans, width), BF16)
+    edge = struct((3, chans, width), BF16)
+
+    volume_planes = (swap_planes(volume, 0), swap_planes(volume, 1))
+    grad_planes = (swap_planes(cotangent, 0), swap_planes(cotangent, 1))
     first_weights, second_weights, back_weights = call(
         weights_kernel,
         "weights",
@@ -386,84 +393,83 @@
         (first_filter.transpose(1, 0, 2), second_filter.transpose(1, 0, 2)),
         scalars=False,
     )
-
-    def across(own, even, odd):
-        (out,) = call(
-            edge_kernel,
-            "edges",
-            [struct((3, chans, width), BF16)],
-            (where, own, even, odd),
-        )
-        return swap_rows(out, 1)
-
-    edges = across(own, after(own_even, first_weights), own_odd)
-    slabs = (own, own_even, own_odd, own_pair, swap_rows(own_even, 0), swap_rows(own_odd, 0))
-    hidden, slope = call(
+    own, across, inside = call(
+        gather_kernel,
+        "gather_volume",
+        [stack, edge, edge],
+        (where, volume, after(volume_planes[0], first_weights), volume_planes[1]),
+    )
+    slabs = (own, swap_rows(inside, 0), swap_rows(across, 1))
+    own, across, inside = call(
+        gather_kernel,
+        "gather_cotangent",
+        [stack, edge, edge],
+        (where, cotangent, *grad_planes),
+    )
+    grad_slabs = (own, swap_rows(inside, 0), swap_rows(across, 1))
+    hidden, slope, shared = call(
         first_kernel,
         "first_conv",
-        [slab, struct(slab.shape, F32)],
-        (where, *slabs, edges, first_weights),
+        [slab, struct(slab.shape, F32), struct((4 * rows + 3, chans, width), BF16)],
+        (where, *slabs, first_weights),
         [field],
         flops,
-    )
-    hidden_pair = swap_rows(hidden, 0)
+        busy=1,
+    )
+    pair_shared = swap_rows(shared, 0)
     hidden_even, hidden_odd = swap_planes(hidden, 0), swap_planes(hidden, 1)
-    grad_edges = across(grad_own, grad_even, grad_odd)
-    grad_slabs = (
-        grad_own,
-        grad_even,
-        grad_odd,
-        swap_rows(grad_own, 0),
-        swap_rows(grad_even, 0),
-        swap_rows(grad_odd, 0),
-    )
     half = struct((rows, chans // 2, width), BF16)
     grads = call(
         grad_kernel,
         "hidden_grad",
         [half, half] if pairwise else [slab],
-        (where, *grad_slabs, grad_edges, back_weights, slope),
+        (where, *grad_slabs, back_weights, slope),
         [field, struct((chans, width), BF16)],
         flops,
+        busy=20,
     )
     shape = (outs // row_count, taps, ins // plane_count)
 
-    def hidden_rows(even, odd, *others):
-        across, inside = call(
-            edge_kernel,
-            "hidden_edges",
-            [struct((3, chans, width), BF16)] * 2,
-            (where, hidden, even, odd),
-        )
-        across, inside, *_ = lax.optimization_barrier((across, inside, *others))
-        return swap_rows(inside, 0), swap_rows(across, 1)
-
-    def convolved(inside, across):
+    def hidden_rows(even, odd):
+        own, across, inside = call(
+            gather_hidden_kernel, "gather_hidden", [stack, edge, edge], (where, hidden, even, odd)
+        )
+        return own, swap_rows(inside, 0), swap_rows(across, 1)
+
+    def convolved(*slabs):
         (out,) = call(
             second_kernel,
             "second_conv",
             [struct(volume.shape, BF16)],
-            (where, hidden, hidden_even, hidden_odd, inside, across, second_weights),
+            (where, *slabs, second_weights),
             [field, slab],
             flops,
         )
         return out
 
     if pairwise:
-        pair_edges, pair_grad_edges = swap_rows(edges, 0), swap_rows(grad_edges, 0)
         wide = 2 * rows + 2
         block = shape[0]
         second_send, second_keep = call(
             second_grad_kernel,
             "second_filter_grad",
             [struct((9, block, 3 * ins), BF16), struct((9, block, 3 * ins), F32)],
-            (where, *grad_slabs, grad_edges, pair_grad_edges, hidden, hidden_pair),
+            (
+                where,
+                grad_slabs[0],
+                swap_rows(after(grad_slabs[0], hidden), 0),
+                grad_slabs[2],
+                swap_rows(grad_slabs[2], 0),
+                hidden,
+                pair_shared,
+            ),
             [
                 struct((wide, 3, 2 * block, width), BF16),
                 struct((2 * rows, chans, width), BF16),
                 struct((9, 2 * block, 3 * ins), F32),
             ],
             flops,
+            busy=0,
         )
         second_arrived = cross(second_send)
         first_send, first_keep = call(
@@ -472,9 +478,9 @@
             [struct((3, block, 9 * ins), BF16), struct((3, block, 9 * ins), F32)],
             (
                 where,
-                *slabs,
-                edges,
-                pair_edges,
+                slabs[0],
+                slabs[2],
+                pair_shared,
                 after(grads[0], second_send),
                 swap_rows(grads[1], 0),
             ),
@@ -484,14 +490,15 @@
                 struct((3, 2 * block, 9 * ins), F32),
             ],
             flops,
+            busy=0,
         )
         first_arrived = cross(first_send)
-        inside, across = hidden_rows(after(hidden_even, first_send), hidden_odd, second_arrived)
+        hidden_slabs = hidden_rows(after(hidden_even, first_send), hidden_odd)
         steps = range(3)
         second_taps = [26 - (a * 9 + b * 3 + e) for b in steps for a in steps for e in steps]
         first_taps = [a * 9 + b * 3 + e for e in steps for b in steps for a in steps]
         *second_parts, second_keep = packed_parts(
-            where, after(second_keep, inside), second_arrived
+            where, after(second_keep, hidden_slabs[1]), second_arrived
         )
         second_parts = exchanged(second_parts)
         *first_parts, first_keep = packed_parts(
@@ -501,15 +508,17 @@
         second_sum = finished(
             after(second_keep, first_keep), second_parts, second_taps, factor, shape
         )
-        first_sum = finished(first_keep, first_parts, first_taps, factor, shape)
-        second_out = convolved(after(inside, first_keep), across)
+        second_out = convolved(after(hidden_slabs[0], second_sum), *hidden_slabs[1:])
+        first_sum = finished(
+            after(first_keep, second_out), first_parts, first_taps, factor, shape
+        )
     else:
         second_out = convolved(*hidden_rows(hidden_even, hidden_odd))
         (second_total,) = call(
             second_total_kernel,
             "second_filter_grad",
             [struct((9, outs, 3 * ins), F32)],
-            (where, *grad_slabs, grad_edges, hidden),
+            (where, *grad_slabs, hidden),
             [field],
             flops,
         )
@@ -517,7 +526,7 @@
             first_total_kernel,
             "first_filter_grad",
             [struct((3, outs, 9 * ins), F32)],
-            (where, *slabs, edges, *grads),
+            (where, *slabs, *grads),
             [field],
             flops,
         )

time: 65.7 us -> 60.7 us (0.924)
  starting transfers between devices: 34.8 us -> 29.9 us
    ppermute x6, starting transfers between devices: 11.3 us -> 7.62 us  [exchanged(): lax.ppermute(value, 'cin', [(i, i ^ k + 1) for i in range(parts)])]
    ppermute x2, waiting for transfers between devices: 4.96 us -> 1.89 us  [cross(): lax.ppermute(values, 'cout', [(i, i ^ 2) for i in range(lax.axis_size('co...]
    ppermute x14 -> x10, starting transfers between devices: 10.2 us -> 7.23 us  [swap_rows(): return lax.ppermute(values, 'cout', links(lax.axis_size('cout'), odd))]
    ppermute x6, waiting for transfers between devices: 1.46 us -> 4.39 us  [exchanged(): lax.ppermute(value, 'cin', [(i, i ^ k + 1) for i in range(parts)])]
    ppermute x6, starting transfers between devices: 11.2 us -> 12.9 us  [swap_planes(): return lax.ppermute(values, 'cin', links(lax.axis_size('cin'), odd))]
    ppermute x14 -> x10, waiting for transfers between devices: 0.8 us -> 1.56 us  [swap_rows(): return lax.ppermute(values, 'cout', links(lax.axis_size('cout'), odd))]
    pallas_call x15 -> x13, Pallas kernels: 17.2 us -> 17.7 us  [call(): pl.pallas_call(kernel, name=name, in_specs=[SMEM] * scalars + [VMEM] * (l...]
  transfers between devices with their start and end apart: 28 -> 24, of which waited for: 5 -> 5; matrix products, arithmetic and copies ran while one was open for 0% -> 0% of each run, Pallas kernels for 25% -> 28%
where the time goes in v4:
time: 60.7 us; the launch traced here: 60.4 us
  starting transfers between devices  29.9 us (49%)
  Pallas kernels  17.7 us (29%)
  waiting for transfers between devices  9.27 us (15%)
  local copies, waits for them, and re-layouts  2.66 us (4%)
  between operations  0.86 us (1%)
    pallas_call x13, Pallas kernels, call(): pl.pallas_call(kernel, name=name, in_specs=[SMEM] * scalars + [VMEM] * (l...  17.7 us
    ppermute x6, starting transfers between devices, swap_planes(): return lax.ppermute(values, 'cin', links(lax.axis_size('cin'), odd))  12.9 us
    ppermute x6, starting transfers between devices, exchanged(): lax.ppermute(value, 'cin', [(i, i ^ k + 1) for i in range(parts)])  7.62 us
    ppermute x10, starting transfers between devices, swap_rows(): return lax.ppermute(values, 'cout', links(lax.axis_size('cout'), odd))  7.23 us
    ppermute x6, waiting for transfers between devices, exchanged(): lax.ppermute(value, 'cin', [(i, i ^ k + 1) for i in range(parts)])  4.39 us
    unnamed x8, local copies, waits for them, and re-layouts  2.66 us
    ppermute x2, starting transfers between devices, cross(): lax.ppermute(values, 'cout', [(i, i ^ 2) for i in range(lax.axis_size('co...  2.09 us
    ppermute x2, waiting for transfers between devices, cross(): lax.ppermute(values, 'cout', [(i, i ^ 2) for i in range(lax.axis_size('co...  1.89 us
  transfers between devices with their start and end apart: 24, of which 5 were waited for; matrix products, arithmetic and copies ran while one was open for 0% of the time, Pallas kernels for 28%

profile of v4, /device:TPU:0, one launch (start us, length us, event | category | flops | bytes accessed | tf_op | source)
XLA Modules:
  0.0 60.4 jit_solution(10134288394698109447)
XLA Ops:
  0.6 3.1 %collective-permute-start = (bf16[128,1,4,256]{3,2,1,0:T(4,128)(2,1)}, bf16[128,1,4,256]{3,2,1,0:T(4,128)(2,1)S(1)}, u32[]{:S(2)}, u32[]{:S(2)}) collective-permute-start(bf16[128,1,4,256]{3,2,1,0:T(4,128)(2,1)} %own.2), channel_id=1, source_target_pairs={{0,4},{4,0},{8,12},{12,8},{1,5},{5,1},{9,13},{13,9},{2,6},{6,2},{1... | collective-permute-start | bytes 786440 | tf_op jit(solution)/shard_map/ppermute | solution.py:26
  4.4 4.4 %collective-permute-start.6 = (bf16[128,1,4,256]{3,2,1,0:T(4,128)(2,1)}, bf16[128,1,4,256]{3,2,1,0:T(4,128)(2,1)S(1)}, u32[]{:S(2)}, u32[]{:S(2)}) collective-permute-start(bf16[128,1,4,256]{3,2,1,0:T(4,128)(2,1)} %own.3), channel_id=1, source_target_pairs={{0,4},{4,0},{8,12},{12,8},{1,5},{5,1},{9,13},{13,9},{2,6},{6,2},{1... | collective-permute-start | bytes 786440 | tf_op jit(solution)/shard_map/ppermute | solution.py:26
  9.6 1.2 %copy-done = bf16[128,27,128]{2,0,1:T(8,128)(2,1)S(1)} copy-done((bf16[128,27,128]{2,0,1:T(8,128)(2,1)S(1)}, bf16[128,27,128]{2,0,1:T(8,128)(2,1)}, u32[]{:S(2)}) %copy-start) | copy-done | bytes 884760
  10.7 1.2 %copy-done.1 = bf16[128,27,128]{2,0,1:T(8,128)(2,1)S(1)} copy-done((bf16[128,27,128]{2,0,1:T(8,128)(2,1)S(1)}, bf16[128,27,128]{2,0,1:T(8,128)(2,1)}, u32[]{:S(2)}) %copy-start.1) | copy-done | bytes 884760
  14.4 1.4 %collective-permute-done.6.even = bf16[128,1,4,256]{3,2,1,0:T(4,128)(2,1)S(1)} collective-permute-done((bf16[128,1,4,256]{3,2,1,0:T(4,128)(2,1)}, bf16[128,1,4,256]{3,2,1,0:T(4,128)(2,1)S(1)}, u32[]{:S(2)}, u32[]{:S(2)}) %collective-permute-start.6) | collective-permute-done | bytes 262176 | tf_op jit(solution)/shard_map/ppermute | solution.py:26
  16.7 1.5 %collective-permute-start.8 = (bf16[3,128,256]{2,1,0:T(8,128)(2,1)S(1)}, bf16[3,128,256]{2,1,0:T(8,128)(2,1)S(1)}, u32[]{:S(2)}, u32[]{:S(2)}) collective-permute-start(bf16[3,128,256]{2,1,0:T(8,128)(2,1)S(1)} %get-tuple-element.49), channel_id=1, source_target_pairs={{0,1},{1,0},{2,3},{3,2},{4,5},{5,4},{6,7},{7,6},{8,9},{9,8},{10,11... | collective-permute-start | bytes 589832 | tf_op jit(solution)/shard_map/ppermute | solution.py:30
  18.9 2.0 %first_conv.1 = (bf16[4,128,256]{2,1,0:T(8,128)(2,1)S(1)}, f32[4,128,256]{2,1,0:T(8,128)S(1)}, bf16[19,128,256]{2,1,0:T(8,128)(2,1)S(1)}) custom-call(s32[4]{0:T(128)S(1)} %pad_add_fusion.where, bf16[3,4,128,256]{3,2,1,0:T(8,128)(2,1)S(1)} %get-tuple-element.43.refs_0_, bf16[3,128,256]{2,1,0:T(8,128)(2,1)S(1)} %collective-permute-done.2.refs_1_, ...), custom_call_target="tpu_custom_call" | custom-call | flops 905969664 | bytes 4096016 | tf_op jit(solution)/shard_map/first_conv/pallas_call | solution.py:307
  20.9 3.4 %collective-permute-start.4 = (bf16[4,128,256]{2,1,0:T(8,128)(2,1)S(1)}, bf16[4,128,256]{2,1,0:T(8,128)(2,1)S(1)}, u32[]{:S(2)}, u32[]{:S(2)}) collective-permute-start(bf16[4,128,256]{2,1,0:T(8,128)(2,1)S(1)} %get-tuple-element.46.refs_4_.own), channel_id=1, source_target_pairs={{0,4},{4,0},{8,12},{12,8},{1,5},{5,1},{9,13},{13,9},{2,6},{6,2},{1... | collective-permute-start | bytes 786440 | tf_op jit(solution)/shard_map/ppermute | solution.py:26
  25.0 2.6 %collective-permute-start.5 = (bf16[19,128,256]{2,1,0:T(8,128)(2,1)S(1)}, bf16[19,128,256]{2,1,0:T(8,128)(2,1)S(1)}, u32[]{:S(2)}, u32[]{:S(2)}) collective-permute-start(bf16[19,128,256]{2,1,0:T(8,128)(2,1)S(1)} %get-tuple-element.47), channel_id=1, source_target_pairs={{0,1},{1,0},{2,3},{3,2},{4,5},{5,4},{6,7},{7,6},{8,9},{9,8},{10,11... | collective-permute-start | bytes 3735560 | tf_op jit(solution)/shard_map/ppermute | solution.py:30
  28.2 1.9 %hidden_grad.1 = (bf16[4,64,256]{2,1,0:T(8,128)(2,1)S(1)}, bf16[4,64,256]{2,1,0:T(8,128)(2,1)S(1)}) custom-call(s32[4]{0:T(128)S(1)} %pad_add_fusion.where, bf16[3,4,128,256]{3,2,1,0:T(8,128)(2,1)S(1)} %get-tuple-element.54.refs_0_, bf16[3,128,256]{2,1,0:T(8,128)(2,1)S(1)} %collective-permute-done.8.refs_1_, ...), custom_call_target="tpu_custom_call" | custom-call | flops 18119393280 | bytes 57016640 | tf_op jit(solution)/shard_map/hidden_grad/pallas_call | solution.py:307
  30.1 1.5 %collective-permute-done.11.refs_3_ = bf16[3,128,256]{2,1,0:T(8,128)(2,1)S(1)} collective-permute-done((bf16[3,128,256]{2,1,0:T(8,128)(2,1)S(1)}, bf16[3,128,256]{2,1,0:T(8,128)(2,1)S(1)}, u32[]{:S(2)}, u32[]{:S(2)}) %collective-permute-start.11) | collective-permute-done | bytes 196640 | tf_op jit(solution)/shard_map/ppermute | solution.py:30
  32.0 2.1 %second_filter_grad.1 = (bf16[9,32,384]{2,1,0:T(8,128)(2,1)S(1)}, f32[9,32,384]{2,1,0:T(8,128)S(1)}) custom-call(s32[4]{0:T(128)S(1)} %pad_add_fusion.where, bf16[3,4,128,256]{3,2,1,0:T(8,128)(2,1)S(1)} %get-tuple-element.54.refs_0_, bf16[3,4,128,256]{3,2,1,0:T(8,128)(2,1)S(1)} %collective-permute-done.10.refs_1_, ...), custom_call_target="tpu_custom_call" | custom-call | tf_op jit(solution)/shard_map/second_filter_grad/pallas_call | solution.py:307
  34.1 1.0 %collective-permute-start.15 = (bf16[9,32,384]{2,1,0:T(8,128)(2,1)S(1)}, bf16[9,32,384]{2,1,0:T(8,128)(2,1)S(1)}, u32[]{:S(2)}, u32[]{:S(2)}) collective-permute-start(bf16[9,32,384]{2,1,0:T(8,128)(2,1)S(1)} %get-tuple-element.55), channel_id=1, source_target_pairs={{0,2},{1,3},{2,0},{3,1},{4,6},{5,7},{6,4},{7,5},{8,10},{9,11},{10,... | collective-permute-start | bytes 663560 | tf_op jit(solution)/shard_map/ppermute | solution.py:360
  35.1 2.3 %first_filter_grad.1 = (bf16[3,32,1152]{2,1,0:T(8,128)(2,1)S(1)}, f32[3,32,1152]{2,1,0:T(8,128)S(1)}) custom-call(s32[4]{0:T(128)S(1)} %pad_add_fusion.where, bf16[3,4,128,256]{3,2,1,0:T(8,128)(2,1)S(1)} %get-tuple-element.43.refs_0_, bf16[3,128,256]{2,1,0:T(8,128)(2,1)S(1)} %collective-permute-done.3.refs_2_.refs_1_, ...), custom_call_target="tpu_custom_call" | custom-call | tf_op jit(solution)/shard_map/first_filter_grad/pallas_call | solution.py:307
  38.3 1.1 %collective-permute-start.16 = (bf16[3,32,1152]{2,1,0:T(8,128)(2,1)S(1)}, bf16[3,32,1152]{2,1,0:T(8,128)(2,1)S(1)}, u32[]{:S(2)}, u32[]{:S(2)}) collective-permute-start(bf16[3,32,1152]{2,1,0:T(8,128)(2,1)S(1)} %get-tuple-element.58), channel_id=1, source_target_pairs={{0,2},{1,3},{2,0},{3,1},{4,6},{5,7},{6,4},{7,5},{8,10},{9,11},{10,... | collective-permute-start | bytes 663560 | tf_op jit(solution)/shard_map/ppermute | solution.py:360
  40.0 1.9 %collective-permute-done.15.arrived = bf16[9,32,384]{2,1,0:T(8,128)(2,1)S(1)} collective-permute-done((bf16[9,32,384]{2,1,0:T(8,128)(2,1)S(1)}, bf16[9,32,384]{2,1,0:T(8,128)(2,1)S(1)}, u32[]{:S(2)}, u32[]{:S(2)}) %collective-permute-start.15) | collective-permute-done | bytes 221216 | tf_op jit(solution)/shard_map/ppermute | solution.py:360
  41.9 1.0 %pack_parts.2 = (bf16[7,32,128]{2,1,0:T(8,128)(2,1)S(1)}, bf16[7,32,128]{2,1,0:T(8,128)(2,1)S(1)}, bf16[7,32,128]{2,1,0:T(8,128)(2,1)S(1)}, f32[7,32,128]{2,1,0:T(8,128)S(1)}) custom-call(s32[4]{0:T(128)S(1)} %pad_add_fusion.where, f32[9,32,384]{2,1,0:T(8,128)S(1)} %get-tuple-element.63.held, bf16[9,32,384]{2,1,0:T(8,128)(2,1)S(1)} %collective-permute-done.15.arrived), custom_call_target="tpu_custom_call" | custom-call | bytes 950288 | tf_op jit(solution)/shard_map/pack_parts/pallas_call | solution.py:307
  42.9 2.8 %collective-permute-start.17 = (bf16[7,32,128]{2,1,0:T(8,128)(2,1)S(1)}, bf16[7,32,128]{2,1,0:T(8,128)(2,1)S(1)}, u32[]{:S(2)}, u32[]{:S(2)}) collective-permute-start(bf16[7,32,128]{2,1,0:T(8,128)(2,1)S(1)} %get-tuple-element.69), channel_id=1, source_target_pairs={{0,4},{4,0},{8,12},{12,8},{1,5},{5,1},{9,13},{13,9},{2,6},{6,2},{1... | collective-permute-start | bytes 172040 | tf_op jit(solution)/shard_map/ppermute | solution.py:343
  45.9 2.2 %collective-permute-start.19 = (bf16[7,32,128]{2,1,0:T(8,128)(2,1)S(1)}, bf16[7,32,128]{2,1,0:T(8,128)(2,1)S(1)}, u32[]{:S(2)}, u32[]{:S(2)}) collective-permute-start(bf16[7,32,128]{2,1,0:T(8,128)(2,1)S(1)} %get-tuple-element.71), channel_id=1, source_target_pairs={{0,12},{4,8},{8,4},{12,0},{1,13},{5,9},{9,5},{13,1},{2,14},{6,10},... | collective-permute-start | bytes 172040 | tf_op jit(solution)/shard_map/ppermute | solution.py:343
  48.1 1.0 %pack_parts.3 = (bf16[7,32,128]{2,1,0:T(8,128)(2,1)S(1)}, bf16[7,32,128]{2,1,0:T(8,128)(2,1)S(1)}, bf16[7,32,128]{2,1,0:T(8,128)(2,1)S(1)}, f32[7,32,128]{2,1,0:T(8,128)S(1)}) custom-call(s32[4]{0:T(128)S(1)} %pad_add_fusion.where, f32[3,32,1152]{2,1,0:T(8,128)S(1)} %get-tuple-element.66.held, bf16[3,32,1152]{2,1,0:T(8,128)(2,1)S(1)} %collective-permute-done.16.arrived), custom_call_target="tpu_custom_call" | custom-call | bytes 950288 | tf_op jit(solution)/shard_map/pack_parts/pallas_call | solution.py:307
  49.1 1.3 %collective-permute-start.21 = (bf16[7,32,128]{2,1,0:T(8,128)(2,1)S(1)}, bf16[7,32,128]{2,1,0:T(8,128)(2,1)S(1)}, u32[]{:S(2)}, u32[]{:S(2)}) collective-permute-start(bf16[7,32,128]{2,1,0:T(8,128)(2,1)S(1)} %get-tuple-element.76), channel_id=1, source_target_pairs={{0,4},{4,0},{8,12},{12,8},{1,5},{5,1},{9,13},{13,9},{2,6},{6,2},{1... | collective-permute-start | bytes 172040 | tf_op jit(solution)/shard_map/ppermute | solution.py:343
  51.3 2.1 %collective-permute-done.18.refs_1_ = bf16[7,32,128]{2,1,0:T(8,128)(2,1)S(1)} collective-permute-done((bf16[7,32,128]{2,1,0:T(8,128)(2,1)S(1)}, bf16[7,32,128]{2,1,0:T(8,128)(2,1)S(1)}, u32[]{:S(2)}, u32[]{:S(2)}) %collective-permute-start.18) | collective-permute-done | bytes 57376 | tf_op jit(solution)/shard_map/ppermute | solution.py:343
  54.5 2.7 %second_conv.1 = bf16[128,1,4,256]{3,2,1,0:T(4,128)(2,1)} custom-call(s32[4]{0:T(128)S(1)} %pad_add_fusion.where, bf16[3,4,128,256]{3,2,1,0:T(8,128)(2,1)S(1)} %get-tuple-element.72.refs_0_, bf16[3,128,256]{2,1,0:T(8,128)(2,1)S(1)} %collective-permute-done.14.refs_1_, bf16[3,128,256]{2,1,0:T(8,128)(2,1)S(1)} %collective-permute-done.20.refs_2_, ...), custom_call_target="tpu_custom_call" | custom-call | flops 905969664 | bytes 2326544 | tf_op jit(solution)/shard_map/second_conv/pallas_call | solution.py:307
  57.2 2.3 %collective-permute-done.23.refs_2_ = bf16[7,32,128]{2,1,0:T(8,128)(2,1)S(1)} collective-permute-done((bf16[7,32,128]{2,1,0:T(8,128)(2,1)S(1)}, bf16[7,32,128]{2,1,0:T(8,128)(2,1)S(1)}, u32[]{:S(2)}, u32[]{:S(2)}) %collective-permute-start.23) | collective-permute-done | bytes 57376 | tf_op jit(solution)/shard_map/ppermute | solution.py:343
  (46 shorter events, 11.5 us)
Async XLA Ops:
  0.6 11.9 %collective-permute-start = (bf16[128,1,4,256]{3,2,1,0:T(4,128)(2,1)}, bf16[128,1,4,256]{3,2,1,0:T(4,128)(2,1)S(1)}, u32[]{:S(2)}, u32[]{:S(2)}) collective-permute-start(bf16[128,1,4,256]{3,2,1,0:T(4,128)(2,1)} %own.2), channel_id=1, source_target_pairs={{0,4},{4,0},{8,12},{12,8},{1,5},{5,1},{9,13},{13,9},{2,6},{6,2},{1... | collective-permute-start | bytes 786440 | tf_op jit(solution)/shard_map/ppermute | solution.py:26
  3.7 8.8 %collective-permute-start.1 = (bf16[128,1,4,256]{3,2,1,0:T(4,128)(2,1)}, bf16[128,1,4,256]{3,2,1,0:T(4,128)(2,1)S(1)}, u32[]{:S(2)}, u32[]{:S(2)}) collective-permute-start(bf16[128,1,4,256]{3,2,1,0:T(4,128)(2,1)} %own.2), channel_id=1, source_target_pairs={{4,8},{8,4},{5,9},{9,5},{6,10},{10,6},{7,11},{11,7},{20,24},{24,20... | collective-permute-start | bytes 786440 | tf_op jit(solution)/shard_map/ppermute | solution.py:26
  4.4 11.5 %collective-permute-start.6 = (bf16[128,1,4,256]{3,2,1,0:T(4,128)(2,1)}, bf16[128,1,4,256]{3,2,1,0:T(4,128)(2,1)S(1)}, u32[]{:S(2)}, u32[]{:S(2)}) collective-permute-start(bf16[128,1,4,256]{3,2,1,0:T(4,128)(2,1)} %own.3), channel_id=1, source_target_pairs={{0,4},{4,0},{8,12},{12,8},{1,5},{5,1},{9,13},{13,9},{2,6},{6,2},{1... | collective-permute-start | bytes 786440 | tf_op jit(solution)/shard_map/ppermute | solution.py:26
  8.8 7.0 %collective-permute-start.7 = (bf16[128,1,4,256]{3,2,1,0:T(4,128)(2,1)}, bf16[128,1,4,256]{3,2,1,0:T(4,128)(2,1)S(1)}, u32[]{:S(2)}, u32[]{:S(2)}) collective-permute-start(bf16[128,1,4,256]{3,2,1,0:T(4,128)(2,1)} %own.3), channel_id=1, source_target_pairs={{4,8},{8,4},{5,9},{9,5},{6,10},{10,6},{7,11},{11,7},{20,24},{24,20... | collective-permute-start | bytes 786440 | tf_op jit(solution)/shard_map/ppermute | solution.py:26
  13.7 5.2 %collective-permute-start.2 = (bf16[3,128,256]{2,1,0:T(8,128)(2,1)S(1)}, bf16[3,128,256]{2,1,0:T(8,128)(2,1)S(1)}, u32[]{:S(2)}, u32[]{:S(2)}) collective-permute-start(bf16[3,128,256]{2,1,0:T(8,128)(2,1)S(1)} %get-tuple-element.44), channel_id=1, source_target_pairs={{0,1},{1,0},{2,3},{3,2},{4,5},{5,4},{6,7},{7,6},{8,9},{9,8},{10,11... | collective-permute-start | bytes 589832 | tf_op jit(solution)/shard_map/ppermute | solution.py:30
  13.8 5.1 %collective-permute-start.3 = (bf16[3,128,256]{2,1,0:T(8,128)(2,1)S(1)}, bf16[3,128,256]{2,1,0:T(8,128)(2,1)S(1)}, u32[]{:S(2)}, u32[]{:S(2)}) collective-permute-start(bf16[3,128,256]{2,1,0:T(8,128)(2,1)S(1)} %get-tuple-element.45), channel_id=1, source_target_pairs={{1,2},{2,1},{5,6},{6,5},{9,10},{10,9},{13,14},{14,13},{17,18},{18,... | collective-permute-start | bytes 589832 | tf_op jit(solution)/shard_map/ppermute | solution.py:30
  16.7 10.9 %collective-permute-start.8 = (bf16[3,128,256]{2,1,0:T(8,128)(2,1)S(1)}, bf16[3,128,256]{2,1,0:T(8,128)(2,1)S(1)}, u32[]{:S(2)}, u32[]{:S(2)}) collective-permute-start(bf16[3,128,256]{2,1,0:T(8,128)(2,1)S(1)} %get-tuple-element.49), channel_id=1, source_target_pairs={{0,1},{1,0},{2,3},{3,2},{4,5},{5,4},{6,7},{7,6},{8,9},{9,8},{10,11... | collective-permute-start | bytes 589832 | tf_op jit(solution)/shard_map/ppermute | solution.py:30
  18.2 9.5 %collective-permute-start.9 = (bf16[3,128,256]{2,1,0:T(8,128)(2,1)S(1)}, bf16[3,128,256]{2,1,0:T(8,128)(2,1)S(1)}, u32[]{:S(2)}, u32[]{:S(2)}) collective-permute-start(bf16[3,128,256]{2,1,0:T(8,128)(2,1)S(1)} %get-tuple-element.50), channel_id=1, source_target_pairs={{1,2},{2,1},{5,6},{6,5},{9,10},{10,9},{13,14},{14,13},{17,18},{18,... | collective-permute-start | bytes 589832 | tf_op jit(solution)/shard_map/ppermute | solution.py:30
  20.9 16.5 %collective-permute-start.4 = (bf16[4,128,256]{2,1,0:T(8,128)(2,1)S(1)}, bf16[4,128,256]{2,1,0:T(8,128)(2,1)S(1)}, u32[]{:S(2)}, u32[]{:S(2)}) collective-permute-start(bf16[4,128,256]{2,1,0:T(8,128)(2,1)S(1)} %get-tuple-element.46.refs_4_.own), channel_id=1, source_target_pairs={{0,4},{4,0},{8,12},{12,8},{1,5},{5,1},{9,13},{13,9},{2,6},{6,2},{1... | collective-permute-start | bytes 786440 | tf_op jit(solution)/shard_map/ppermute | solution.py:26
  24.3 13.2 %collective-permute-start.13 = (bf16[4,128,256]{2,1,0:T(8,128)(2,1)S(1)}, bf16[4,128,256]{2,1,0:T(8,128)(2,1)S(1)}, u32[]{:S(2)}, u32[]{:S(2)}) collective-permute-start(bf16[4,128,256]{2,1,0:T(8,128)(2,1)S(1)} %get-tuple-element.46.refs_4_.own), channel_id=1, source_target_pairs={{4,8},{8,4},{5,9},{9,5},{6,10},{10,6},{7,11},{11,7},{20,24},{24,20... | collective-permute-start | bytes 786440 | tf_op jit(solution)/shard_map/ppermute | solution.py:26
  25.0 7.0 %collective-permute-start.5 = (bf16[19,128,256]{2,1,0:T(8,128)(2,1)S(1)}, bf16[19,128,256]{2,1,0:T(8,128)(2,1)S(1)}, u32[]{:S(2)}, u32[]{:S(2)}) collective-permute-start(bf16[19,128,256]{2,1,0:T(8,128)(2,1)S(1)} %get-tuple-element.47), channel_id=1, source_target_pairs={{0,1},{1,0},{2,3},{3,2},{4,5},{5,4},{6,7},{7,6},{8,9},{9,8},{10,11... | collective-permute-start | bytes 3735560 | tf_op jit(solution)/shard_map/ppermute | solution.py:30
  27.6 4.3 %collective-permute-start.10 = (bf16[3,4,128,256]{3,2,1,0:T(8,128)(2,1)S(1)}, bf16[3,4,128,256]{3,2,1,0:T(8,128)(2,1)S(1)}, u32[]{:S(2)}, u32[]{:S(2)}) collective-permute-start(bf16[3,4,128,256]{3,2,1,0:T(8,128)(2,1)S(1)} %get-tuple-element.54.refs_0_), channel_id=1, source_target_pairs={{0,1},{1,0},{2,3},{3,2},{4,5},{5,4},{6,7},{7,6},{8,9},{9,8},{10,11... | collective-permute-start | bytes 2359304 | tf_op jit(solution)/shard_map/ppermute | solution.py:30
  27.7 3.9 %collective-permute-start.11 = (bf16[3,128,256]{2,1,0:T(8,128)(2,1)S(1)}, bf16[3,128,256]{2,1,0:T(8,128)(2,1)S(1)}, u32[]{:S(2)}, u32[]{:S(2)}) collective-permute-start(bf16[3,128,256]{2,1,0:T(8,128)(2,1)S(1)} %collective-permute-done.9.refs_2_), channel_id=1, source_target_pairs={{0,1},{1,0},{2,3},{3,2},{4,5},{5,4},{6,7},{7,6},{8,9},{9,8},{10,11... | collective-permute-start | bytes 589832 | tf_op jit(solution)/shard_map/ppermute | solution.py:30
  31.6 3.5 %collective-permute-start.12 = (bf16[4,64,256]{2,1,0:T(8,128)(2,1)S(1)}, bf16[4,64,256]{2,1,0:T(8,128)(2,1)S(1)}, u32[]{:S(2)}, u32[]{:S(2)}) collective-permute-start(bf16[4,64,256]{2,1,0:T(8,128)(2,1)S(1)} %get-tuple-element.57), channel_id=1, source_target_pairs={{0,1},{1,0},{2,3},{3,2},{4,5},{5,4},{6,7},{7,6},{8,9},{9,8},{10,11... | collective-permute-start | bytes 393224 | tf_op jit(solution)/shard_map/ppermute | solution.py:30
  34.1 7.8 %collective-permute-start.15 = (bf16[9,32,384]{2,1,0:T(8,128)(2,1)S(1)}, bf16[9,32,384]{2,1,0:T(8,128)(2,1)S(1)}, u32[]{:S(2)}, u32[]{:S(2)}) collective-permute-start(bf16[9,32,384]{2,1,0:T(8,128)(2,1)S(1)} %get-tuple-element.55), channel_id=1, source_target_pairs={{0,2},{1,3},{2,0},{3,1},{4,6},{5,7},{6,4},{7,5},{8,10},{9,11},{10,... | collective-permute-start | bytes 663560 | tf_op jit(solution)/shard_map/ppermute | solution.py:360
  38.1 1.9 %collective-permute-start.14 = (bf16[3,128,256]{2,1,0:T(8,128)(2,1)S(1)}, bf16[3,128,256]{2,1,0:T(8,128)(2,1)S(1)}, u32[]{:S(2)}, u32[]{:S(2)}) collective-permute-start(bf16[3,128,256]{2,1,0:T(8,128)(2,1)S(1)} %get-tuple-element.62), channel_id=1, source_target_pairs={{0,1},{1,0},{2,3},{3,2},{4,5},{5,4},{6,7},{7,6},{8,9},{9,8},{10,11... | collective-permute-start | bytes 589832 | tf_op jit(solution)/shard_map/ppermute | solution.py:30
  38.3 9.9 %collective-permute-start.16 = (bf16[3,32,1152]{2,1,0:T(8,128)(2,1)S(1)}, bf16[3,32,1152]{2,1,0:T(8,128)(2,1)S(1)}, u32[]{:S(2)}, u32[]{:S(2)}) collective-permute-start(bf16[3,32,1152]{2,1,0:T(8,128)(2,1)S(1)} %get-tuple-element.58), channel_id=1, source_target_pairs={{0,2},{1,3},{2,0},{3,1},{4,6},{5,7},{6,4},{7,5},{8,10},{9,11},{10,... | collective-permute-start | bytes 663560 | tf_op jit(solution)/shard_map/ppermute | solution.py:360
  39.4 15.2 %collective-permute-start.20 = (bf16[3,128,256]{2,1,0:T(8,128)(2,1)S(1)}, bf16[3,128,256]{2,1,0:T(8,128)(2,1)S(1)}, u32[]{:S(2)}, u32[]{:S(2)}) collective-permute-start(bf16[3,128,256]{2,1,0:T(8,128)(2,1)S(1)} %get-tuple-element.73), channel_id=1, source_target_pairs={{1,2},{2,1},{5,6},{6,5},{9,10},{10,9},{13,14},{14,13},{17,18},{18,... | collective-permute-start | bytes 589832 | tf_op jit(solution)/shard_map/ppermute | solution.py:30
  42.9 7.5 %collective-permute-start.17 = (bf16[7,32,128]{2,1,0:T(8,128)(2,1)S(1)}, bf16[7,32,128]{2,1,0:T(8,128)(2,1)S(1)}, u32[]{:S(2)}, u32[]{:S(2)}) collective-permute-start(bf16[7,32,128]{2,1,0:T(8,128)(2,1)S(1)} %get-tuple-element.69), channel_id=1, source_target_pairs={{0,4},{4,0},{8,12},{12,8},{1,5},{5,1},{9,13},{13,9},{2,6},{6,2},{1... | collective-permute-start | bytes 172040 | tf_op jit(solution)/shard_map/ppermute | solution.py:343
  45.7 7.8 %collective-permute-start.18 = (bf16[7,32,128]{2,1,0:T(8,128)(2,1)S(1)}, bf16[7,32,128]{2,1,0:T(8,128)(2,1)S(1)}, u32[]{:S(2)}, u32[]{:S(2)}) collective-permute-start(bf16[7,32,128]{2,1,0:T(8,128)(2,1)S(1)} %get-tuple-element.70), channel_id=1, source_target_pairs={{0,8},{4,12},{8,0},{12,4},{1,9},{5,13},{9,1},{13,5},{2,10},{6,14},... | collective-permute-start | bytes 172040 | tf_op jit(solution)/shard_map/ppermute | solution.py:343
  45.9 7.7 %collective-permute-start.19 = (bf16[7,32,128]{2,1,0:T(8,128)(2,1)S(1)}, bf16[7,32,128]{2,1,0:T(8,128)(2,1)S(1)}, u32[]{:S(2)}, u32[]{:S(2)}) collective-permute-start(bf16[7,32,128]{2,1,0:T(8,128)(2,1)S(1)} %get-tuple-element.71), channel_id=1, source_target_pairs={{0,12},{4,8},{8,4},{12,0},{1,13},{5,9},{9,5},{13,1},{2,14},{6,10},... | collective-permute-start | bytes 172040 | tf_op jit(solution)/shard_map/ppermute | solution.py:343
  49.1 8.1 %collective-permute-start.21 = (bf16[7,32,128]{2,1,0:T(8,128)(2,1)S(1)}, bf16[7,32,128]{2,1,0:T(8,128)(2,1)S(1)}, u32[]{:S(2)}, u32[]{:S(2)}) collective-permute-start(bf16[7,32,128]{2,1,0:T(8,128)(2,1)S(1)} %get-tuple-element.76), channel_id=1, source_target_pairs={{0,4},{4,0},{8,12},{12,8},{1,5},{5,1},{9,13},{13,9},{2,6},{6,2},{1... | collective-permute-start | bytes 172040 | tf_op jit(solution)/shard_map/ppermute | solution.py:343
  50.4 6.8 %collective-permute-start.22 = (bf16[7,32,128]{2,1,0:T(8,128)(2,1)S(1)}, bf16[7,32,128]{2,1,0:T(8,128)(2,1)S(1)}, u32[]{:S(2)}, u32[]{:S(2)}) collective-permute-start(bf16[7,32,128]{2,1,0:T(8,128)(2,1)S(1)} %get-tuple-element.77), channel_id=1, source_target_pairs={{0,8},{4,12},{8,0},{12,4},{1,9},{5,13},{9,1},{13,5},{2,10},{6,14},... | collective-permute-start | bytes 172040 | tf_op jit(solution)/shard_map/ppermute | solution.py:343
  53.4 6.0 %collective-permute-start.23 = (bf16[7,32,128]{2,1,0:T(8,128)(2,1)S(1)}, bf16[7,32,128]{2,1,0:T(8,128)(2,1)S(1)}, u32[]{:S(2)}, u32[]{:S(2)}) collective-permute-start(bf16[7,32,128]{2,1,0:T(8,128)(2,1)S(1)} %get-tuple-element.78), channel_id=1, source_target_pairs={{0,12},{4,8},{8,4},{12,0},{1,13},{5,9},{9,5},{13,1},{2,14},{6,10},... | collective-permute-start | bytes 172040 | tf_op jit(solution)/shard_map/ppermute | solution.py:343
  (4 other events, 7.3 us)

commit v5 on v4

--- a/solution.py
+++ b/solution.py
@@ -58,7 +58,7 @@
 
 
 def planes_of(where):
-    return (1, 2 * (1 - where[0]), 2 * where[0])
+    return (1, 2 * where[0], 2 * (1 - where[0]))
 
 
 def fill(where, stack, inside, edges, field):
@@ -105,17 +105,17 @@
     return combine(jnp.dot(weights[...], window(field, row), preferred_element_type=F32))
 
 
-def gather_kernel(where, own, even, odd, *refs):
+def gather_kernel(where, own, odd, even, *refs):
     stack, across, inside = refs
-    for plane, slab in zip(planes_of(where), (own, even, odd)):
+    for plane, slab in zip(planes_of(where), (own, odd, even)):
         stack[plane] = jnp.transpose(slab[:, 0], (1, 0, 2))
         across[plane] = stack[plane, where[1] * (stack.shape[1] - 1)]
         inside[plane] = stack[plane, (1 - where[1]) * (stack.shape[1] - 1)]
 
 
-def gather_hidden_kernel(where, own, even, odd, stack, across, inside):
+def gather_hidden_kernel(where, own, odd, even, stack, across, inside):
     last = own.shape[0] - 1
-    for plane, slab in zip(planes_of(where), (own, even, odd)):
+    for plane, slab in zip(planes_of(where), (own, odd, even)):
         stack[plane] = slab[...]
         across[plane] = slab[where[1] * last]
         inside[plane] = slab[(1 - where[1]) * last]
@@ -341,7 +341,7 @@
     parts = lax.axis_size("cin")
     return [
         lax.ppermute(value, "cin", [(i, i ^ (k + 1)) for i in range(parts)])
-        for k, value in enumerate(sends)
+        for k, value in reversed(list(enumerate(sends)))
     ]
 
 
@@ -384,8 +384,8 @@
     stack = struct((3, rows, chans, width), BF16)
     edge = struct((3, chans, width), BF16)
 
-    volume_planes = (swap_planes(volume, 0), swap_planes(volume, 1))
-    grad_planes = (swap_planes(cotangent, 0), swap_planes(cotangent, 1))
+    volume_planes = (swap_planes(volume, 1), swap_planes(volume, 0))
+    grad_planes = (swap_planes(cotangent, 1), swap_planes(cotangent, 0))
     first_weights, second_weights, back_weights = call(
         weights_kernel,
         "weights",
@@ -417,7 +417,7 @@
         busy=1,
     )
     pair_shared = swap_rows(shared, 0)
-    hidden_even, hidden_odd = swap_planes(hidden, 0), swap_planes(hidden, 1)
+    hidden_odd, hidden_even = swap_planes(hidden, 1), swap_planes(hidden, 0)
     half = struct((rows, chans // 2, width), BF16)
     grads = call(
         grad_kernel,
@@ -430,9 +430,9 @@
     )
     shape = (outs // row_count, taps, ins // plane_count)
 
-    def hidden_rows(even, odd):
+    def hidden_rows(odd, even):
         own, across, inside = call(
-            gather_hidden_kernel, "gather_hidden", [stack, edge, edge], (where, hidden, even, odd)
+            gather_hidden_kernel, "gather_hidden", [stack, edge, edge], (where, hidden, odd, even)
         )
         return own, swap_rows(inside, 0), swap_rows(across, 1)
 
@@ -457,7 +457,7 @@
             (
                 where,
                 grad_slabs[0],
-                swap_rows(after(grad_slabs[0], hidden), 0),
+                swap_rows(grad_slabs[0], 0),
                 grad_slabs[2],
                 swap_rows(grad_slabs[2], 0),
                 hidden,
@@ -493,7 +493,7 @@
             busy=0,
         )
         first_arrived = cross(first_send)
-        hidden_slabs = hidden_rows(after(hidden_even, first_send), hidden_odd)
+        hidden_slabs = hidden_rows(after(hidden_odd, first_send), hidden_even)
         steps = range(3)
         second_taps = [26 - (a * 9 + b * 3 + e) for b in steps for a in steps for e in steps]
         first_taps = [a * 9 + b * 3 + e for e in steps for b in steps for a in steps]
@@ -513,7 +513,7 @@
             after(first_keep, second_out), first_parts, first_taps, factor, shape
         )
     else:
-        second_out = convolved(*hidden_rows(hidden_even, hidden_odd))
+        second_out = convolved(*hidden_rows(hidden_odd, hidden_even))
         (second_total,) = call(
             second_total_kernel,
             "second_filter_grad",

time: 60.7 us -> 59.3 us (0.977)
  waiting for transfers between devices: 9.27 us -> 8.3 us
    ppermute x6, waiting for transfers between devices: 4.39 us -> 0.25 us  [exchanged(): lax.ppermute(value, 'cin', [(i, i ^ k + 1) for i in range(parts)])]
    ppermute x6, waiting for transfers between devices: 1.43 us -> 4.85 us  [swap_planes(): return lax.ppermute(values, 'cin', links(lax.axis_size('cin'), odd))]
    ppermute x10, starting transfers between devices: 7.23 us -> 5.85 us  [swap_rows(): return lax.ppermute(values, 'cout', links(lax.axis_size('cout'), odd))]
    ppermute x6, starting transfers between devices: 7.62 us -> 8.67 us  [exchanged(): lax.ppermute(value, 'cin', [(i, i ^ k + 1) for i in range(parts)])]
    ppermute x10, waiting for transfers between devices: 1.56 us -> 0.81 us  [swap_rows(): return lax.ppermute(values, 'cout', links(lax.axis_size('cout'), odd))]
where the time goes in v5:
time: 59.3 us; the launch traced here: 59 us
  starting transfers between devices  29.8 us (50%)
  Pallas kernels  17.7 us (30%)
  waiting for transfers between devices  8.3 us (14%)
  local copies, waits for them, and re-layouts  2.34 us (4%)
  between operations  0.83 us (1%)
    pallas_call x13, Pallas kernels, call(): pl.pallas_call(kernel, name=name, in_specs=[SMEM] * scalars + [VMEM] * (l...  17.7 us
    ppermute x6, starting transfers between devices, swap_planes(): return lax.ppermute(values, 'cin', links(lax.axis_size('cin'), odd))  13.2 us
    ppermute x6, starting transfers between devices, exchanged(): lax.ppermute(value, 'cin', [(i, i ^ k + 1) for i in range(parts)])  8.67 us
    ppermute x10, starting transfers between devices, swap_rows(): return lax.ppermute(values, 'cout', links(lax.axis_size('cout'), odd))  5.85 us
    ppermute x6, waiting for transfers between devices, swap_planes(): return lax.ppermute(values, 'cin', links(lax.axis_size('cin'), odd))  4.85 us
    ppermute x2, waiting for transfers between devices, cross(): lax.ppermute(values, 'cout', [(i, i ^ 2) for i in range(lax.axis_size('co...  2.4 us
    unnamed x8, local copies, waits for them, and re-layouts  2.34 us
    ppermute x2, starting transfers between devices, cross(): lax.ppermute(values, 'cout', [(i, i ^ 2) for i in range(lax.axis_size('co...  2.11 us
  transfers between devices with their start and end apart: 24, of which 5 were waited for; matrix products, arithmetic and copies ran while one was open for 0% of the time, Pallas kernels for 28%

profile of v5, /device:TPU:0, one launch (start us, length us, event | category | flops | bytes accessed | tf_op | source)
XLA Modules:
  0.0 59.0 jit_solution(13659807083294209718)
XLA Ops:
  1.3 5.9 %collective-permute-start.1 = (bf16[128,1,4,256]{3,2,1,0:T(4,128)(2,1)}, bf16[128,1,4,256]{3,2,1,0:T(4,128)(2,1)S(1)}, u32[]{:S(2)}, u32[]{:S(2)}) collective-permute-start(bf16[128,1,4,256]{3,2,1,0:T(4,128)(2,1)} %own.2), channel_id=1, source_target_pairs={{0,4},{4,0},{8,12},{12,8},{1,5},{5,1},{9,13},{13,9},{2,6},{6,2},{1... | collective-permute-start | bytes 786440 | tf_op jit(solution)/shard_map/ppermute | solution.py:26
  7.9 1.8 %collective-permute-start.7 = (bf16[128,1,4,256]{3,2,1,0:T(4,128)(2,1)}, bf16[128,1,4,256]{3,2,1,0:T(4,128)(2,1)S(1)}, u32[]{:S(2)}, u32[]{:S(2)}) collective-permute-start(bf16[128,1,4,256]{3,2,1,0:T(4,128)(2,1)} %own.3), channel_id=1, source_target_pairs={{0,4},{4,0},{8,12},{12,8},{1,5},{5,1},{9,13},{13,9},{2,6},{6,2},{1... | collective-permute-start | bytes 786440 | tf_op jit(solution)/shard_map/ppermute | solution.py:26
  9.7 1.2 %copy-done = bf16[128,27,128]{2,0,1:T(8,128)(2,1)S(1)} copy-done((bf16[128,27,128]{2,0,1:T(8,128)(2,1)S(1)}, bf16[128,27,128]{2,0,1:T(8,128)(2,1)}, u32[]{:S(2)}) %copy-start) | copy-done | bytes 884760
  10.8 1.2 %copy-done.1 = bf16[128,27,128]{2,0,1:T(8,128)(2,1)S(1)} copy-done((bf16[128,27,128]{2,0,1:T(8,128)(2,1)S(1)}, bf16[128,27,128]{2,0,1:T(8,128)(2,1)}, u32[]{:S(2)}) %copy-start.1) | copy-done | bytes 884760
  12.6 2.0 %collective-permute-done.1.even = bf16[128,1,4,256]{3,2,1,0:T(4,128)(2,1)S(1)} collective-permute-done((bf16[128,1,4,256]{3,2,1,0:T(4,128)(2,1)}, bf16[128,1,4,256]{3,2,1,0:T(4,128)(2,1)S(1)}, u32[]{:S(2)}, u32[]{:S(2)}) %collective-permute-start.1) | collective-permute-done | bytes 262176 | tf_op jit(solution)/shard_map/ppermute | solution.py:26
  16.2 2.9 %collective-permute-done.7.even = bf16[128,1,4,256]{3,2,1,0:T(4,128)(2,1)S(1)} collective-permute-done((bf16[128,1,4,256]{3,2,1,0:T(4,128)(2,1)}, bf16[128,1,4,256]{3,2,1,0:T(4,128)(2,1)S(1)}, u32[]{:S(2)}, u32[]{:S(2)}) %collective-permute-start.7) | collective-permute-done | bytes 262176 | tf_op jit(solution)/shard_map/ppermute | solution.py:26
  19.1 0.8 %gather_cotangent.1 = (bf16[3,4,128,256]{3,2,1,0:T(8,128)(2,1)S(1)}, bf16[3,128,256]{2,1,0:T(8,128)(2,1)S(1)}, bf16[3,128,256]{2,1,0:T(8,128)(2,1)S(1)}) custom-call(s32[4]{0:T(128)S(1)} %pad_add_fusion.where, bf16[128,1,4,256]{3,2,1,0:T(4,128)(2,1)S(1)} %copy-done.3, bf16[128,1,4,256]{3,2,1,0:T(4,128)(2,1)S(1)} %collective-permute-done.6.odd, ...), custom_call_target="tpu_custom_call" | custom-call | bytes 1966096 | tf_op jit(solution)/shard_map/gather_cotangent/pallas_call | solution.py:307
  20.7 2.9 %collective-permute-start.10 = (bf16[3,4,128,256]{3,2,1,0:T(8,128)(2,1)S(1)}, bf16[3,4,128,256]{3,2,1,0:T(8,128)(2,1)S(1)}, u32[]{:S(2)}, u32[]{:S(2)}) collective-permute-start(bf16[3,4,128,256]{3,2,1,0:T(8,128)(2,1)S(1)} %get-tuple-element.47.refs_0_), channel_id=1, source_target_pairs={{0,1},{1,0},{2,3},{3,2},{4,5},{5,4},{6,7},{7,6},{8,9},{9,8},{10,11... | collective-permute-start | bytes 2359304 | tf_op jit(solution)/shard_map/ppermute | solution.py:30
  23.6 2.0 %first_conv.1 = (bf16[4,128,256]{2,1,0:T(8,128)(2,1)S(1)}, f32[4,128,256]{2,1,0:T(8,128)S(1)}, bf16[19,128,256]{2,1,0:T(8,128)(2,1)S(1)}) custom-call(s32[4]{0:T(128)S(1)} %pad_add_fusion.where, bf16[3,4,128,256]{3,2,1,0:T(8,128)(2,1)S(1)} %get-tuple-element.42.refs_0_, bf16[3,128,256]{2,1,0:T(8,128)(2,1)S(1)} %collective-permute-done.2.refs_1_, ...), custom_call_target="tpu_custom_call" | custom-call | flops 905969664 | bytes 4096016 | tf_op jit(solution)/shard_map/first_conv/pallas_call | solution.py:307
  26.3 3.5 %collective-permute-start.13 = (bf16[4,128,256]{2,1,0:T(8,128)(2,1)S(1)}, bf16[4,128,256]{2,1,0:T(8,128)(2,1)S(1)}, u32[]{:S(2)}, u32[]{:S(2)}) collective-permute-start(bf16[4,128,256]{2,1,0:T(8,128)(2,1)S(1)} %get-tuple-element.45.refs_4_.own), channel_id=1, source_target_pairs={{0,4},{4,0},{8,12},{12,8},{1,5},{5,1},{9,13},{13,9},{2,6},{6,2},{1... | collective-permute-start | bytes 786440 | tf_op jit(solution)/shard_map/ppermute | solution.py:26
  30.3 1.9 %hidden_grad.1 = (bf16[4,64,256]{2,1,0:T(8,128)(2,1)S(1)}, bf16[4,64,256]{2,1,0:T(8,128)(2,1)S(1)}) custom-call(s32[4]{0:T(128)S(1)} %pad_add_fusion.where, bf16[3,4,128,256]{3,2,1,0:T(8,128)(2,1)S(1)} %get-tuple-element.47.refs_0_, bf16[3,128,256]{2,1,0:T(8,128)(2,1)S(1)} %collective-permute-done.8.refs_1_, ...), custom_call_target="tpu_custom_call" | custom-call | flops 18119393280 | bytes 57016640 | tf_op jit(solution)/shard_map/hidden_grad/pallas_call | solution.py:307
  33.2 2.1 %second_filter_grad.1 = (bf16[9,32,384]{2,1,0:T(8,128)(2,1)S(1)}, f32[9,32,384]{2,1,0:T(8,128)S(1)}) custom-call(s32[4]{0:T(128)S(1)} %pad_add_fusion.where, bf16[3,4,128,256]{3,2,1,0:T(8,128)(2,1)S(1)} %get-tuple-element.47.refs_0_, bf16[3,4,128,256]{3,2,1,0:T(8,128)(2,1)S(1)} %collective-permute-done.10.refs_1_, ...), custom_call_target="tpu_custom_call" | custom-call | tf_op jit(solution)/shard_map/second_filter_grad/pallas_call | solution.py:307
  36.1 2.3 %first_filter_grad.1 = (bf16[3,32,1152]{2,1,0:T(8,128)(2,1)S(1)}, f32[3,32,1152]{2,1,0:T(8,128)S(1)}) custom-call(s32[4]{0:T(128)S(1)} %pad_add_fusion.where, bf16[3,4,128,256]{3,2,1,0:T(8,128)(2,1)S(1)} %get-tuple-element.42.refs_0_, bf16[3,128,256]{2,1,0:T(8,128)(2,1)S(1)} %collective-permute-done.3.refs_2_.refs_1_, ...), custom_call_target="tpu_custom_call" | custom-call | tf_op jit(solution)/shard_map/first_filter_grad/pallas_call | solution.py:307
  39.2 1.3 %collective-permute-start.16 = (bf16[3,32,1152]{2,1,0:T(8,128)(2,1)S(1)}, bf16[3,32,1152]{2,1,0:T(8,128)(2,1)S(1)}, u32[]{:S(2)}, u32[]{:S(2)}) collective-permute-start(bf16[3,32,1152]{2,1,0:T(8,128)(2,1)S(1)} %get-tuple-element.56), channel_id=1, source_target_pairs={{0,2},{1,3},{2,0},{3,1},{4,6},{5,7},{6,4},{7,5},{8,10},{9,11},{10,... | collective-permute-start | bytes 663560 | tf_op jit(solution)/shard_map/ppermute | solution.py:360
  41.2 2.4 %collective-permute-done.15.arrived = bf16[9,32,384]{2,1,0:T(8,128)(2,1)S(1)} collective-permute-done((bf16[9,32,384]{2,1,0:T(8,128)(2,1)S(1)}, bf16[9,32,384]{2,1,0:T(8,128)(2,1)S(1)}, u32[]{:S(2)}, u32[]{:S(2)}) %collective-permute-start.15) | collective-permute-done | bytes 221216 | tf_op jit(solution)/shard_map/ppermute | solution.py:360
  43.6 1.0 %pack_parts.2 = (bf16[7,32,128]{2,1,0:T(8,128)(2,1)S(1)}, bf16[7,32,128]{2,1,0:T(8,128)(2,1)S(1)}, bf16[7,32,128]{2,1,0:T(8,128)(2,1)S(1)}, f32[7,32,128]{2,1,0:T(8,128)S(1)}) custom-call(s32[4]{0:T(128)S(1)} %pad_add_fusion.where, f32[9,32,384]{2,1,0:T(8,128)S(1)} %get-tuple-element.61.held, bf16[9,32,384]{2,1,0:T(8,128)(2,1)S(1)} %collective-permute-done.15.arrived), custom_call_target="tpu_custom_call" | custom-call | bytes 950288 | tf_op jit(solution)/shard_map/pack_parts/pallas_call | solution.py:307
  44.6 2.5 %collective-permute-start.17 = (bf16[7,32,128]{2,1,0:T(8,128)(2,1)S(1)}, bf16[7,32,128]{2,1,0:T(8,128)(2,1)S(1)}, u32[]{:S(2)}, u32[]{:S(2)}) collective-permute-start(bf16[7,32,128]{2,1,0:T(8,128)(2,1)S(1)} %get-tuple-element.67), channel_id=1, source_target_pairs={{0,12},{4,8},{8,4},{12,0},{1,13},{5,9},{9,5},{13,1},{2,14},{6,10},... | collective-permute-start | bytes 172040 | tf_op jit(solution)/shard_map/ppermute | solution.py:343
  47.1 1.9 %collective-permute-start.19 = (bf16[7,32,128]{2,1,0:T(8,128)(2,1)S(1)}, bf16[7,32,128]{2,1,0:T(8,128)(2,1)S(1)}, u32[]{:S(2)}, u32[]{:S(2)}) collective-permute-start(bf16[7,32,128]{2,1,0:T(8,128)(2,1)S(1)} %get-tuple-element.69), channel_id=1, source_target_pairs={{0,4},{4,0},{8,12},{12,8},{1,5},{5,1},{9,13},{13,9},{2,6},{6,2},{1... | collective-permute-start | bytes 172040 | tf_op jit(solution)/shard_map/ppermute | solution.py:343
  49.1 1.0 %pack_parts.3 = (bf16[7,32,128]{2,1,0:T(8,128)(2,1)S(1)}, bf16[7,32,128]{2,1,0:T(8,128)(2,1)S(1)}, bf16[7,32,128]{2,1,0:T(8,128)(2,1)S(1)}, f32[7,32,128]{2,1,0:T(8,128)S(1)}) custom-call(s32[4]{0:T(128)S(1)} %pad_add_fusion.where, f32[3,32,1152]{2,1,0:T(8,128)S(1)} %get-tuple-element.64.held, bf16[3,32,1152]{2,1,0:T(8,128)(2,1)S(1)} %collective-permute-done.16.arrived), custom_call_target="tpu_custom_call" | custom-call | bytes 950288 | tf_op jit(solution)/shard_map/pack_parts/pallas_call | solution.py:307
  50.0 2.5 %collective-permute-start.21 = (bf16[7,32,128]{2,1,0:T(8,128)(2,1)S(1)}, bf16[7,32,128]{2,1,0:T(8,128)(2,1)S(1)}, u32[]{:S(2)}, u32[]{:S(2)}) collective-permute-start(bf16[7,32,128]{2,1,0:T(8,128)(2,1)S(1)} %get-tuple-element.74), channel_id=1, source_target_pairs={{0,12},{4,8},{8,4},{12,0},{1,13},{5,9},{9,5},{13,1},{2,14},{6,10},... | collective-permute-start | bytes 172040 | tf_op jit(solution)/shard_map/ppermute | solution.py:343
  52.8 1.7 %collective-permute-start.23 = (bf16[7,32,128]{2,1,0:T(8,128)(2,1)S(1)}, bf16[7,32,128]{2,1,0:T(8,128)(2,1)S(1)}, u32[]{:S(2)}, u32[]{:S(2)}) collective-permute-start(bf16[7,32,128]{2,1,0:T(8,128)(2,1)S(1)} %get-tuple-element.76), channel_id=1, source_target_pairs={{0,4},{4,0},{8,12},{12,8},{1,5},{5,1},{9,13},{13,9},{2,6},{6,2},{1... | collective-permute-start | bytes 172040 | tf_op jit(solution)/shard_map/ppermute | solution.py:343
  54.5 0.9 %finish_sum.2 = f32[27,32,32]{2,1,0:T(8,128)} custom-call(f32[7,32,128]{2,1,0:T(8,128)S(1)} %get-tuple-element.66.held, bf16[7,32,128]{2,1,0:T(8,128)(2,1)S(1)} %collective-permute-done.17.refs_0_, bf16[7,32,128]{2,1,0:T(8,128)(2,1)S(1)} %collective-permute-done.18.refs_1_, bf16[7,32,128]{2,1,0:T(8,128)(2,1)S(1)} %collective-permute-done.19.refs_2_), custom_call_target="tpu_custom_call" | custom-call | bytes 397312 | tf_op jit(solution)/shard_map/finish_sum/pallas_call | solution.py:307
  55.4 2.7 %second_conv.1 = bf16[128,1,4,256]{3,2,1,0:T(4,128)(2,1)} custom-call(s32[4]{0:T(128)S(1)} %pad_add_fusion.where, bf16[3,4,128,256]{3,2,1,0:T(8,128)(2,1)S(1)} %get-tuple-element.70.refs_0_, bf16[3,128,256]{2,1,0:T(8,128)(2,1)S(1)} %collective-permute-done.14.refs_1_, bf16[3,128,256]{2,1,0:T(8,128)(2,1)S(1)} %collective-permute-done.20.refs_2_, ...), custom_call_target="tpu_custom_call" | custom-call | flops 905969664 | bytes 2326544 | tf_op jit(solution)/shard_map/second_conv/pallas_call | solution.py:307
  58.1 0.9 %finish_sum.3 = f32[27,32,32]{2,1,0:T(8,128)} custom-call(f32[7,32,128]{2,1,0:T(8,128)S(1)} %get-tuple-element.73.held, bf16[7,32,128]{2,1,0:T(8,128)(2,1)S(1)} %collective-permute-done.21.refs_0_, bf16[7,32,128]{2,1,0:T(8,128)(2,1)S(1)} %collective-permute-done.22.refs_1_, bf16[7,32,128]{2,1,0:T(8,128)(2,1)S(1)} %collective-permute-done.23.refs_2_), custom_call_target="tpu_custom_call" | custom-call | bytes 397312 | tf_op jit(solution)/shard_map/finish_sum/pallas_call | solution.py:307
  (46 shorter events, 8.9 us)
Async XLA Ops:
  0.6 12.0 %collective-permute-start = (bf16[128,1,4,256]{3,2,1,0:T(4,128)(2,1)}, bf16[128,1,4,256]{3,2,1,0:T(4,128)(2,1)S(1)}, u32[]{:S(2)}, u32[]{:S(2)}) collective-permute-start(bf16[128,1,4,256]{3,2,1,0:T(4,128)(2,1)} %own.2), channel_id=1, source_target_pairs={{4,8},{8,4},{5,9},{9,5},{6,10},{10,6},{7,11},{11,7},{20,24},{24,20... | collective-permute-start | bytes 786440 | tf_op jit(solution)/shard_map/ppermute | solution.py:26
  1.3 13.3 %collective-permute-start.1 = (bf16[128,1,4,256]{3,2,1,0:T(4,128)(2,1)}, bf16[128,1,4,256]{3,2,1,0:T(4,128)(2,1)S(1)}, u32[]{:S(2)}, u32[]{:S(2)}) collective-permute-start(bf16[128,1,4,256]{3,2,1,0:T(4,128)(2,1)} %own.2), channel_id=1, source_target_pairs={{0,4},{4,0},{8,12},{12,8},{1,5},{5,1},{9,13},{13,9},{2,6},{6,2},{1... | collective-permute-start | bytes 786440 | tf_op jit(solution)/shard_map/ppermute | solution.py:26
  7.2 9.0 %collective-permute-start.6 = (bf16[128,1,4,256]{3,2,1,0:T(4,128)(2,1)}, bf16[128,1,4,256]{3,2,1,0:T(4,128)(2,1)S(1)}, u32[]{:S(2)}, u32[]{:S(2)}) collective-permute-start(bf16[128,1,4,256]{3,2,1,0:T(4,128)(2,1)} %own.3), channel_id=1, source_target_pairs={{4,8},{8,4},{5,9},{9,5},{6,10},{10,6},{7,11},{11,7},{20,24},{24,20... | collective-permute-start | bytes 786440 | tf_op jit(solution)/shard_map/ppermute | solution.py:26
  7.9 11.2 %collective-permute-start.7 = (bf16[128,1,4,256]{3,2,1,0:T(4,128)(2,1)}, bf16[128,1,4,256]{3,2,1,0:T(4,128)(2,1)S(1)}, u32[]{:S(2)}, u32[]{:S(2)}) collective-permute-start(bf16[128,1,4,256]{3,2,1,0:T(4,128)(2,1)} %own.3), channel_id=1, source_target_pairs={{0,4},{4,0},{8,12},{12,8},{1,5},{5,1},{9,13},{13,9},{2,6},{6,2},{1... | collective-permute-start | bytes 786440 | tf_op jit(solution)/shard_map/ppermute | solution.py:26
  15.4 8.1 %collective-permute-start.2 = (bf16[3,128,256]{2,1,0:T(8,128)(2,1)S(1)}, bf16[3,128,256]{2,1,0:T(8,128)(2,1)S(1)}, u32[]{:S(2)}, u32[]{:S(2)}) collective-permute-start(bf16[3,128,256]{2,1,0:T(8,128)(2,1)S(1)} %get-tuple-element.43), channel_id=1, source_target_pairs={{0,1},{1,0},{2,3},{3,2},{4,5},{5,4},{6,7},{7,6},{8,9},{9,8},{10,11... | collective-permute-start | bytes 589832 | tf_op jit(solution)/shard_map/ppermute | solution.py:30
  15.5 8.1 %collective-permute-start.3 = (bf16[3,128,256]{2,1,0:T(8,128)(2,1)S(1)}, bf16[3,128,256]{2,1,0:T(8,128)(2,1)S(1)}, u32[]{:S(2)}, u32[]{:S(2)}) collective-permute-start(bf16[3,128,256]{2,1,0:T(8,128)(2,1)S(1)} %get-tuple-element.44), channel_id=1, source_target_pairs={{1,2},{2,1},{5,6},{6,5},{9,10},{10,9},{13,14},{14,13},{17,18},{18,... | collective-permute-start | bytes 589832 | tf_op jit(solution)/shard_map/ppermute | solution.py:30
  19.9 9.9 %collective-permute-start.8 = (bf16[3,128,256]{2,1,0:T(8,128)(2,1)S(1)}, bf16[3,128,256]{2,1,0:T(8,128)(2,1)S(1)}, u32[]{:S(2)}, u32[]{:S(2)}) collective-permute-start(bf16[3,128,256]{2,1,0:T(8,128)(2,1)S(1)} %get-tuple-element.48), channel_id=1, source_target_pairs={{0,1},{1,0},{2,3},{3,2},{4,5},{5,4},{6,7},{7,6},{8,9},{9,8},{10,11... | collective-permute-start | bytes 589832 | tf_op jit(solution)/shard_map/ppermute | solution.py:30
  20.0 9.8 %collective-permute-start.9 = (bf16[3,128,256]{2,1,0:T(8,128)(2,1)S(1)}, bf16[3,128,256]{2,1,0:T(8,128)(2,1)S(1)}, u32[]{:S(2)}, u32[]{:S(2)}) collective-permute-start(bf16[3,128,256]{2,1,0:T(8,128)(2,1)S(1)} %get-tuple-element.49), channel_id=1, source_target_pairs={{1,2},{2,1},{5,6},{6,5},{9,10},{10,9},{13,14},{14,13},{17,18},{18,... | collective-permute-start | bytes 589832 | tf_op jit(solution)/shard_map/ppermute | solution.py:30
  20.7 12.5 %collective-permute-start.10 = (bf16[3,4,128,256]{3,2,1,0:T(8,128)(2,1)S(1)}, bf16[3,4,128,256]{3,2,1,0:T(8,128)(2,1)S(1)}, u32[]{:S(2)}, u32[]{:S(2)}) collective-permute-start(bf16[3,4,128,256]{3,2,1,0:T(8,128)(2,1)S(1)} %get-tuple-element.47.refs_0_), channel_id=1, source_target_pairs={{0,1},{1,0},{2,3},{3,2},{4,5},{5,4},{6,7},{7,6},{8,9},{9,8},{10,11... | collective-permute-start | bytes 2359304 | tf_op jit(solution)/shard_map/ppermute | solution.py:30
  25.6 12.8 %collective-permute-start.4 = (bf16[4,128,256]{2,1,0:T(8,128)(2,1)S(1)}, bf16[4,128,256]{2,1,0:T(8,128)(2,1)S(1)}, u32[]{:S(2)}, u32[]{:S(2)}) collective-permute-start(bf16[4,128,256]{2,1,0:T(8,128)(2,1)S(1)} %get-tuple-element.45.refs_4_.own), channel_id=1, source_target_pairs={{4,8},{8,4},{5,9},{9,5},{6,10},{10,6},{7,11},{11,7},{20,24},{24,20... | collective-permute-start | bytes 786440 | tf_op jit(solution)/shard_map/ppermute | solution.py:26
  26.3 12.2 %collective-permute-start.13 = (bf16[4,128,256]{2,1,0:T(8,128)(2,1)S(1)}, bf16[4,128,256]{2,1,0:T(8,128)(2,1)S(1)}, u32[]{:S(2)}, u32[]{:S(2)}) collective-permute-start(bf16[4,128,256]{2,1,0:T(8,128)(2,1)S(1)} %get-tuple-element.45.refs_4_.own), channel_id=1, source_target_pairs={{0,4},{4,0},{8,12},{12,8},{1,5},{5,1},{9,13},{13,9},{2,6},{6,2},{1... | collective-permute-start | bytes 786440 | tf_op jit(solution)/shard_map/ppermute | solution.py:26
  29.8 3.4 %collective-permute-start.5 = (bf16[19,128,256]{2,1,0:T(8,128)(2,1)S(1)}, bf16[19,128,256]{2,1,0:T(8,128)(2,1)S(1)}, u32[]{:S(2)}, u32[]{:S(2)}) collective-permute-start(bf16[19,128,256]{2,1,0:T(8,128)(2,1)S(1)} %get-tuple-element.46), channel_id=1, source_target_pairs={{0,1},{1,0},{2,3},{3,2},{4,5},{5,4},{6,7},{7,6},{8,9},{9,8},{10,11... | collective-permute-start | bytes 3735560 | tf_op jit(solution)/shard_map/ppermute | solution.py:30
  29.8 3.2 %collective-permute-start.11 = (bf16[3,128,256]{2,1,0:T(8,128)(2,1)S(1)}, bf16[3,128,256]{2,1,0:T(8,128)(2,1)S(1)}, u32[]{:S(2)}, u32[]{:S(2)}) collective-permute-start(bf16[3,128,256]{2,1,0:T(8,128)(2,1)S(1)} %collective-permute-done.9.refs_2_), channel_id=1, source_target_pairs={{0,1},{1,0},{2,3},{3,2},{4,5},{5,4},{6,7},{7,6},{8,9},{9,8},{10,11... | collective-permute-start | bytes 589832 | tf_op jit(solution)/shard_map/ppermute | solution.py:30
  33.0 3.1 %collective-permute-start.12 = (bf16[4,64,256]{2,1,0:T(8,128)(2,1)S(1)}, bf16[4,64,256]{2,1,0:T(8,128)(2,1)S(1)}, u32[]{:S(2)}, u32[]{:S(2)}) collective-permute-start(bf16[4,64,256]{2,1,0:T(8,128)(2,1)S(1)} %get-tuple-element.55), channel_id=1, source_target_pairs={{0,1},{1,0},{2,3},{3,2},{4,5},{5,4},{6,7},{7,6},{8,9},{9,8},{10,11... | collective-permute-start | bytes 393224 | tf_op jit(solution)/shard_map/ppermute | solution.py:30
  35.3 8.3 %collective-permute-start.15 = (bf16[9,32,384]{2,1,0:T(8,128)(2,1)S(1)}, bf16[9,32,384]{2,1,0:T(8,128)(2,1)S(1)}, u32[]{:S(2)}, u32[]{:S(2)}) collective-permute-start(bf16[9,32,384]{2,1,0:T(8,128)(2,1)S(1)} %get-tuple-element.53), channel_id=1, source_target_pairs={{0,2},{1,3},{2,0},{3,1},{4,6},{5,7},{6,4},{7,5},{8,10},{9,11},{10,... | collective-permute-start | bytes 663560 | tf_op jit(solution)/shard_map/ppermute | solution.py:360
  39.1 2.1 %collective-permute-start.14 = (bf16[3,128,256]{2,1,0:T(8,128)(2,1)S(1)}, bf16[3,128,256]{2,1,0:T(8,128)(2,1)S(1)}, u32[]{:S(2)}, u32[]{:S(2)}) collective-permute-start(bf16[3,128,256]{2,1,0:T(8,128)(2,1)S(1)} %get-tuple-element.60), channel_id=1, source_target_pairs={{0,1},{1,0},{2,3},{3,2},{4,5},{5,4},{6,7},{7,6},{8,9},{9,8},{10,11... | collective-permute-start | bytes 589832 | tf_op jit(solution)/shard_map/ppermute | solution.py:30
  39.2 9.8 %collective-permute-start.16 = (bf16[3,32,1152]{2,1,0:T(8,128)(2,1)S(1)}, bf16[3,32,1152]{2,1,0:T(8,128)(2,1)S(1)}, u32[]{:S(2)}, u32[]{:S(2)}) collective-permute-start(bf16[3,32,1152]{2,1,0:T(8,128)(2,1)S(1)} %get-tuple-element.56), channel_id=1, source_target_pairs={{0,2},{1,3},{2,0},{3,1},{4,6},{5,7},{6,4},{7,5},{8,10},{9,11},{10,... | collective-permute-start | bytes 663560 | tf_op jit(solution)/shard_map/ppermute | solution.py:360
  40.5 14.9 %collective-permute-start.20 = (bf16[3,128,256]{2,1,0:T(8,128)(2,1)S(1)}, bf16[3,128,256]{2,1,0:T(8,128)(2,1)S(1)}, u32[]{:S(2)}, u32[]{:S(2)}) collective-permute-start(bf16[3,128,256]{2,1,0:T(8,128)(2,1)S(1)} %get-tuple-element.71), channel_id=1, source_target_pairs={{1,2},{2,1},{5,6},{6,5},{9,10},{10,9},{13,14},{14,13},{17,18},{18,... | collective-permute-start | bytes 589832 | tf_op jit(solution)/shard_map/ppermute | solution.py:30
  44.6 8.0 %collective-permute-start.17 = (bf16[7,32,128]{2,1,0:T(8,128)(2,1)S(1)}, bf16[7,32,128]{2,1,0:T(8,128)(2,1)S(1)}, u32[]{:S(2)}, u32[]{:S(2)}) collective-permute-start(bf16[7,32,128]{2,1,0:T(8,128)(2,1)S(1)} %get-tuple-element.67), channel_id=1, source_target_pairs={{0,12},{4,8},{8,4},{12,0},{1,13},{5,9},{9,5},{13,1},{2,14},{6,10},... | collective-permute-start | bytes 172040 | tf_op jit(solution)/shard_map/ppermute | solution.py:343
  47.1 5.7 %collective-permute-start.18 = (bf16[7,32,128]{2,1,0:T(8,128)(2,1)S(1)}, bf16[7,32,128]{2,1,0:T(8,128)(2,1)S(1)}, u32[]{:S(2)}, u32[]{:S(2)}) collective-permute-start(bf16[7,32,128]{2,1,0:T(8,128)(2,1)S(1)} %get-tuple-element.68), channel_id=1, source_target_pairs={{0,8},{4,12},{8,0},{12,4},{1,9},{5,13},{9,1},{13,5},{2,10},{6,14},... | collective-permute-start | bytes 172040 | tf_op jit(solution)/shard_map/ppermute | solution.py:343
  47.1 7.4 %collective-permute-start.19 = (bf16[7,32,128]{2,1,0:T(8,128)(2,1)S(1)}, bf16[7,32,128]{2,1,0:T(8,128)(2,1)S(1)}, u32[]{:S(2)}, u32[]{:S(2)}) collective-permute-start(bf16[7,32,128]{2,1,0:T(8,128)(2,1)S(1)} %get-tuple-element.69), channel_id=1, source_target_pairs={{0,4},{4,0},{8,12},{12,8},{1,5},{5,1},{9,13},{13,9},{2,6},{6,2},{1... | collective-permute-start | bytes 172040 | tf_op jit(solution)/shard_map/ppermute | solution.py:343
  50.0 8.0 %collective-permute-start.21 = (bf16[7,32,128]{2,1,0:T(8,128)(2,1)S(1)}, bf16[7,32,128]{2,1,0:T(8,128)(2,1)S(1)}, u32[]{:S(2)}, u32[]{:S(2)}) collective-permute-start(bf16[7,32,128]{2,1,0:T(8,128)(2,1)S(1)} %get-tuple-element.74), channel_id=1, source_target_pairs={{0,12},{4,8},{8,4},{12,0},{1,13},{5,9},{9,5},{13,1},{2,14},{6,10},... | collective-permute-start | bytes 172040 | tf_op jit(solution)/shard_map/ppermute | solution.py:343
  52.6 5.5 %collective-permute-start.22 = (bf16[7,32,128]{2,1,0:T(8,128)(2,1)S(1)}, bf16[7,32,128]{2,1,0:T(8,128)(2,1)S(1)}, u32[]{:S(2)}, u32[]{:S(2)}) collective-permute-start(bf16[7,32,128]{2,1,0:T(8,128)(2,1)S(1)} %get-tuple-element.75), channel_id=1, source_target_pairs={{0,8},{4,12},{8,0},{12,4},{1,9},{5,13},{9,1},{13,5},{2,10},{6,14},... | collective-permute-start | bytes 172040 | tf_op jit(solution)/shard_map/ppermute | solution.py:343
  52.8 5.3 %collective-permute-start.23 = (bf16[7,32,128]{2,1,0:T(8,128)(2,1)S(1)}, bf16[7,32,128]{2,1,0:T(8,128)(2,1)S(1)}, u32[]{:S(2)}, u32[]{:S(2)}) collective-permute-start(bf16[7,32,128]{2,1,0:T(8,128)(2,1)S(1)} %get-tuple-element.76), channel_id=1, source_target_pairs={{0,4},{4,0},{8,12},{12,8},{1,5},{5,1},{9,13},{13,9},{2,6},{6,2},{1... | collective-permute-start | bytes 172040 | tf_op jit(solution)/shard_map/ppermute | solution.py:343
  (4 other events, 12.0 us)

commit v6 on v5

--- a/solution.py
+++ b/solution.py
@@ -113,7 +113,7 @@
         inside[plane] = stack[plane, (1 - where[1]) * (stack.shape[1] - 1)]
 
 
-def gather_hidden_kernel(where, own, odd, even, stack, across, inside):
+def gather_hidden_kernel(where, own, even, odd, stack, across, inside):
     last = own.shape[0] - 1
     for plane, slab in zip(planes_of(where), (own, odd, even)):
         stack[plane] = slab[...]
@@ -341,7 +341,7 @@
     parts = lax.axis_size("cin")
     return [
         lax.ppermute(value, "cin", [(i, i ^ (k + 1)) for i in range(parts)])
-        for k, value in reversed(list(enumerate(sends)))
+        for k, value in [(k, sends[k]) for k in (2, 0, 1)]
     ]
 
 
@@ -430,9 +430,9 @@
     )
     shape = (outs // row_count, taps, ins // plane_count)
 
-    def hidden_rows(odd, even):
+    def hidden_rows(even, odd):
         own, across, inside = call(
-            gather_hidden_kernel, "gather_hidden", [stack, edge, edge], (where, hidden, odd, even)
+            gather_hidden_kernel, "gather_hidden", [stack, edge, edge], (where, hidden, even, odd)
         )
         return own, swap_rows(inside, 0), swap_rows(across, 1)
 
@@ -493,7 +493,7 @@
             busy=0,
         )
         first_arrived = cross(first_send)
-        hidden_slabs = hidden_rows(after(hidden_odd, first_send), hidden_even)
+        hidden_slabs = hidden_rows(after(hidden_even, first_send), hidden_odd)
         steps = range(3)
         second_taps = [26 - (a * 9 + b * 3 + e) for b in steps for a in steps for e in steps]
         first_taps = [a * 9 + b * 3 + e for e in steps for b in steps for a in steps]
@@ -513,7 +513,7 @@
             after(first_keep, second_out), first_parts, first_taps, factor, shape
         )
     else:
-        second_out = convolved(*hidden_rows(hidden_odd, hidden_even))
+        second_out = convolved(*hidden_rows(hidden_even, hidden_odd))
         (second_total,) = call(
             second_total_kernel,
             "second_filter_grad",

time: 59.3 us -> 58.1 us (0.980)
  starting transfers between devices: 29.8 us -> 28.4 us
    ppermute x6, starting transfers between devices: 13.2 us -> 11.5 us  [swap_planes(): return lax.ppermute(values, 'cin', links(lax.axis_size('cin'), odd))]
  transfers between devices with their start and end apart: 24 -> 24, of which waited for: 5 -> 6; matrix products, arithmetic and copies ran while one was open for 0% -> 0% of each run, Pallas kernels for 28% -> 29%
where the time goes in v6:
time: 58.1 us; the launch traced here: 57.7 us
  starting transfers between devices  28.4 us (49%)
  Pallas kernels  17.7 us (30%)
  waiting for transfers between devices  8.43 us (15%)
  local copies, waits for them, and re-layouts  2.34 us (4%)
  between operations  0.84 us (1%)
    pallas_call x13, Pallas kernels, call(): pl.pallas_call(kernel, name=name, in_specs=[SMEM] * scalars + [VMEM] * (l...  17.7 us
    ppermute x6, starting transfers between devices, swap_planes(): return lax.ppermute(values, 'cin', links(lax.axis_size('cin'), odd))  11.5 us
    ppermute x6, starting transfers between devices, exchanged(): lax.ppermute(value, 'cin', [(i, i ^ k + 1) for i in range(parts)])  8.91 us
    ppermute x10, starting transfers between devices, swap_rows(): return lax.ppermute(values, 'cout', links(lax.axis_size('cout'), odd))  5.9 us
    ppermute x6, waiting for transfers between devices, swap_planes(): return lax.ppermute(values, 'cin', links(lax.axis_size('cin'), odd))  4.85 us
    ppermute x2, waiting for transfers between devices, cross(): lax.ppermute(values, 'cout', [(i, i ^ 2) for i in range(lax.axis_size('co...  2.4 us
    unnamed x8, local copies, waits for them, and re-layouts  2.34 us
    ppermute x2, starting transfers between devices, cross(): lax.ppermute(values, 'cout', [(i, i ^ 2) for i in range(lax.axis_size('co...  2.1 us
  transfers between devices with their start and end apart: 24, of which 6 were waited for; matrix products, arithmetic and copies ran while one was open for 0% of the time, Pallas kernels for 29%

profile of v6, /device:TPU:0, one launch (start us, length us, event | category | flops | bytes accessed | tf_op | source)
XLA Modules:
  0.0 57.7 jit_solution(5917663772088394414)
XLA Ops:
  1.3 5.9 %collective-permute-start.1 = (bf16[128,1,4,256]{3,2,1,0:T(4,128)(2,1)}, bf16[128,1,4,256]{3,2,1,0:T(4,128)(2,1)S(1)}, u32[]{:S(2)}, u32[]{:S(2)}) collective-permute-start(bf16[128,1,4,256]{3,2,1,0:T(4,128)(2,1)} %own.2), channel_id=1, source_target_pairs={{0,4},{4,0},{8,12},{12,8},{1,5},{5,1},{9,13},{13,9},{2,6},{6,2},{1... | collective-permute-start | bytes 786440 | tf_op jit(solution)/shard_map/ppermute | solution.py:26
  7.9 1.8 %collective-permute-start.7 = (bf16[128,1,4,256]{3,2,1,0:T(4,128)(2,1)}, bf16[128,1,4,256]{3,2,1,0:T(4,128)(2,1)S(1)}, u32[]{:S(2)}, u32[]{:S(2)}) collective-permute-start(bf16[128,1,4,256]{3,2,1,0:T(4,128)(2,1)} %own.3), channel_id=1, source_target_pairs={{0,4},{4,0},{8,12},{12,8},{1,5},{5,1},{9,13},{13,9},{2,6},{6,2},{1... | collective-permute-start | bytes 786440 | tf_op jit(solution)/shard_map/ppermute | solution.py:26
  9.7 1.2 %copy-done = bf16[128,27,128]{2,0,1:T(8,128)(2,1)S(1)} copy-done((bf16[128,27,128]{2,0,1:T(8,128)(2,1)S(1)}, bf16[128,27,128]{2,0,1:T(8,128)(2,1)}, u32[]{:S(2)}) %copy-start) | copy-done | bytes 884760
  10.8 1.2 %copy-done.1 = bf16[128,27,128]{2,0,1:T(8,128)(2,1)S(1)} copy-done((bf16[128,27,128]{2,0,1:T(8,128)(2,1)S(1)}, bf16[128,27,128]{2,0,1:T(8,128)(2,1)}, u32[]{:S(2)}) %copy-start.1) | copy-done | bytes 884760
  12.6 2.0 %collective-permute-done.1.even = bf16[128,1,4,256]{3,2,1,0:T(4,128)(2,1)S(1)} collective-permute-done((bf16[128,1,4,256]{3,2,1,0:T(4,128)(2,1)}, bf16[128,1,4,256]{3,2,1,0:T(4,128)(2,1)S(1)}, u32[]{:S(2)}, u32[]{:S(2)}) %collective-permute-start.1) | collective-permute-done | bytes 262176 | tf_op jit(solution)/shard_map/ppermute | solution.py:26
  16.2 2.9 %collective-permute-done.7.even = bf16[128,1,4,256]{3,2,1,0:T(4,128)(2,1)S(1)} collective-permute-done((bf16[128,1,4,256]{3,2,1,0:T(4,128)(2,1)}, bf16[128,1,4,256]{3,2,1,0:T(4,128)(2,1)S(1)}, u32[]{:S(2)}, u32[]{:S(2)}) %collective-permute-start.7) | collective-permute-done | bytes 262176 | tf_op jit(solution)/shard_map/ppermute | solution.py:26
  20.7 2.9 %collective-permute-start.10 = (bf16[3,4,128,256]{3,2,1,0:T(8,128)(2,1)S(1)}, bf16[3,4,128,256]{3,2,1,0:T(8,128)(2,1)S(1)}, u32[]{:S(2)}, u32[]{:S(2)}) collective-permute-start(bf16[3,4,128,256]{3,2,1,0:T(8,128)(2,1)S(1)} %get-tuple-element.47.refs_0_), channel_id=1, source_target_pairs={{0,1},{1,0},{2,3},{3,2},{4,5},{5,4},{6,7},{7,6},{8,9},{9,8},{10,11... | collective-permute-start | bytes 2359304 | tf_op jit(solution)/shard_map/ppermute | solution.py:30
  23.6 2.0 %first_conv.1 = (bf16[4,128,256]{2,1,0:T(8,128)(2,1)S(1)}, f32[4,128,256]{2,1,0:T(8,128)S(1)}, bf16[19,128,256]{2,1,0:T(8,128)(2,1)S(1)}) custom-call(s32[4]{0:T(128)S(1)} %pad_add_fusion.where, bf16[3,4,128,256]{3,2,1,0:T(8,128)(2,1)S(1)} %get-tuple-element.42.refs_0_, bf16[3,128,256]{2,1,0:T(8,128)(2,1)S(1)} %collective-permute-done.2.refs_1_, ...), custom_call_target="tpu_custom_call" | custom-call | flops 905969664 | bytes 4096016 | tf_op jit(solution)/shard_map/first_conv/pallas_call | solution.py:307
  25.6 1.8 %collective-permute-start.4 = (bf16[4,128,256]{2,1,0:T(8,128)(2,1)S(1)}, bf16[4,128,256]{2,1,0:T(8,128)(2,1)S(1)}, u32[]{:S(2)}, u32[]{:S(2)}) collective-permute-start(bf16[4,128,256]{2,1,0:T(8,128)(2,1)S(1)} %get-tuple-element.45.refs_4_.own), channel_id=1, source_target_pairs={{0,4},{4,0},{8,12},{12,8},{1,5},{5,1},{9,13},{13,9},{2,6},{6,2},{1... | collective-permute-start | bytes 786440 | tf_op jit(solution)/shard_map/ppermute | solution.py:26
  28.7 1.9 %hidden_grad.1 = (bf16[4,64,256]{2,1,0:T(8,128)(2,1)S(1)}, bf16[4,64,256]{2,1,0:T(8,128)(2,1)S(1)}) custom-call(s32[4]{0:T(128)S(1)} %pad_add_fusion.where, bf16[3,4,128,256]{3,2,1,0:T(8,128)(2,1)S(1)} %get-tuple-element.47.refs_0_, bf16[3,128,256]{2,1,0:T(8,128)(2,1)S(1)} %collective-permute-done.8.refs_1_, ...), custom_call_target="tpu_custom_call" | custom-call | flops 18119393280 | bytes 57016640 | tf_op jit(solution)/shard_map/hidden_grad/pallas_call | solution.py:307
  31.5 2.1 %second_filter_grad.1 = (bf16[9,32,384]{2,1,0:T(8,128)(2,1)S(1)}, f32[9,32,384]{2,1,0:T(8,128)S(1)}) custom-call(s32[4]{0:T(128)S(1)} %pad_add_fusion.where, bf16[3,4,128,256]{3,2,1,0:T(8,128)(2,1)S(1)} %get-tuple-element.47.refs_0_, bf16[3,4,128,256]{3,2,1,0:T(8,128)(2,1)S(1)} %collective-permute-done.10.refs_1_, ...), custom_call_target="tpu_custom_call" | custom-call | tf_op jit(solution)/shard_map/second_filter_grad/pallas_call | solution.py:307
  34.5 2.3 %first_filter_grad.1 = (bf16[3,32,1152]{2,1,0:T(8,128)(2,1)S(1)}, f32[3,32,1152]{2,1,0:T(8,128)S(1)}) custom-call(s32[4]{0:T(128)S(1)} %pad_add_fusion.where, bf16[3,4,128,256]{3,2,1,0:T(8,128)(2,1)S(1)} %get-tuple-element.42.refs_0_, bf16[3,128,256]{2,1,0:T(8,128)(2,1)S(1)} %collective-permute-done.3.refs_2_.refs_1_, ...), custom_call_target="tpu_custom_call" | custom-call | tf_op jit(solution)/shard_map/first_filter_grad/pallas_call | solution.py:307
  37.6 1.3 %collective-permute-start.16 = (bf16[3,32,1152]{2,1,0:T(8,128)(2,1)S(1)}, bf16[3,32,1152]{2,1,0:T(8,128)(2,1)S(1)}, u32[]{:S(2)}, u32[]{:S(2)}) collective-permute-start(bf16[3,32,1152]{2,1,0:T(8,128)(2,1)S(1)} %get-tuple-element.56), channel_id=1, source_target_pairs={{0,2},{1,3},{2,0},{3,1},{4,6},{5,7},{6,4},{7,5},{8,10},{9,11},{10,... | collective-permute-start | bytes 663560 | tf_op jit(solution)/shard_map/ppermute | solution.py:360
  39.6 2.4 %collective-permute-done.15.arrived = bf16[9,32,384]{2,1,0:T(8,128)(2,1)S(1)} collective-permute-done((bf16[9,32,384]{2,1,0:T(8,128)(2,1)S(1)}, bf16[9,32,384]{2,1,0:T(8,128)(2,1)S(1)}, u32[]{:S(2)}, u32[]{:S(2)}) %collective-permute-start.15) | collective-permute-done | bytes 221216 | tf_op jit(solution)/shard_map/ppermute | solution.py:360
  42.0 1.0 %pack_parts.2 = (bf16[7,32,128]{2,1,0:T(8,128)(2,1)S(1)}, bf16[7,32,128]{2,1,0:T(8,128)(2,1)S(1)}, bf16[7,32,128]{2,1,0:T(8,128)(2,1)S(1)}, f32[7,32,128]{2,1,0:T(8,128)S(1)}) custom-call(s32[4]{0:T(128)S(1)} %pad_add_fusion.where, f32[9,32,384]{2,1,0:T(8,128)S(1)} %get-tuple-element.61.held, bf16[9,32,384]{2,1,0:T(8,128)(2,1)S(1)} %collective-permute-done.15.arrived), custom_call_target="tpu_custom_call" | custom-call | bytes 950288 | tf_op jit(solution)/shard_map/pack_parts/pallas_call | solution.py:307
  43.0 1.4 %collective-permute-start.17 = (bf16[7,32,128]{2,1,0:T(8,128)(2,1)S(1)}, bf16[7,32,128]{2,1,0:T(8,128)(2,1)S(1)}, u32[]{:S(2)}, u32[]{:S(2)}) collective-permute-start(bf16[7,32,128]{2,1,0:T(8,128)(2,1)S(1)} %get-tuple-element.67), channel_id=1, source_target_pairs={{0,12},{4,8},{8,4},{12,0},{1,13},{5,9},{9,5},{13,1},{2,14},{6,10},... | collective-permute-start | bytes 172040 | tf_op jit(solution)/shard_map/ppermute | solution.py:343
  44.4 2.2 %collective-permute-start.18 = (bf16[7,32,128]{2,1,0:T(8,128)(2,1)S(1)}, bf16[7,32,128]{2,1,0:T(8,128)(2,1)S(1)}, u32[]{:S(2)}, u32[]{:S(2)}) collective-permute-start(bf16[7,32,128]{2,1,0:T(8,128)(2,1)S(1)} %get-tuple-element.68), channel_id=1, source_target_pairs={{0,4},{4,0},{8,12},{12,8},{1,5},{5,1},{9,13},{13,9},{2,6},{6,2},{1... | collective-permute-start | bytes 172040 | tf_op jit(solution)/shard_map/ppermute | solution.py:343
  47.4 1.0 %pack_parts.3 = (bf16[7,32,128]{2,1,0:T(8,128)(2,1)S(1)}, bf16[7,32,128]{2,1,0:T(8,128)(2,1)S(1)}, bf16[7,32,128]{2,1,0:T(8,128)(2,1)S(1)}, f32[7,32,128]{2,1,0:T(8,128)S(1)}) custom-call(s32[4]{0:T(128)S(1)} %pad_add_fusion.where, f32[3,32,1152]{2,1,0:T(8,128)S(1)} %get-tuple-element.64.held, bf16[3,32,1152]{2,1,0:T(8,128)(2,1)S(1)} %collective-permute-done.16.arrived), custom_call_target="tpu_custom_call" | custom-call | bytes 950288 | tf_op jit(solution)/shard_map/pack_parts/pallas_call | solution.py:307
  48.4 1.6 %collective-permute-start.21 = (bf16[7,32,128]{2,1,0:T(8,128)(2,1)S(1)}, bf16[7,32,128]{2,1,0:T(8,128)(2,1)S(1)}, u32[]{:S(2)}, u32[]{:S(2)}) collective-permute-start(bf16[7,32,128]{2,1,0:T(8,128)(2,1)S(1)} %get-tuple-element.74), channel_id=1, source_target_pairs={{0,12},{4,8},{8,4},{12,0},{1,13},{5,9},{9,5},{13,1},{2,14},{6,10},... | collective-permute-start | bytes 172040 | tf_op jit(solution)/shard_map/ppermute | solution.py:343
  50.0 1.1 %collective-permute-start.22 = (bf16[7,32,128]{2,1,0:T(8,128)(2,1)S(1)}, bf16[7,32,128]{2,1,0:T(8,128)(2,1)S(1)}, u32[]{:S(2)}, u32[]{:S(2)}) collective-permute-start(bf16[7,32,128]{2,1,0:T(8,128)(2,1)S(1)} %get-tuple-element.75), channel_id=1, source_target_pairs={{0,4},{4,0},{8,12},{12,8},{1,5},{5,1},{9,13},{13,9},{2,6},{6,2},{1... | collective-permute-start | bytes 172040 | tf_op jit(solution)/shard_map/ppermute | solution.py:343
  51.1 1.7 %collective-permute-start.23 = (bf16[7,32,128]{2,1,0:T(8,128)(2,1)S(1)}, bf16[7,32,128]{2,1,0:T(8,128)(2,1)S(1)}, u32[]{:S(2)}, u32[]{:S(2)}) collective-permute-start(bf16[7,32,128]{2,1,0:T(8,128)(2,1)S(1)} %get-tuple-element.76), channel_id=1, source_target_pairs={{0,8},{4,12},{8,0},{12,4},{1,9},{5,13},{9,1},{13,5},{2,10},{6,14},... | collective-permute-start | bytes 172040 | tf_op jit(solution)/shard_map/ppermute | solution.py:343
  52.9 0.9 %finish_sum.2 = f32[27,32,32]{2,1,0:T(8,128)} custom-call(f32[7,32,128]{2,1,0:T(8,128)S(1)} %get-tuple-element.66.held, bf16[7,32,128]{2,1,0:T(8,128)(2,1)S(1)} %collective-permute-done.17.refs_0_, bf16[7,32,128]{2,1,0:T(8,128)(2,1)S(1)} %collective-permute-done.18.refs_1_, bf16[7,32,128]{2,1,0:T(8,128)(2,1)S(1)} %collective-permute-done.19.refs_2_), custom_call_target="tpu_custom_call" | custom-call | bytes 397312 | tf_op jit(solution)/shard_map/finish_sum/pallas_call | solution.py:307
  53.9 2.7 %second_conv.1 = bf16[128,1,4,256]{3,2,1,0:T(4,128)(2,1)} custom-call(s32[4]{0:T(128)S(1)} %pad_add_fusion.where, bf16[3,4,128,256]{3,2,1,0:T(8,128)(2,1)S(1)} %get-tuple-element.70.refs_0_, bf16[3,128,256]{2,1,0:T(8,128)(2,1)S(1)} %collective-permute-done.14.refs_1_, bf16[3,128,256]{2,1,0:T(8,128)(2,1)S(1)} %collective-permute-done.20.refs_2_, ...), custom_call_target="tpu_custom_call" | custom-call | flops 905969664 | bytes 2326544 | tf_op jit(solution)/shard_map/second_conv/pallas_call | solution.py:307
  56.8 0.9 %finish_sum.3 = f32[27,32,32]{2,1,0:T(8,128)} custom-call(f32[7,32,128]{2,1,0:T(8,128)S(1)} %get-tuple-element.73.held, bf16[7,32,128]{2,1,0:T(8,128)(2,1)S(1)} %collective-permute-done.21.refs_0_, bf16[7,32,128]{2,1,0:T(8,128)(2,1)S(1)} %collective-permute-done.22.refs_1_, bf16[7,32,128]{2,1,0:T(8,128)(2,1)S(1)} %collective-permute-done.23.refs_2_), custom_call_target="tpu_custom_call" | custom-call | bytes 397312 | tf_op jit(solution)/shard_map/finish_sum/pallas_call | solution.py:307
  (46 shorter events, 10.8 us)
Async XLA Ops:
  0.6 12.0 %collective-permute-start = (bf16[128,1,4,256]{3,2,1,0:T(4,128)(2,1)}, bf16[128,1,4,256]{3,2,1,0:T(4,128)(2,1)S(1)}, u32[]{:S(2)}, u32[]{:S(2)}) collective-permute-start(bf16[128,1,4,256]{3,2,1,0:T(4,128)(2,1)} %own.2), channel_id=1, source_target_pairs={{4,8},{8,4},{5,9},{9,5},{6,10},{10,6},{7,11},{11,7},{20,24},{24,20... | collective-permute-start | bytes 786440 | tf_op jit(solution)/shard_map/ppermute | solution.py:26
  1.3 13.3 %collective-permute-start.1 = (bf16[128,1,4,256]{3,2,1,0:T(4,128)(2,1)}, bf16[128,1,4,256]{3,2,1,0:T(4,128)(2,1)S(1)}, u32[]{:S(2)}, u32[]{:S(2)}) collective-permute-start(bf16[128,1,4,256]{3,2,1,0:T(4,128)(2,1)} %own.2), channel_id=1, source_target_pairs={{0,4},{4,0},{8,12},{12,8},{1,5},{5,1},{9,13},{13,9},{2,6},{6,2},{1... | collective-permute-start | bytes 786440 | tf_op jit(solution)/shard_map/ppermute | solution.py:26
  7.2 9.0 %collective-permute-start.6 = (bf16[128,1,4,256]{3,2,1,0:T(4,128)(2,1)}, bf16[128,1,4,256]{3,2,1,0:T(4,128)(2,1)S(1)}, u32[]{:S(2)}, u32[]{:S(2)}) collective-permute-start(bf16[128,1,4,256]{3,2,1,0:T(4,128)(2,1)} %own.3), channel_id=1, source_target_pairs={{4,8},{8,4},{5,9},{9,5},{6,10},{10,6},{7,11},{11,7},{20,24},{24,20... | collective-permute-start | bytes 786440 | tf_op jit(solution)/shard_map/ppermute | solution.py:26
  7.9 11.2 %collective-permute-start.7 = (bf16[128,1,4,256]{3,2,1,0:T(4,128)(2,1)}, bf16[128,1,4,256]{3,2,1,0:T(4,128)(2,1)S(1)}, u32[]{:S(2)}, u32[]{:S(2)}) collective-permute-start(bf16[128,1,4,256]{3,2,1,0:T(4,128)(2,1)} %own.3), channel_id=1, source_target_pairs={{0,4},{4,0},{8,12},{12,8},{1,5},{5,1},{9,13},{13,9},{2,6},{6,2},{1... | collective-permute-start | bytes 786440 | tf_op jit(solution)/shard_map/ppermute | solution.py:26
  15.4 8.1 %collective-permute-start.2 = (bf16[3,128,256]{2,1,0:T(8,128)(2,1)S(1)}, bf16[3,128,256]{2,1,0:T(8,128)(2,1)S(1)}, u32[]{:S(2)}, u32[]{:S(2)}) collective-permute-start(bf16[3,128,256]{2,1,0:T(8,128)(2,1)S(1)} %get-tuple-element.43), channel_id=1, source_target_pairs={{0,1},{1,0},{2,3},{3,2},{4,5},{5,4},{6,7},{7,6},{8,9},{9,8},{10,11... | collective-permute-start | bytes 589832 | tf_op jit(solution)/shard_map/ppermute | solution.py:30
  15.5 8.1 %collective-permute-start.3 = (bf16[3,128,256]{2,1,0:T(8,128)(2,1)S(1)}, bf16[3,128,256]{2,1,0:T(8,128)(2,1)S(1)}, u32[]{:S(2)}, u32[]{:S(2)}) collective-permute-start(bf16[3,128,256]{2,1,0:T(8,128)(2,1)S(1)} %get-tuple-element.44), channel_id=1, source_target_pairs={{1,2},{2,1},{5,6},{6,5},{9,10},{10,9},{13,14},{14,13},{17,18},{18,... | collective-permute-start | bytes 589832 | tf_op jit(solution)/shard_map/ppermute | solution.py:30
  19.9 8.2 %collective-permute-start.8 = (bf16[3,128,256]{2,1,0:T(8,128)(2,1)S(1)}, bf16[3,128,256]{2,1,0:T(8,128)(2,1)S(1)}, u32[]{:S(2)}, u32[]{:S(2)}) collective-permute-start(bf16[3,128,256]{2,1,0:T(8,128)(2,1)S(1)} %get-tuple-element.48), channel_id=1, source_target_pairs={{0,1},{1,0},{2,3},{3,2},{4,5},{5,4},{6,7},{7,6},{8,9},{9,8},{10,11... | collective-permute-start | bytes 589832 | tf_op jit(solution)/shard_map/ppermute | solution.py:30
  20.0 8.2 %collective-permute-start.9 = (bf16[3,128,256]{2,1,0:T(8,128)(2,1)S(1)}, bf16[3,128,256]{2,1,0:T(8,128)(2,1)S(1)}, u32[]{:S(2)}, u32[]{:S(2)}) collective-permute-start(bf16[3,128,256]{2,1,0:T(8,128)(2,1)S(1)} %get-tuple-element.49), channel_id=1, source_target_pairs={{1,2},{2,1},{5,6},{6,5},{9,10},{10,9},{13,14},{14,13},{17,18},{18,... | collective-permute-start | bytes 589832 | tf_op jit(solution)/shard_map/ppermute | solution.py:30
  20.7 10.9 %collective-permute-start.10 = (bf16[3,4,128,256]{3,2,1,0:T(8,128)(2,1)S(1)}, bf16[3,4,128,256]{3,2,1,0:T(8,128)(2,1)S(1)}, u32[]{:S(2)}, u32[]{:S(2)}) collective-permute-start(bf16[3,4,128,256]{3,2,1,0:T(8,128)(2,1)S(1)} %get-tuple-element.47.refs_0_), channel_id=1, source_target_pairs={{0,1},{1,0},{2,3},{3,2},{4,5},{5,4},{6,7},{7,6},{8,9},{9,8},{10,11... | collective-permute-start | bytes 2359304 | tf_op jit(solution)/shard_map/ppermute | solution.py:30
  25.6 11.2 %collective-permute-start.4 = (bf16[4,128,256]{2,1,0:T(8,128)(2,1)S(1)}, bf16[4,128,256]{2,1,0:T(8,128)(2,1)S(1)}, u32[]{:S(2)}, u32[]{:S(2)}) collective-permute-start(bf16[4,128,256]{2,1,0:T(8,128)(2,1)S(1)} %get-tuple-element.45.refs_4_.own), channel_id=1, source_target_pairs={{0,4},{4,0},{8,12},{12,8},{1,5},{5,1},{9,13},{13,9},{2,6},{6,2},{1... | collective-permute-start | bytes 786440 | tf_op jit(solution)/shard_map/ppermute | solution.py:26
  27.4 9.4 %collective-permute-start.13 = (bf16[4,128,256]{2,1,0:T(8,128)(2,1)S(1)}, bf16[4,128,256]{2,1,0:T(8,128)(2,1)S(1)}, u32[]{:S(2)}, u32[]{:S(2)}) collective-permute-start(bf16[4,128,256]{2,1,0:T(8,128)(2,1)S(1)} %get-tuple-element.45.refs_4_.own), channel_id=1, source_target_pairs={{4,8},{8,4},{5,9},{9,5},{6,10},{10,6},{7,11},{11,7},{20,24},{24,20... | collective-permute-start | bytes 786440 | tf_op jit(solution)/shard_map/ppermute | solution.py:26
  28.1 3.4 %collective-permute-start.5 = (bf16[19,128,256]{2,1,0:T(8,128)(2,1)S(1)}, bf16[19,128,256]{2,1,0:T(8,128)(2,1)S(1)}, u32[]{:S(2)}, u32[]{:S(2)}) collective-permute-start(bf16[19,128,256]{2,1,0:T(8,128)(2,1)S(1)} %get-tuple-element.46), channel_id=1, source_target_pairs={{0,1},{1,0},{2,3},{3,2},{4,5},{5,4},{6,7},{7,6},{8,9},{9,8},{10,11... | collective-permute-start | bytes 3735560 | tf_op jit(solution)/shard_map/ppermute | solution.py:30
  28.2 3.2 %collective-permute-start.11 = (bf16[3,128,256]{2,1,0:T(8,128)(2,1)S(1)}, bf16[3,128,256]{2,1,0:T(8,128)(2,1)S(1)}, u32[]{:S(2)}, u32[]{:S(2)}) collective-permute-start(bf16[3,128,256]{2,1,0:T(8,128)(2,1)S(1)} %collective-permute-done.9.refs_2_), channel_id=1, source_target_pairs={{0,1},{1,0},{2,3},{3,2},{4,5},{5,4},{6,7},{7,6},{8,9},{9,8},{10,11... | collective-permute-start | bytes 589832 | tf_op jit(solution)/shard_map/ppermute | solution.py:30
  31.4 3.1 %collective-permute-start.12 = (bf16[4,64,256]{2,1,0:T(8,128)(2,1)S(1)}, bf16[4,64,256]{2,1,0:T(8,128)(2,1)S(1)}, u32[]{:S(2)}, u32[]{:S(2)}) collective-permute-start(bf16[4,64,256]{2,1,0:T(8,128)(2,1)S(1)} %get-tuple-element.55), channel_id=1, source_target_pairs={{0,1},{1,0},{2,3},{3,2},{4,5},{5,4},{6,7},{7,6},{8,9},{9,8},{10,11... | collective-permute-start | bytes 393224 | tf_op jit(solution)/shard_map/ppermute | solution.py:30
  33.7 8.3 %collective-permute-start.15 = (bf16[9,32,384]{2,1,0:T(8,128)(2,1)S(1)}, bf16[9,32,384]{2,1,0:T(8,128)(2,1)S(1)}, u32[]{:S(2)}, u32[]{:S(2)}) collective-permute-start(bf16[9,32,384]{2,1,0:T(8,128)(2,1)S(1)} %get-tuple-element.53), channel_id=1, source_target_pairs={{0,2},{1,3},{2,0},{3,1},{4,6},{5,7},{6,4},{7,5},{8,10},{9,11},{10,... | collective-permute-start | bytes 663560 | tf_op jit(solution)/shard_map/ppermute | solution.py:360
  37.5 2.1 %collective-permute-start.14 = (bf16[3,128,256]{2,1,0:T(8,128)(2,1)S(1)}, bf16[3,128,256]{2,1,0:T(8,128)(2,1)S(1)}, u32[]{:S(2)}, u32[]{:S(2)}) collective-permute-start(bf16[3,128,256]{2,1,0:T(8,128)(2,1)S(1)} %get-tuple-element.60), channel_id=1, source_target_pairs={{0,1},{1,0},{2,3},{3,2},{4,5},{5,4},{6,7},{7,6},{8,9},{9,8},{10,11... | collective-permute-start | bytes 589832 | tf_op jit(solution)/shard_map/ppermute | solution.py:30
  37.6 9.8 %collective-permute-start.16 = (bf16[3,32,1152]{2,1,0:T(8,128)(2,1)S(1)}, bf16[3,32,1152]{2,1,0:T(8,128)(2,1)S(1)}, u32[]{:S(2)}, u32[]{:S(2)}) collective-permute-start(bf16[3,32,1152]{2,1,0:T(8,128)(2,1)S(1)} %get-tuple-element.56), channel_id=1, source_target_pairs={{0,2},{1,3},{2,0},{3,1},{4,6},{5,7},{6,4},{7,5},{8,10},{9,11},{10,... | collective-permute-start | bytes 663560 | tf_op jit(solution)/shard_map/ppermute | solution.py:360
  38.9 15.0 %collective-permute-start.20 = (bf16[3,128,256]{2,1,0:T(8,128)(2,1)S(1)}, bf16[3,128,256]{2,1,0:T(8,128)(2,1)S(1)}, u32[]{:S(2)}, u32[]{:S(2)}) collective-permute-start(bf16[3,128,256]{2,1,0:T(8,128)(2,1)S(1)} %get-tuple-element.71), channel_id=1, source_target_pairs={{1,2},{2,1},{5,6},{6,5},{9,10},{10,9},{13,14},{14,13},{17,18},{18,... | collective-permute-start | bytes 589832 | tf_op jit(solution)/shard_map/ppermute | solution.py:30
  43.0 7.0 %collective-permute-start.17 = (bf16[7,32,128]{2,1,0:T(8,128)(2,1)S(1)}, bf16[7,32,128]{2,1,0:T(8,128)(2,1)S(1)}, u32[]{:S(2)}, u32[]{:S(2)}) collective-permute-start(bf16[7,32,128]{2,1,0:T(8,128)(2,1)S(1)} %get-tuple-element.67), channel_id=1, source_target_pairs={{0,12},{4,8},{8,4},{12,0},{1,13},{5,9},{9,5},{13,1},{2,14},{6,10},... | collective-permute-start | bytes 172040 | tf_op jit(solution)/shard_map/ppermute | solution.py:343
  44.4 6.7 %collective-permute-start.18 = (bf16[7,32,128]{2,1,0:T(8,128)(2,1)S(1)}, bf16[7,32,128]{2,1,0:T(8,128)(2,1)S(1)}, u32[]{:S(2)}, u32[]{:S(2)}) collective-permute-start(bf16[7,32,128]{2,1,0:T(8,128)(2,1)S(1)} %get-tuple-element.68), channel_id=1, source_target_pairs={{0,4},{4,0},{8,12},{12,8},{1,5},{5,1},{9,13},{13,9},{2,6},{6,2},{1... | collective-permute-start | bytes 172040 | tf_op jit(solution)/shard_map/ppermute | solution.py:343
  46.6 6.4 %collective-permute-start.19 = (bf16[7,32,128]{2,1,0:T(8,128)(2,1)S(1)}, bf16[7,32,128]{2,1,0:T(8,128)(2,1)S(1)}, u32[]{:S(2)}, u32[]{:S(2)}) collective-permute-start(bf16[7,32,128]{2,1,0:T(8,128)(2,1)S(1)} %get-tuple-element.69), channel_id=1, source_target_pairs={{0,8},{4,12},{8,0},{12,4},{1,9},{5,13},{9,1},{13,5},{2,10},{6,14},... | collective-permute-start | bytes 172040 | tf_op jit(solution)/shard_map/ppermute | solution.py:343
  48.4 8.1 %collective-permute-start.21 = (bf16[7,32,128]{2,1,0:T(8,128)(2,1)S(1)}, bf16[7,32,128]{2,1,0:T(8,128)(2,1)S(1)}, u32[]{:S(2)}, u32[]{:S(2)}) collective-permute-start(bf16[7,32,128]{2,1,0:T(8,128)(2,1)S(1)} %get-tuple-element.74), channel_id=1, source_target_pairs={{0,12},{4,8},{8,4},{12,0},{1,13},{5,9},{9,5},{13,1},{2,14},{6,10},... | collective-permute-start | bytes 172040 | tf_op jit(solution)/shard_map/ppermute | solution.py:343
  50.0 6.5 %collective-permute-start.22 = (bf16[7,32,128]{2,1,0:T(8,128)(2,1)S(1)}, bf16[7,32,128]{2,1,0:T(8,128)(2,1)S(1)}, u32[]{:S(2)}, u32[]{:S(2)}) collective-permute-start(bf16[7,32,128]{2,1,0:T(8,128)(2,1)S(1)} %get-tuple-element.75), channel_id=1, source_target_pairs={{0,4},{4,0},{8,12},{12,8},{1,5},{5,1},{9,13},{13,9},{2,6},{6,2},{1... | collective-permute-start | bytes 172040 | tf_op jit(solution)/shard_map/ppermute | solution.py:343
  51.1 5.7 %collective-permute-start.23 = (bf16[7,32,128]{2,1,0:T(8,128)(2,1)S(1)}, bf16[7,32,128]{2,1,0:T(8,128)(2,1)S(1)}, u32[]{:S(2)}, u32[]{:S(2)}) collective-permute-start(bf16[7,32,128]{2,1,0:T(8,128)(2,1)S(1)} %get-tuple-element.76), channel_id=1, source_target_pairs={{0,8},{4,12},{8,0},{12,4},{1,9},{5,13},{9,1},{13,5},{2,10},{6,14},... | collective-permute-start | bytes 172040 | tf_op jit(solution)/shard_map/ppermute | solution.py:343
  (4 other events, 12.0 us)

commit v7 on v6

--- a/solution.py
+++ b/solution.py
@@ -105,7 +105,7 @@
     return combine(jnp.dot(weights[...], window(field, row), preferred_element_type=F32))
 
 
-def gather_kernel(where, own, odd, even, *refs):
+def gather_kernel(where, own, even, odd, *refs):
     stack, across, inside = refs
     for plane, slab in zip(planes_of(where), (own, odd, even)):
         stack[plane] = jnp.transpose(slab[:, 0], (1, 0, 2))
@@ -113,10 +113,9 @@
         inside[plane] = stack[plane, (1 - where[1]) * (stack.shape[1] - 1)]
 
 
-def gather_hidden_kernel(where, own, even, odd, stack, across, inside):
+def hidden_rows_kernel(where, own, even, odd, across, inside):
     last = own.shape[0] - 1
     for plane, slab in zip(planes_of(where), (own, odd, even)):
-        stack[plane] = slab[...]
         across[plane] = slab[where[1] * last]
         inside[plane] = slab[(1 - where[1]) * last]
 
@@ -151,11 +150,17 @@
         slope[row] = gate * (1.0 + value * (1.0 - gate))
 
 
-def second_kernel(where, *refs):
-    stack, inside, edges, weights, out, field, held = refs
-    fill(where, stack, inside, edges, field)
-    for row in range(held.shape[0]):
-        held[row] = conv_rows(weights, field, row).astype(BF16)
+def second_kernel(where, own, even, odd, inside, edges, weights, out, field, held):
+    rows = held.shape[0]
+    row = where[1]
+    for plane, slab in zip(planes_of(where), (own, odd, even)):
+        for r in range(rows):
+            field[1 + r, plane] = slab[r]
+    for plane in range(3):
+        field[(1 - row) * (rows + 1), plane] = inside[plane]
+        field[row * (rows + 1), plane] = edges[plane]
+    for at in range(rows):
+        held[at] = conv_rows(weights, field, at).astype(BF16)
     out[:, 0] = jnp.transpose(held[...], (1, 0, 2))
 
 
@@ -384,8 +389,8 @@
     stack = struct((3, rows, chans, width), BF16)
     edge = struct((3, chans, width), BF16)
 
-    volume_planes = (swap_planes(volume, 1), swap_planes(volume, 0))
-    grad_planes = (swap_planes(cotangent, 1), swap_planes(cotangent, 0))
+    volume_planes = (swap_planes(volume, 0), swap_planes(volume, 1))
+    grad_planes = (swap_planes(cotangent, 0), swap_planes(cotangent, 1))
     first_weights, second_weights, back_weights = call(
         weights_kernel,
         "weights",
@@ -431,17 +436,17 @@
     shape = (outs // row_count, taps, ins // plane_count)
 
     def hidden_rows(even, odd):
-        own, across, inside = call(
-            gather_hidden_kernel, "gather_hidden", [stack, edge, edge], (where, hidden, even, odd)
-        )
-        return own, swap_rows(inside, 0), swap_rows(across, 1)
-
-    def convolved(*slabs):
+        across, inside = call(
+            hidden_rows_kernel, "hidden_rows", [edge, edge], (where, hidden, even, odd)
+        )
+        return swap_rows(inside, 0), swap_rows(across, 1)
+
+    def convolved(inside, across):
         (out,) = call(
             second_kernel,
             "second_conv",
             [struct(volume.shape, BF16)],
-            (where, *slabs, second_weights),
+            (where, hidden, hidden_even, hidden_odd, inside, across, second_weights),
             [field, slab],
             flops,
         )
@@ -493,12 +498,12 @@
             busy=0,
         )
         first_arrived = cross(first_send)
-        hidden_slabs = hidden_rows(after(hidden_even, first_send), hidden_odd)
+        hidden_edges = hidden_rows(after(hidden_even, first_send), hidden_odd)
         steps = range(3)
         second_taps = [26 - (a * 9 + b * 3 + e) for b in steps for a in steps for e in steps]
         first_taps = [a * 9 + b * 3 + e for e in steps for b in steps for a in steps]
         *second_parts, second_keep = packed_parts(
-            where, after(second_keep, hidden_slabs[1]), second_arrived
+            where, after(second_keep, hidden_edges[0]), second_arrived
         )
         second_parts = exchanged(second_parts)
         *first_parts, first_keep = packed_parts(
@@ -508,7 +513,7 @@
         second_sum = finished(
             after(second_keep, first_keep), second_parts, second_taps, factor, shape
         )
-        second_out = convolved(after(hidden_slabs[0], second_sum), *hidden_slabs[1:])
+        second_out = convolved(after(hidden_edges[0], second_sum), hidden_edges[1])
         first_sum = finished(
             after(first_keep, second_out), first_parts, first_taps, factor, shape
         )

time: 58.1 us -> 57.6 us (level)
  waiting for transfers between devices: 8.43 us -> 4.71 us
  starting transfers between devices: 28.4 us -> 31.3 us
    ppermute x6, waiting for transfers between devices: 4.85 us -> 1.43 us  [swap_planes(): return lax.ppermute(values, 'cin', links(lax.axis_size('cin'), odd))]
    ppermute x6, starting transfers between devices: 11.5 us -> 13.9 us  [swap_planes(): return lax.ppermute(values, 'cin', links(lax.axis_size('cin'), odd))]
  transfers between devices with their start and end apart: 24 -> 24, of which waited for: 6 -> 3; matrix products, arithmetic and copies ran while one was open for 0% -> 0% of each run, Pallas kernels for 29% -> 29%
where the time goes in v7:
time: 57.6 us; the launch traced here: 57.3 us
  starting transfers between devices  31.3 us (54%)
  Pallas kernels  17.6 us (31%)
  waiting for transfers between devices  4.71 us (8%)
  local copies, waits for them, and re-layouts  2.66 us (5%)
  between operations  0.87 us (2%)
    pallas_call x13, Pallas kernels, call(): pl.pallas_call(kernel, name=name, in_specs=[SMEM] * scalars + [VMEM] * (l...  17.6 us
    ppermute x6, starting transfers between devices, swap_planes(): return lax.ppermute(values, 'cin', links(lax.axis_size('cin'), odd))  13.9 us
    ppermute x6, starting transfers between devices, exchanged(): lax.ppermute(value, 'cin', [(i, i ^ k + 1) for i in range(parts)])  8.98 us
    ppermute x10, starting transfers between devices, swap_rows(): return lax.ppermute(values, 'cout', links(lax.axis_size('cout'), odd))  6.32 us
    unnamed x8, local copies, waits for them, and re-layouts  2.66 us
    ppermute x2, waiting for transfers between devices, cross(): lax.ppermute(values, 'cout', [(i, i ^ 2) for i in range(lax.axis_size('co...  2.44 us
    ppermute x2, starting transfers between devices, cross(): lax.ppermute(values, 'cout', [(i, i ^ 2) for i in range(lax.axis_size('co...  2.16 us
    ppermute x6, waiting for transfers between devices, swap_planes(): return lax.ppermute(values, 'cin', links(lax.axis_size('cin'), odd))  1.43 us
  transfers between devices with their start and end apart: 24, of which 3 were waited for; matrix products, arithmetic and copies ran while one was open for 0% of the time, Pallas kernels for 29%

profile of v7, /device:TPU:0, one launch (start us, length us, event | category | flops | bytes accessed | tf_op | source)
XLA Modules:
  0.0 57.3 jit_solution(13042708645990643260)
XLA Ops:
  0.6 3.1 %collective-permute-start = (bf16[128,1,4,256]{3,2,1,0:T(4,128)(2,1)}, bf16[128,1,4,256]{3,2,1,0:T(4,128)(2,1)S(1)}, u32[]{:S(2)}, u32[]{:S(2)}) collective-permute-start(bf16[128,1,4,256]{3,2,1,0:T(4,128)(2,1)} %own.2), channel_id=1, source_target_pairs={{0,4},{4,0},{8,12},{12,8},{1,5},{5,1},{9,13},{13,9},{2,6},{6,2},{1... | collective-permute-start | bytes 786440 | tf_op jit(solution)/shard_map/ppermute | solution.py:26
  4.4 4.4 %collective-permute-start.7 = (bf16[128,1,4,256]{3,2,1,0:T(4,128)(2,1)}, bf16[128,1,4,256]{3,2,1,0:T(4,128)(2,1)S(1)}, u32[]{:S(2)}, u32[]{:S(2)}) collective-permute-start(bf16[128,1,4,256]{3,2,1,0:T(4,128)(2,1)} %own.3), channel_id=1, source_target_pairs={{0,4},{4,0},{8,12},{12,8},{1,5},{5,1},{9,13},{13,9},{2,6},{6,2},{1... | collective-permute-start | bytes 786440 | tf_op jit(solution)/shard_map/ppermute | solution.py:26
  9.6 1.2 %copy-done = bf16[128,27,128]{2,0,1:T(8,128)(2,1)S(1)} copy-done((bf16[128,27,128]{2,0,1:T(8,128)(2,1)S(1)}, bf16[128,27,128]{2,0,1:T(8,128)(2,1)}, u32[]{:S(2)}) %copy-start) | copy-done | bytes 884760
  10.7 1.2 %copy-done.1 = bf16[128,27,128]{2,0,1:T(8,128)(2,1)S(1)} copy-done((bf16[128,27,128]{2,0,1:T(8,128)(2,1)S(1)}, bf16[128,27,128]{2,0,1:T(8,128)(2,1)}, u32[]{:S(2)}) %copy-start.1) | copy-done | bytes 884760
  14.4 1.4 %collective-permute-done.7.even = bf16[128,1,4,256]{3,2,1,0:T(4,128)(2,1)S(1)} collective-permute-done((bf16[128,1,4,256]{3,2,1,0:T(4,128)(2,1)}, bf16[128,1,4,256]{3,2,1,0:T(4,128)(2,1)S(1)}, u32[]{:S(2)}, u32[]{:S(2)}) %collective-permute-start.7) | collective-permute-done | bytes 262176 | tf_op jit(solution)/shard_map/ppermute | solution.py:26
  15.9 0.8 %gather_cotangent.1 = (bf16[3,4,128,256]{3,2,1,0:T(8,128)(2,1)S(1)}, bf16[3,128,256]{2,1,0:T(8,128)(2,1)S(1)}, bf16[3,128,256]{2,1,0:T(8,128)(2,1)S(1)}) custom-call(s32[4]{0:T(128)S(1)} %pad_add_fusion.where, bf16[128,1,4,256]{3,2,1,0:T(4,128)(2,1)S(1)} %copy-done.3, bf16[128,1,4,256]{3,2,1,0:T(4,128)(2,1)S(1)} %collective-permute-done.7.even, ...), custom_call_target="tpu_custom_call" | custom-call | bytes 1966096 | tf_op jit(solution)/shard_map/gather_cotangent/pallas_call | solution.py:312
  16.7 1.5 %collective-permute-start.9 = (bf16[3,128,256]{2,1,0:T(8,128)(2,1)S(1)}, bf16[3,128,256]{2,1,0:T(8,128)(2,1)S(1)}, u32[]{:S(2)}, u32[]{:S(2)}) collective-permute-start(bf16[3,128,256]{2,1,0:T(8,128)(2,1)S(1)} %get-tuple-element.47), channel_id=1, source_target_pairs={{0,1},{1,0},{2,3},{3,2},{4,5},{5,4},{6,7},{7,6},{8,9},{9,8},{10,11... | collective-permute-start | bytes 589832 | tf_op jit(solution)/shard_map/ppermute | solution.py:30
  18.9 1.9 %collective-permute-start.11 = (bf16[3,4,128,256]{3,2,1,0:T(8,128)(2,1)S(1)}, bf16[3,4,128,256]{3,2,1,0:T(8,128)(2,1)S(1)}, u32[]{:S(2)}, u32[]{:S(2)}) collective-permute-start(bf16[3,4,128,256]{3,2,1,0:T(8,128)(2,1)S(1)} %get-tuple-element.46.refs_0_), channel_id=1, source_target_pairs={{0,1},{1,0},{2,3},{3,2},{4,5},{5,4},{6,7},{7,6},{8,9},{9,8},{10,11... | collective-permute-start | bytes 2359304 | tf_op jit(solution)/shard_map/ppermute | solution.py:30
  20.8 2.0 %first_conv.1 = (bf16[4,128,256]{2,1,0:T(8,128)(2,1)S(1)}, f32[4,128,256]{2,1,0:T(8,128)S(1)}, bf16[19,128,256]{2,1,0:T(8,128)(2,1)S(1)}) custom-call(s32[4]{0:T(128)S(1)} %pad_add_fusion.where, bf16[3,4,128,256]{3,2,1,0:T(8,128)(2,1)S(1)} %get-tuple-element.41.refs_0_, bf16[3,128,256]{2,1,0:T(8,128)(2,1)S(1)} %collective-permute-done.2.refs_1_, ...), custom_call_target="tpu_custom_call" | custom-call | flops 905969664 | bytes 4096016 | tf_op jit(solution)/shard_map/first_conv/pallas_call | solution.py:312
  22.9 4.4 %collective-permute-start.4 = (bf16[4,128,256]{2,1,0:T(8,128)(2,1)S(1)}, bf16[4,128,256]{2,1,0:T(8,128)(2,1)S(1)}, u32[]{:S(2)}, u32[]{:S(2)}) collective-permute-start(bf16[4,128,256]{2,1,0:T(8,128)(2,1)S(1)} %get-tuple-element.44.refs_4_.own), channel_id=1, source_target_pairs={{0,4},{4,0},{8,12},{12,8},{1,5},{5,1},{9,13},{13,9},{2,6},{6,2},{1... | collective-permute-start | bytes 786440 | tf_op jit(solution)/shard_map/ppermute | solution.py:26
  28.5 1.9 %hidden_grad.1 = (bf16[4,64,256]{2,1,0:T(8,128)(2,1)S(1)}, bf16[4,64,256]{2,1,0:T(8,128)(2,1)S(1)}) custom-call(s32[4]{0:T(128)S(1)} %pad_add_fusion.where, bf16[3,4,128,256]{3,2,1,0:T(8,128)(2,1)S(1)} %get-tuple-element.46.refs_0_, bf16[3,128,256]{2,1,0:T(8,128)(2,1)S(1)} %collective-permute-done.9.refs_1_, ...), custom_call_target="tpu_custom_call" | custom-call | flops 18119393280 | bytes 57016640 | tf_op jit(solution)/shard_map/hidden_grad/pallas_call | solution.py:312
  31.3 2.1 %second_filter_grad.1 = (bf16[9,32,384]{2,1,0:T(8,128)(2,1)S(1)}, f32[9,32,384]{2,1,0:T(8,128)S(1)}) custom-call(s32[4]{0:T(128)S(1)} %pad_add_fusion.where, bf16[3,4,128,256]{3,2,1,0:T(8,128)(2,1)S(1)} %get-tuple-element.46.refs_0_, bf16[3,4,128,256]{3,2,1,0:T(8,128)(2,1)S(1)} %collective-permute-done.11.refs_1_, ...), custom_call_target="tpu_custom_call" | custom-call | tf_op jit(solution)/shard_map/second_filter_grad/pallas_call | solution.py:312
  34.1 2.3 %first_filter_grad.1 = (bf16[3,32,1152]{2,1,0:T(8,128)(2,1)S(1)}, f32[3,32,1152]{2,1,0:T(8,128)S(1)}) custom-call(s32[4]{0:T(128)S(1)} %pad_add_fusion.where, bf16[3,4,128,256]{3,2,1,0:T(8,128)(2,1)S(1)} %get-tuple-element.41.refs_0_, bf16[3,128,256]{2,1,0:T(8,128)(2,1)S(1)} %collective-permute-done.3.refs_2_.refs_1_, ...), custom_call_target="tpu_custom_call" | custom-call | tf_op jit(solution)/shard_map/first_filter_grad/pallas_call | solution.py:312
  37.2 1.5 %collective-permute-start.16 = (bf16[3,32,1152]{2,1,0:T(8,128)(2,1)S(1)}, bf16[3,32,1152]{2,1,0:T(8,128)(2,1)S(1)}, u32[]{:S(2)}, u32[]{:S(2)}) collective-permute-start(bf16[3,32,1152]{2,1,0:T(8,128)(2,1)S(1)} %get-tuple-element.55), channel_id=1, source_target_pairs={{0,2},{1,3},{2,0},{3,1},{4,6},{5,7},{6,4},{7,5},{8,10},{9,11},{10,... | collective-permute-start | bytes 663560 | tf_op jit(solution)/shard_map/ppermute | solution.py:365
  39.4 2.4 %collective-permute-done.15.arrived = bf16[9,32,384]{2,1,0:T(8,128)(2,1)S(1)} collective-permute-done((bf16[9,32,384]{2,1,0:T(8,128)(2,1)S(1)}, bf16[9,32,384]{2,1,0:T(8,128)(2,1)S(1)}, u32[]{:S(2)}, u32[]{:S(2)}) %collective-permute-start.15) | collective-permute-done | bytes 221216 | tf_op jit(solution)/shard_map/ppermute | solution.py:365
  41.8 1.0 %pack_parts.2 = (bf16[7,32,128]{2,1,0:T(8,128)(2,1)S(1)}, bf16[7,32,128]{2,1,0:T(8,128)(2,1)S(1)}, bf16[7,32,128]{2,1,0:T(8,128)(2,1)S(1)}, f32[7,32,128]{2,1,0:T(8,128)S(1)}) custom-call(s32[4]{0:T(128)S(1)} %pad_add_fusion.where, f32[9,32,384]{2,1,0:T(8,128)S(1)} %get-tuple-element.59.held, bf16[9,32,384]{2,1,0:T(8,128)(2,1)S(1)} %collective-permute-done.15.arrived), custom_call_target="tpu_custom_call" | custom-call | bytes 950288 | tf_op jit(solution)/shard_map/pack_parts/pallas_call | solution.py:312
  42.8 2.7 %collective-permute-start.17 = (bf16[7,32,128]{2,1,0:T(8,128)(2,1)S(1)}, bf16[7,32,128]{2,1,0:T(8,128)(2,1)S(1)}, u32[]{:S(2)}, u32[]{:S(2)}) collective-permute-start(bf16[7,32,128]{2,1,0:T(8,128)(2,1)S(1)} %get-tuple-element.65), channel_id=1, source_target_pairs={{0,12},{4,8},{8,4},{12,0},{1,13},{5,9},{9,5},{13,1},{2,14},{6,10},... | collective-permute-start | bytes 172040 | tf_op jit(solution)/shard_map/ppermute | solution.py:348
  46.1 1.2 %collective-permute-start.19 = (bf16[7,32,128]{2,1,0:T(8,128)(2,1)S(1)}, bf16[7,32,128]{2,1,0:T(8,128)(2,1)S(1)}, u32[]{:S(2)}, u32[]{:S(2)}) collective-permute-start(bf16[7,32,128]{2,1,0:T(8,128)(2,1)S(1)} %get-tuple-element.67), channel_id=1, source_target_pairs={{0,8},{4,12},{8,0},{12,4},{1,9},{5,13},{9,1},{13,5},{2,10},{6,14},... | collective-permute-start | bytes 172040 | tf_op jit(solution)/shard_map/ppermute | solution.py:348
  47.3 1.0 %pack_parts.3 = (bf16[7,32,128]{2,1,0:T(8,128)(2,1)S(1)}, bf16[7,32,128]{2,1,0:T(8,128)(2,1)S(1)}, bf16[7,32,128]{2,1,0:T(8,128)(2,1)S(1)}, f32[7,32,128]{2,1,0:T(8,128)S(1)}) custom-call(s32[4]{0:T(128)S(1)} %pad_add_fusion.where, f32[3,32,1152]{2,1,0:T(8,128)S(1)} %get-tuple-element.62.held, bf16[3,32,1152]{2,1,0:T(8,128)(2,1)S(1)} %collective-permute-done.16.arrived), custom_call_target="tpu_custom_call" | custom-call | bytes 950288 | tf_op jit(solution)/shard_map/pack_parts/pallas_call | solution.py:312
  48.3 2.6 %collective-permute-start.21 = (bf16[7,32,128]{2,1,0:T(8,128)(2,1)S(1)}, bf16[7,32,128]{2,1,0:T(8,128)(2,1)S(1)}, u32[]{:S(2)}, u32[]{:S(2)}) collective-permute-start(bf16[7,32,128]{2,1,0:T(8,128)(2,1)S(1)} %get-tuple-element.72), channel_id=1, source_target_pairs={{0,12},{4,8},{8,4},{12,0},{1,13},{5,9},{9,5},{13,1},{2,14},{6,10},... | collective-permute-start | bytes 172040 | tf_op jit(solution)/shard_map/ppermute | solution.py:348
  51.3 1.4 %collective-permute-start.23 = (bf16[7,32,128]{2,1,0:T(8,128)(2,1)S(1)}, bf16[7,32,128]{2,1,0:T(8,128)(2,1)S(1)}, u32[]{:S(2)}, u32[]{:S(2)}) collective-permute-start(bf16[7,32,128]{2,1,0:T(8,128)(2,1)S(1)} %get-tuple-element.74), channel_id=1, source_target_pairs={{0,8},{4,12},{8,0},{12,4},{1,9},{5,13},{9,1},{13,5},{2,10},{6,14},... | collective-permute-start | bytes 172040 | tf_op jit(solution)/shard_map/ppermute | solution.py:348
  52.8 0.9 %finish_sum.2 = f32[27,32,32]{2,1,0:T(8,128)} custom-call(f32[7,32,128]{2,1,0:T(8,128)S(1)} %get-tuple-element.64.held, bf16[7,32,128]{2,1,0:T(8,128)(2,1)S(1)} %collective-permute-done.17.refs_0_, bf16[7,32,128]{2,1,0:T(8,128)(2,1)S(1)} %collective-permute-done.18.refs_1_, bf16[7,32,128]{2,1,0:T(8,128)(2,1)S(1)} %collective-permute-done.19.refs_2_), custom_call_target="tpu_custom_call" | custom-call | bytes 397312 | tf_op jit(solution)/shard_map/finish_sum/pallas_call | solution.py:312
  53.7 2.7 %second_conv.1 = bf16[128,1,4,256]{3,2,1,0:T(4,128)(2,1)} custom-call(s32[4]{0:T(128)S(1)} %pad_add_fusion.where, bf16[4,128,256]{2,1,0:T(8,128)(2,1)S(1)} %get-tuple-element.44.refs_4_.own, bf16[4,128,256]{2,1,0:T(8,128)(2,1)S(1)} %collective-permute-done.4.even, bf16[4,128,256]{2,1,0:T(8,128)(2,1)S(1)} %collective-permute-done.5.odd, ...), custom_call_target="tpu_custom_call" | custom-call | flops 905969664 | bytes 2326544 | tf_op jit(solution)/shard_map/second_conv/pallas_call | solution.py:312
  56.4 0.9 %finish_sum.3 = f32[27,32,32]{2,1,0:T(8,128)} custom-call(f32[7,32,128]{2,1,0:T(8,128)S(1)} %get-tuple-element.71.held, bf16[7,32,128]{2,1,0:T(8,128)(2,1)S(1)} %collective-permute-done.21.refs_0_, bf16[7,32,128]{2,1,0:T(8,128)(2,1)S(1)} %collective-permute-done.22.refs_1_, bf16[7,32,128]{2,1,0:T(8,128)(2,1)S(1)} %collective-permute-done.23.refs_2_), custom_call_target="tpu_custom_call" | custom-call | bytes 397312 | tf_op jit(solution)/shard_map/finish_sum/pallas_call | solution.py:312
  (46 shorter events, 9.8 us)
Async XLA Ops:
  0.6 11.9 %collective-permute-start = (bf16[128,1,4,256]{3,2,1,0:T(4,128)(2,1)}, bf16[128,1,4,256]{3,2,1,0:T(4,128)(2,1)S(1)}, u32[]{:S(2)}, u32[]{:S(2)}) collective-permute-start(bf16[128,1,4,256]{3,2,1,0:T(4,128)(2,1)} %own.2), channel_id=1, source_target_pairs={{0,4},{4,0},{8,12},{12,8},{1,5},{5,1},{9,13},{13,9},{2,6},{6,2},{1... | collective-permute-start | bytes 786440 | tf_op jit(solution)/shard_map/ppermute | solution.py:26
  3.7 8.8 %collective-permute-start.1 = (bf16[128,1,4,256]{3,2,1,0:T(4,128)(2,1)}, bf16[128,1,4,256]{3,2,1,0:T(4,128)(2,1)S(1)}, u32[]{:S(2)}, u32[]{:S(2)}) collective-permute-start(bf16[128,1,4,256]{3,2,1,0:T(4,128)(2,1)} %own.2), channel_id=1, source_target_pairs={{4,8},{8,4},{5,9},{9,5},{6,10},{10,6},{7,11},{11,7},{20,24},{24,20... | collective-permute-start | bytes 786440 | tf_op jit(solution)/shard_map/ppermute | solution.py:26
  4.4 11.5 %collective-permute-start.7 = (bf16[128,1,4,256]{3,2,1,0:T(4,128)(2,1)}, bf16[128,1,4,256]{3,2,1,0:T(4,128)(2,1)S(1)}, u32[]{:S(2)}, u32[]{:S(2)}) collective-permute-start(bf16[128,1,4,256]{3,2,1,0:T(4,128)(2,1)} %own.3), channel_id=1, source_target_pairs={{0,4},{4,0},{8,12},{12,8},{1,5},{5,1},{9,13},{13,9},{2,6},{6,2},{1... | collective-permute-start | bytes 786440 | tf_op jit(solution)/shard_map/ppermute | solution.py:26
  8.8 7.0 %collective-permute-start.8 = (bf16[128,1,4,256]{3,2,1,0:T(4,128)(2,1)}, bf16[128,1,4,256]{3,2,1,0:T(4,128)(2,1)S(1)}, u32[]{:S(2)}, u32[]{:S(2)}) collective-permute-start(bf16[128,1,4,256]{3,2,1,0:T(4,128)(2,1)} %own.3), channel_id=1, source_target_pairs={{4,8},{8,4},{5,9},{9,5},{6,10},{10,6},{7,11},{11,7},{20,24},{24,20... | collective-permute-start | bytes 786440 | tf_op jit(solution)/shard_map/ppermute | solution.py:26
  13.7 7.2 %collective-permute-start.2 = (bf16[3,128,256]{2,1,0:T(8,128)(2,1)S(1)}, bf16[3,128,256]{2,1,0:T(8,128)(2,1)S(1)}, u32[]{:S(2)}, u32[]{:S(2)}) collective-permute-start(bf16[3,128,256]{2,1,0:T(8,128)(2,1)S(1)} %get-tuple-element.42), channel_id=1, source_target_pairs={{0,1},{1,0},{2,3},{3,2},{4,5},{5,4},{6,7},{7,6},{8,9},{9,8},{10,11... | collective-permute-start | bytes 589832 | tf_op jit(solution)/shard_map/ppermute | solution.py:30
  13.8 7.1 %collective-permute-start.3 = (bf16[3,128,256]{2,1,0:T(8,128)(2,1)S(1)}, bf16[3,128,256]{2,1,0:T(8,128)(2,1)S(1)}, u32[]{:S(2)}, u32[]{:S(2)}) collective-permute-start(bf16[3,128,256]{2,1,0:T(8,128)(2,1)S(1)} %get-tuple-element.43), channel_id=1, source_target_pairs={{1,2},{2,1},{5,6},{6,5},{9,10},{10,9},{13,14},{14,13},{17,18},{18,... | collective-permute-start | bytes 589832 | tf_op jit(solution)/shard_map/ppermute | solution.py:30
  16.7 11.2 %collective-permute-start.9 = (bf16[3,128,256]{2,1,0:T(8,128)(2,1)S(1)}, bf16[3,128,256]{2,1,0:T(8,128)(2,1)S(1)}, u32[]{:S(2)}, u32[]{:S(2)}) collective-permute-start(bf16[3,128,256]{2,1,0:T(8,128)(2,1)S(1)} %get-tuple-element.47), channel_id=1, source_target_pairs={{0,1},{1,0},{2,3},{3,2},{4,5},{5,4},{6,7},{7,6},{8,9},{9,8},{10,11... | collective-permute-start | bytes 589832 | tf_op jit(solution)/shard_map/ppermute | solution.py:30
  18.2 9.8 %collective-permute-start.10 = (bf16[3,128,256]{2,1,0:T(8,128)(2,1)S(1)}, bf16[3,128,256]{2,1,0:T(8,128)(2,1)S(1)}, u32[]{:S(2)}, u32[]{:S(2)}) collective-permute-start(bf16[3,128,256]{2,1,0:T(8,128)(2,1)S(1)} %get-tuple-element.48), channel_id=1, source_target_pairs={{1,2},{2,1},{5,6},{6,5},{9,10},{10,9},{13,14},{14,13},{17,18},{18,... | collective-permute-start | bytes 589832 | tf_op jit(solution)/shard_map/ppermute | solution.py:30
  18.9 12.4 %collective-permute-start.11 = (bf16[3,4,128,256]{3,2,1,0:T(8,128)(2,1)S(1)}, bf16[3,4,128,256]{3,2,1,0:T(8,128)(2,1)S(1)}, u32[]{:S(2)}, u32[]{:S(2)}) collective-permute-start(bf16[3,4,128,256]{3,2,1,0:T(8,128)(2,1)S(1)} %get-tuple-element.46.refs_0_), channel_id=1, source_target_pairs={{0,1},{1,0},{2,3},{3,2},{4,5},{5,4},{6,7},{7,6},{8,9},{9,8},{10,11... | collective-permute-start | bytes 2359304 | tf_op jit(solution)/shard_map/ppermute | solution.py:30
  22.9 13.6 %collective-permute-start.4 = (bf16[4,128,256]{2,1,0:T(8,128)(2,1)S(1)}, bf16[4,128,256]{2,1,0:T(8,128)(2,1)S(1)}, u32[]{:S(2)}, u32[]{:S(2)}) collective-permute-start(bf16[4,128,256]{2,1,0:T(8,128)(2,1)S(1)} %get-tuple-element.44.refs_4_.own), channel_id=1, source_target_pairs={{0,4},{4,0},{8,12},{12,8},{1,5},{5,1},{9,13},{13,9},{2,6},{6,2},{1... | collective-permute-start | bytes 786440 | tf_op jit(solution)/shard_map/ppermute | solution.py:26
  27.2 9.3 %collective-permute-start.5 = (bf16[4,128,256]{2,1,0:T(8,128)(2,1)S(1)}, bf16[4,128,256]{2,1,0:T(8,128)(2,1)S(1)}, u32[]{:S(2)}, u32[]{:S(2)}) collective-permute-start(bf16[4,128,256]{2,1,0:T(8,128)(2,1)S(1)} %get-tuple-element.44.refs_4_.own), channel_id=1, source_target_pairs={{4,8},{8,4},{5,9},{9,5},{6,10},{10,6},{7,11},{11,7},{20,24},{24,20... | collective-permute-start | bytes 786440 | tf_op jit(solution)/shard_map/ppermute | solution.py:26
  27.9 3.4 %collective-permute-start.6 = (bf16[19,128,256]{2,1,0:T(8,128)(2,1)S(1)}, bf16[19,128,256]{2,1,0:T(8,128)(2,1)S(1)}, u32[]{:S(2)}, u32[]{:S(2)}) collective-permute-start(bf16[19,128,256]{2,1,0:T(8,128)(2,1)S(1)} %get-tuple-element.45), channel_id=1, source_target_pairs={{0,1},{1,0},{2,3},{3,2},{4,5},{5,4},{6,7},{7,6},{8,9},{9,8},{10,11... | collective-permute-start | bytes 3735560 | tf_op jit(solution)/shard_map/ppermute | solution.py:30
  28.0 3.2 %collective-permute-start.12 = (bf16[3,128,256]{2,1,0:T(8,128)(2,1)S(1)}, bf16[3,128,256]{2,1,0:T(8,128)(2,1)S(1)}, u32[]{:S(2)}, u32[]{:S(2)}) collective-permute-start(bf16[3,128,256]{2,1,0:T(8,128)(2,1)S(1)} %collective-permute-done.10.refs_2_), channel_id=1, source_target_pairs={{0,1},{1,0},{2,3},{3,2},{4,5},{5,4},{6,7},{7,6},{8,9},{9,8},{10,11... | collective-permute-start | bytes 589832 | tf_op jit(solution)/shard_map/ppermute | solution.py:30
  31.2 2.9 %collective-permute-start.13 = (bf16[4,64,256]{2,1,0:T(8,128)(2,1)S(1)}, bf16[4,64,256]{2,1,0:T(8,128)(2,1)S(1)}, u32[]{:S(2)}, u32[]{:S(2)}) collective-permute-start(bf16[4,64,256]{2,1,0:T(8,128)(2,1)S(1)} %get-tuple-element.54), channel_id=1, source_target_pairs={{0,1},{1,0},{2,3},{3,2},{4,5},{5,4},{6,7},{7,6},{8,9},{9,8},{10,11... | collective-permute-start | bytes 393224 | tf_op jit(solution)/shard_map/ppermute | solution.py:30
  33.5 8.3 %collective-permute-start.15 = (bf16[9,32,384]{2,1,0:T(8,128)(2,1)S(1)}, bf16[9,32,384]{2,1,0:T(8,128)(2,1)S(1)}, u32[]{:S(2)}, u32[]{:S(2)}) collective-permute-start(bf16[9,32,384]{2,1,0:T(8,128)(2,1)S(1)} %get-tuple-element.52), channel_id=1, source_target_pairs={{0,2},{1,3},{2,0},{3,1},{4,6},{5,7},{6,4},{7,5},{8,10},{9,11},{10,... | collective-permute-start | bytes 663560 | tf_op jit(solution)/shard_map/ppermute | solution.py:365
  37.1 2.3 %collective-permute-start.14 = (bf16[3,128,256]{2,1,0:T(8,128)(2,1)S(1)}, bf16[3,128,256]{2,1,0:T(8,128)(2,1)S(1)}, u32[]{:S(2)}, u32[]{:S(2)}) collective-permute-start(bf16[3,128,256]{2,1,0:T(8,128)(2,1)S(1)} %get-tuple-element.57), channel_id=1, source_target_pairs={{0,1},{1,0},{2,3},{3,2},{4,5},{5,4},{6,7},{7,6},{8,9},{9,8},{10,11... | collective-permute-start | bytes 589832 | tf_op jit(solution)/shard_map/ppermute | solution.py:30
  37.2 10.1 %collective-permute-start.16 = (bf16[3,32,1152]{2,1,0:T(8,128)(2,1)S(1)}, bf16[3,32,1152]{2,1,0:T(8,128)(2,1)S(1)}, u32[]{:S(2)}, u32[]{:S(2)}) collective-permute-start(bf16[3,32,1152]{2,1,0:T(8,128)(2,1)S(1)} %get-tuple-element.55), channel_id=1, source_target_pairs={{0,2},{1,3},{2,0},{3,1},{4,6},{5,7},{6,4},{7,5},{8,10},{9,11},{10,... | collective-permute-start | bytes 663560 | tf_op jit(solution)/shard_map/ppermute | solution.py:365
  38.7 15.0 %collective-permute-start.20 = (bf16[3,128,256]{2,1,0:T(8,128)(2,1)S(1)}, bf16[3,128,256]{2,1,0:T(8,128)(2,1)S(1)}, u32[]{:S(2)}, u32[]{:S(2)}) collective-permute-start(bf16[3,128,256]{2,1,0:T(8,128)(2,1)S(1)} %get-tuple-element.69), channel_id=1, source_target_pairs={{1,2},{2,1},{5,6},{6,5},{9,10},{10,9},{13,14},{14,13},{17,18},{18,... | collective-permute-start | bytes 589832 | tf_op jit(solution)/shard_map/ppermute | solution.py:30
  42.8 8.1 %collective-permute-start.17 = (bf16[7,32,128]{2,1,0:T(8,128)(2,1)S(1)}, bf16[7,32,128]{2,1,0:T(8,128)(2,1)S(1)}, u32[]{:S(2)}, u32[]{:S(2)}) collective-permute-start(bf16[7,32,128]{2,1,0:T(8,128)(2,1)S(1)} %get-tuple-element.65), channel_id=1, source_target_pairs={{0,12},{4,8},{8,4},{12,0},{1,13},{5,9},{9,5},{13,1},{2,14},{6,10},... | collective-permute-start | bytes 172040 | tf_op jit(solution)/shard_map/ppermute | solution.py:348
  45.5 5.8 %collective-permute-start.18 = (bf16[7,32,128]{2,1,0:T(8,128)(2,1)S(1)}, bf16[7,32,128]{2,1,0:T(8,128)(2,1)S(1)}, u32[]{:S(2)}, u32[]{:S(2)}) collective-permute-start(bf16[7,32,128]{2,1,0:T(8,128)(2,1)S(1)} %get-tuple-element.66), channel_id=1, source_target_pairs={{0,4},{4,0},{8,12},{12,8},{1,5},{5,1},{9,13},{13,9},{2,6},{6,2},{1... | collective-permute-start | bytes 172040 | tf_op jit(solution)/shard_map/ppermute | solution.py:348
  46.1 6.6 %collective-permute-start.19 = (bf16[7,32,128]{2,1,0:T(8,128)(2,1)S(1)}, bf16[7,32,128]{2,1,0:T(8,128)(2,1)S(1)}, u32[]{:S(2)}, u32[]{:S(2)}) collective-permute-start(bf16[7,32,128]{2,1,0:T(8,128)(2,1)S(1)} %get-tuple-element.67), channel_id=1, source_target_pairs={{0,8},{4,12},{8,0},{12,4},{1,9},{5,13},{9,1},{13,5},{2,10},{6,14},... | collective-permute-start | bytes 172040 | tf_op jit(solution)/shard_map/ppermute | solution.py:348
  48.3 8.1 %collective-permute-start.21 = (bf16[7,32,128]{2,1,0:T(8,128)(2,1)S(1)}, bf16[7,32,128]{2,1,0:T(8,128)(2,1)S(1)}, u32[]{:S(2)}, u32[]{:S(2)}) collective-permute-start(bf16[7,32,128]{2,1,0:T(8,128)(2,1)S(1)} %get-tuple-element.72), channel_id=1, source_target_pairs={{0,12},{4,8},{8,4},{12,0},{1,13},{5,9},{9,5},{13,1},{2,14},{6,10},... | collective-permute-start | bytes 172040 | tf_op jit(solution)/shard_map/ppermute | solution.py:348
  50.9 5.4 %collective-permute-start.22 = (bf16[7,32,128]{2,1,0:T(8,128)(2,1)S(1)}, bf16[7,32,128]{2,1,0:T(8,128)(2,1)S(1)}, u32[]{:S(2)}, u32[]{:S(2)}) collective-permute-start(bf16[7,32,128]{2,1,0:T(8,128)(2,1)S(1)} %get-tuple-element.73), channel_id=1, source_target_pairs={{0,4},{4,0},{8,12},{12,8},{1,5},{5,1},{9,13},{13,9},{2,6},{6,2},{1... | collective-permute-start | bytes 172040 | tf_op jit(solution)/shard_map/ppermute | solution.py:348
  51.3 5.1 %collective-permute-start.23 = (bf16[7,32,128]{2,1,0:T(8,128)(2,1)S(1)}, bf16[7,32,128]{2,1,0:T(8,128)(2,1)S(1)}, u32[]{:S(2)}, u32[]{:S(2)}) collective-permute-start(bf16[7,32,128]{2,1,0:T(8,128)(2,1)S(1)} %get-tuple-element.74), channel_id=1, source_target_pairs={{0,8},{4,12},{8,0},{12,4},{1,9},{5,13},{9,1},{13,5},{2,10},{6,14},... | collective-permute-start | bytes 172040 | tf_op jit(solution)/shard_map/ppermute | solution.py:348
  (4 other events, 7.3 us)
